TPU v7x, 32 devices: a whole 2x2x4 slice. The times are simulated.
32 devices in a mesh: rep: 4 (over x, core), fsdp: 2 (over y), tp: 4 (over z).
Axes of the slice: x: 2, y: 2, z: 4, core: 2. Of those that a mesh axis runs over, the one named last changes fastest.
Arguments:
- image_input: bfloat16 [8, 896, 1536], P(('rep', 'fsdp'), 'tp'), may hold values from -6 to 6
- text_input: bfloat16 [8, 128, 1536], P(('rep', 'fsdp'), 'tp'), may hold values from -6 to 6
- cond: float32 [8, 1536], P(('rep', 'fsdp')), may hold values from -6 to 6
- image_cotangent: bfloat16 [8, 896, 1536], P(('rep', 'fsdp'), 'tp'), may hold values from -6 to 6
- text_cotangent: bfloat16 [8, 128, 1536], P(('rep', 'fsdp'), 'tp'), may hold values from -6 to 6
- live: int32 [8], P(('rep', 'fsdp')), may hold values from 0 to 1, as said below
- slot_adapter_index: int32 [8], P(('rep', 'fsdp')), may hold values from 0 to 7
- modulation_weight: bfloat16 [2, 1536, 6, 1536], P(None, 'fsdp', None, 'tp'), may hold values from -0.15625 to 0.15625
- query_key_value_weight: bfloat16 [2, 1536, 3, 1536], P(None, 'fsdp', None, 'tp'), may hold values from -0.15625 to 0.15625
- output_weight: bfloat16 [2, 1536, 1536], P(None, 'tp', 'fsdp'), may hold values from -0.625 to 0.625
- first_feed_weight: bfloat16 [2, 1536, 6144], P(None, 'fsdp', 'tp'), may hold values from -0.15625 to 0.15625
- second_feed_weight: bfloat16 [2, 6144, 1536], P(None, 'tp', 'fsdp'), may hold values from -0.078125 to 0.078125
- adapter_down_table: bfloat16 [3, 2, 128, 1536], P(None, None, ('fsdp', 'tp')), may hold values from -0.15625 to 0.15625
- adapter_up_table: bfloat16 [2, 2, 128, 1536], P(None, None, ('fsdp', 'tp')), may hold values from -1.5 to 1.5
- modulation_up_factor: bfloat16 [2, 128, 6, 1536], P(None, 'fsdp', None, 'tp'), may hold values from -1.5 to 1.5
- query_key_value_up: bfloat16 [2, 128, 3, 1536], P(None, 'fsdp', None, 'tp'), may hold values from -1.5 to 1.5
- first_feed_up: bfloat16 [2, 128, 6144], P(None, 'fsdp', 'tp'), may hold values from -1.5 to 1.5
- output_down_factor: bfloat16 [2, 128, 1536], P(None, 'fsdp', 'tp'), may hold values from -0.625 to 0.625
- second_feed_down: bfloat16 [2, 128, 6144], P(None, 'fsdp', 'tp'), may hold values from -0.078125 to 0.078125
Outputs:
- out_img: bfloat16 [8, 896, 1536], P(('rep', 'fsdp'), 'tp')
- out_txt: bfloat16 [8, 128, 1536], P(('rep', 'fsdp'), 'tp')
- dx_img: bfloat16 [8, 896, 1536], P(('rep', 'fsdp'), 'tp')
- dx_txt: bfloat16 [8, 128, 1536], P(('rep', 'fsdp'), 'tp')
- dcond: float32 [8, 1536], P(('rep', 'fsdp'))
- grad_lora_in: float32 [3, 2, 128, 1536], P(None, None, ('fsdp', 'tp'))
- grad_lora_back: float32 [2, 2, 128, 1536], P(None, None, ('fsdp', 'tp'))
- grad_b_ada: float32 [2, 128, 6, 1536], P(None, 'fsdp', None, 'tp')
- grad_b_qkv: float32 [2, 128, 3, 1536], P(None, 'fsdp', None, 'tp')
- grad_b_fc1: float32 [2, 128, 6144], P(None, 'fsdp', 'tp')
- output_down_gradient: float32 [2, 128, 1536], P(None, 'fsdp', 'tp')
- grad_a_fc2: float32 [2, 128, 6144], P(None, 'fsdp', 'tp')
Inputs may be any that keep to these rules, and one draw needn't show every extreme that they name: `live`: slot 0 of each aligned block of 1 slots always holds a sequence; the others may be empty.
All inputs are finite; a program needn't handle non-finite values.
Results may differ from a plain program's by a relative error of at most 0.025.
The roundings to bfloat16 on the way count: a program that leaves them out, or rounds other values in their place, can miss the bound.
Values may be sent and summed in bfloat16 or wider, within the bound.
No kernel may reach another device: no remote copies, remote signals or barrier semaphores. Data moves between devices by JAX's collectives and lax.ppermute only.
A program may use at most 320 MiB of HBM per device.

v0:
```python
import functools

import jax
import jax.numpy as jnp
from jax import lax
from jax.experimental import pallas as pl
from jax.experimental.pallas import tpu as pltpu
from jax.sharding import PartitionSpec as P

HD = 64
RANK = 16
EPSILON = 1e-06
BF = jnp.bfloat16
F32 = jnp.float32
CORES = 2


def dot(left, right, dims):
    return lax.dot_general(left, right, (dims, ((), ())), preferred_element_type=F32)


def mm(left, right):
    return dot(left, right, ((left.ndim - 1,), (0,)))


def mm_t(left, right):
    return dot(left, right, ((left.ndim - 1,), (right.ndim - 1,)))


def t_mm(left, right):
    return dot(left, right, ((0,), (0,)))


def norm_rows(values):
    centred = values - jnp.mean(values, axis=-1, keepdims=True)
    inverse = lax.rsqrt(jnp.mean(centred * centred, axis=-1, keepdims=True) + EPSILON)
    return centred * inverse, inverse


def norm_back(grad_hat, hat, inverse):
    first = jnp.mean(grad_hat, axis=-1, keepdims=True)
    second = jnp.mean(grad_hat * hat, axis=-1, keepdims=True)
    return inverse * (grad_hat - first - hat * second)


def gelu_tanh(values):
    return jax.nn.gelu(values, approximate=True)


def head_tiles(width):
    if width % 128 == 0:
        return [(p * 128, 128, 2) for p in range(width // 128)]
    return [(h * HD, HD, 1) for h in range(width // HD)]


def head_masks(rows, count):
    if count == 1:
        return [None]
    lane = lax.broadcasted_iota(jnp.int32, (rows, 128), 1)
    return [lane < HD, lane >= HD]


def pick(mask, values):
    return values if mask is None else jnp.where(mask, values, jnp.zeros_like(values))


def attend_forward_kernel(width, q_ref, kv_ref, out_ref, lse_ref):
    rows = q_ref.shape[0]
    lses = []
    for start, size, count in head_tiles(width):
        queries = q_ref[:, start : start + size] * jnp.asarray(HD ** (-0.5), BF)
        keys = kv_ref[:, width + start : width + start + size]
        values = kv_ref[:, 2 * width + start : 2 * width + start + size]
        total = None
        for mask in head_masks(rows, count):
            scores = mm_t(pick(mask, queries), keys)
            top = jnp.max(scores, axis=-1, keepdims=True)
            weights = jnp.exp(scores - top)
            norm = jnp.sum(weights, axis=-1, keepdims=True)
            part = mm(weights.astype(BF), values) * (1.0 / norm)
            part = pick(mask, part)
            total = part if total is None else total + part
            lses.append(top + jnp.log(norm))
        out_ref[:, start : start + size] = total.astype(BF)
    lse_ref[...] = jnp.concatenate(lses, axis=1)


def attend_backward_kernel(width, blocks, q_ref, kv_ref, grad_ref, lse_ref, out_ref, dk_ref, dv_ref):
    step = pl.program_id(0)
    rows = q_ref.shape[0]

    @pl.when(step == 0)
    def _():
        dk_ref[...] = jnp.zeros_like(dk_ref)
        dv_ref[...] = jnp.zeros_like(dv_ref)

    row0 = pl.multiple_of(step * rows, rows)
    head = 0
    for start, size, count in head_tiles(width):
        queries = q_ref[:, start : start + size] * jnp.asarray(HD ** (-0.5), BF)
        keys = kv_ref[:, width + start : width + start + size]
        values = kv_ref[:, 2 * width + start : 2 * width + start + size]
        grads = grad_ref[:, start : start + size]
        grad_q = None
        for mask in head_masks(rows, count):
            queries_m = pick(mask, queries)
            grads_m = pick(mask, grads)
            scores = mm_t(queries_m, keys)
            probs = jnp.exp(scores - lse_ref[:, head : head + 1])
            grad_probs = mm_t(grads_m, values)
            product = probs * grad_probs
            inner = jnp.sum(product, axis=-1, keepdims=True)
            grad_scores = (product - probs * inner).astype(BF)
            part = pick(mask, mm(grad_scores, keys))
            grad_q = part if grad_q is None else grad_q + part
            dk_ref[:, start : start + size] += t_mm(grad_scores, queries_m)
            dv_ref[:, start : start + size] += t_mm(probs.astype(BF), grads_m)
            head += 1
        out_ref[pl.ds(row0, rows), start : start + size] = (grad_q * HD ** (-0.5)).astype(BF)

    @pl.when(step == blocks - 1)
    def _():
        out_ref[:, width : 2 * width] = dk_ref[...].astype(BF)
        out_ref[:, 2 * width :] = dv_ref[...].astype(BF)


def query_block(length):
    for rows in (256, 128, 64, 32, 16):
        if length % rows == 0:
            return rows
    return length


def attend_forward(joint):
    length, width3 = joint.shape
    width = width3 // 3
    heads = width // HD
    rows = query_block(length)
    return pl.pallas_call(
        functools.partial(attend_forward_kernel, width),
        grid=(length // rows,),
        in_specs=[
            pl.BlockSpec((rows, width3), lambda i: (i, 0)),
            pl.BlockSpec((length, width3), lambda i: (0, 0)),
        ],
        out_specs=[
            pl.BlockSpec((rows, width), lambda i: (i, 0)),
            pl.BlockSpec((rows, heads), lambda i: (i, 0)),
        ],
        out_shape=[
            jax.ShapeDtypeStruct((length, width), BF),
            jax.ShapeDtypeStruct((length, heads), F32),
        ],
        compiler_params=pltpu.CompilerParams(vmem_limit_bytes=40 * 1024 * 1024),
        cost_estimate=pl.CostEstimate(
            flops=4 * length * length * width,
            transcendentals=length * length * heads,
            bytes_accessed=length * width3 * 4,
        ),
        name="attend_forward",
    )(joint, joint)


def attend_backward(joint, grads, lse):
    length, width3 = joint.shape
    width = width3 // 3
    heads = width // HD
    rows = query_block(length)
    blocks = length // rows
    return pl.pallas_call(
        functools.partial(attend_backward_kernel, width, blocks),
        grid=(blocks,),
        in_specs=[
            pl.BlockSpec((rows, width3), lambda i: (i, 0)),
            pl.BlockSpec((length, width3), lambda i: (0, 0)),
            pl.BlockSpec((rows, width), lambda i: (i, 0)),
            pl.BlockSpec((rows, heads), lambda i: (i, 0)),
        ],
        out_specs=pl.BlockSpec((length, width3), lambda i: (0, 0)),
        out_shape=jax.ShapeDtypeStruct((length, width3), BF),
        scratch_shapes=[pltpu.VMEM((length, width), F32), pltpu.VMEM((length, width), F32)],
        compiler_params=pltpu.CompilerParams(vmem_limit_bytes=48 * 1024 * 1024),
        cost_estimate=pl.CostEstimate(
            flops=10 * length * length * width,
            transcendentals=length * length * heads,
            bytes_accessed=length * width3 * 8,
        ),
        name="attend_backward",
    )(joint, joint, grads, lse)


class Stream:
    pass


def powers(size):
    bits, bit = [], 1
    while bit < size:
        bits.append(bit)
        bit *= 2
    return bits


def body(
    mesh_shape,
    image_input,
    text_input,
    cond,
    image_cotangent,
    text_cotangent,
    live,
    slot_adapter_index,
    modulation_weight,
    query_key_value_weight,
    output_weight,
    first_feed_weight,
    second_feed_weight,
    adapter_down_table,
    adapter_up_table,
    modulation_up_factor,
    query_key_value_up,
    first_feed_up,
    output_down_factor,
    second_feed_down,
):
    R, F, T = mesh_shape
    H = T // CORES
    X = R // CORES
    W = image_input.shape[-1]
    wq = W // T
    Rf = modulation_up_factor.shape[1]
    Rq = adapter_down_table.shape[2]
    ffq = first_feed_weight.shape[-1]
    r = lax.axis_index("rep")
    f = lax.axis_index("fsdp")
    z = lax.axis_index("tp")
    core = lax.rem(r, CORES)
    xi = lax.div(r, CORES)
    high = lax.div(z, H)
    native = core == high
    shard = core * H + lax.rem(z, H)

    def xz(v, bit):
        return lax.ppermute(v, "tp", [(i, i ^ bit) for i in range(T)])

    def xf(v, bit):
        return lax.ppermute(v, "fsdp", [(i, i ^ bit) for i in range(F)])

    def xr(v, bit):
        return lax.ppermute(v, "rep", [(i, i ^ bit) for i in range(R)])

    swap_pairs = []
    for a in range(R):
        for b in range(T):
            here = a * T + b
            stays = a % CORES == b // H
            swap_pairs.append((here, here if stays else (a ^ 1) * T + (b ^ H)))

    def exchange(v):
        return lax.ppermute(v, ("rep", "tp"), swap_pairs)

    def gather_by(v, step, bits):
        blocks = v[None]
        for bit in bits:
            blocks = jnp.concatenate([blocks, step(blocks, bit)], axis=0)
        return blocks

    x_bits = [b for b in powers(R) if b > 1]
    h_bits = powers(H)
    t_bits = powers(T)
    f_bits = powers(F)
    arange_t = jnp.arange(T, dtype=jnp.int32)

    def gather_group(v):
        blocks = [v]
        for bit in h_bits:
            blocks = blocks + [xz(b, bit) for b in blocks]
        blocks = blocks + [xr(b, 1) for b in blocks]
        return jnp.concatenate(blocks, axis=0)

    def scatter_group(v):
        half = v.shape[0] // 2
        v = v[:half] + xr(v[half:], 1)
        for bit in reversed(h_bits):
            half = v.shape[0] // 2
            v = v[:half] + xz(v[half:], bit)
        return v

    def gather_text(v):
        for bit in t_bits:
            v = jnp.concatenate([v, xz(v, bit)], axis=0)
        return v

    def scatter_text(v):
        for bit in reversed(t_bits):
            half = v.shape[0] // 2
            v = v[:half] + xz(v[half:], bit)
        return v

    def to_relative(v, index):
        n = v.shape[-1] // T
        blocks = jnp.moveaxis(v.reshape(v.shape[:-1] + (T, n)), -2, 0)
        return jnp.take(blocks, jnp.bitwise_xor(index, arange_t), axis=0)

    silu = jax.nn.silu(cond).astype(BF)
    info = jnp.concatenate(
        [
            silu.astype(F32),
            jnp.broadcast_to(slot_adapter_index.astype(F32)[:, None], (1, 64)),
            jnp.broadcast_to(live.astype(F32)[:, None], (1, 64)),
        ],
        axis=1,
    )
    info_f = gather_by(info[0], xf, f_bits)
    info_all = gather_by(info_f, xr, [1] + x_bits)
    silu_f = info_f[:, :W].astype(BF)
    ids_f = info_f[:, W].astype(jnp.int32)
    ids_all = info_all[:, :, W].astype(jnp.int32)
    silu_all = info_all[:, :, :W].astype(BF)
    my_id = slot_adapter_index[0]
    alive_txt = live.astype(F32)[0]
    alive_img = jnp.where(native, alive_txt, info_all[1, 0, W + 64])

    img = exchange(image_input[0])
    img_cot = exchange(image_cotangent[0])
    txt = text_input[0]
    txt_cot = text_cotangent[0]

    down_ada = adapter_down_table[0]
    down_rel = gather_by(down_ada, xz, t_bits)
    rank_rel = jnp.einsum("fd,tkid->tfki", silu_f, down_rel, preferred_element_type=F32)
    rank_abs = jnp.take(rank_rel, jnp.bitwise_xor(z, arange_t), axis=0)
    rank_rows = jnp.moveaxis(rank_abs, 0, 2).reshape(F, 2, Rf)
    row_ids = f * Rf + jnp.arange(Rf, dtype=jnp.int32)
    row_adapter = lax.div(row_ids, RANK)
    own_rows = (row_adapter[None] == ids_f[:, None])[:, None, :]
    rank_rows = jnp.where(own_rows, rank_rows, 0.0).astype(BF)
    rows_d = modulation_weight.shape[1]
    silu_rows = lax.dynamic_slice_in_dim(silu_f, f * rows_d, rows_d, axis=1)
    parts = []
    for k in range(2):
        parts.append(
            jnp.einsum("fd,dcj->fcj", silu_rows, modulation_weight[k], preferred_element_type=F32)
            + jnp.einsum(
                "fr,rcj->fcj", rank_rows[:, k], modulation_up_factor[k], preferred_element_type=F32
            )
        )
    partial_mod = jnp.stack(parts, axis=1)
    mod_shard = partial_mod[0]
    for d in range(1, F):
        mod_shard = mod_shard + xf(partial_mod[d], d)
    mod_rel = gather_by(mod_shard, xz, t_bits)
    mod_abs = jnp.take(mod_rel, jnp.bitwise_xor(z, arange_t), axis=0)
    mod_all = jnp.moveaxis(mod_abs, 0, 2).reshape(2, 6, W)
    mod_img = jnp.where(native, mod_all[0], xr(mod_all[0], 1))
    mod_txt = mod_all[1]

    tables = jnp.concatenate([adapter_down_table[1:], adapter_up_table], axis=0)
    base_row = f * Rf + z * Rq

    def own_table_rows(ident):
        wanted = ident * RANK + jnp.arange(RANK, dtype=jnp.int32)
        held = base_row + jnp.arange(Rq, dtype=jnp.int32)
        if Rq == RANK:
            return jnp.where(ident * RANK == base_row, tables, jnp.zeros_like(tables))
        match = (wanted[:, None] == held[None, :]).astype(BF)
        return jnp.einsum("ir,ksrw->ksiw", match, tables, preferred_element_type=F32).astype(BF)

    table_rows = own_table_rows(ids_f[0])
    for d in range(1, F):
        table_rows = table_rows + xf(own_table_rows(ids_f[d]), d)
    for bit in t_bits:
        table_rows = table_rows + xz(table_rows, bit)
    rows_txt = table_rows[:, 1]
    rows_img = jnp.where(native, table_rows[:, 0], xr(table_rows[:, 0], 1))

    columns = jnp.concatenate(
        [
            query_key_value_up.reshape(2, Rf, 3 * wq),
            first_feed_up,
            output_down_factor,
            second_feed_down,
        ],
        axis=2,
    )

    def own_columns(ident):
        start = ident * RANK - f * Rf
        inside = (start >= 0) & (start <= Rf - RANK)
        taken = lax.dynamic_slice_in_dim(columns, jnp.clip(start, 0, Rf - RANK), RANK, axis=1)
        return jnp.where(inside, taken, jnp.zeros_like(taken))

    column_rows = own_columns(ids_f[0])
    for d in range(1, F):
        column_rows = column_rows + xf(own_columns(ids_f[d]), d)
    cols_txt = column_rows[1]
    cols_img = exchange(column_rows[0])
    cuts = (0, 3 * wq, 3 * wq + ffq, 4 * wq + ffq, 4 * wq + 2 * ffq)

    def stream(rows, cols, mod, tokens, cotangent, alive, gather, scatter):
        s = Stream()
        s.a_qkv, s.a_fc1, s.b_out, s.b_fc2 = rows[0], rows[1], rows[2], rows[3]
        s.b_qkv = cols[:, cuts[0] : cuts[1]]
        s.b_fc1 = cols[:, cuts[1] : cuts[2]]
        s.a_out = cols[:, cuts[2] : cuts[3]]
        s.a_fc2 = cols[:, cuts[3] : cuts[4]]
        s.mod, s.x, s.cot, s.live = mod, tokens, cotangent, alive
        s.gather, s.scatter = gather, scatter
        return s

    def place(shape, pieces, axis):
        full = jnp.zeros(shape, BF)
        for piece, offset in pieces:
            full = lax.dynamic_update_slice_in_dim(full, piece, offset, axis=axis)
        return full

    def fetch_image(weight, axis, share):
        rows, cols = weight.shape
        part = rows // X
        mine = lax.dynamic_slice_in_dim(weight, xi * part, part, axis=0)
        moved = gather_by(exchange(mine), xr, x_bits)
        held = place((rows, cols), [(moved[e], (xi ^ e) * part) for e in range(X)], 0)
        held = jnp.where(native, weight, held)
        full_shape = (rows * F, cols) if axis == 0 else (rows, cols * F)
        size = weight.shape[axis]
        full = place(full_shape, [(held, f * size)], axis)
        for d in range(1, F):
            if share:
                piece = xf(lax.dynamic_slice_in_dim(held, xi * part, part, axis=0), d)
                pieces = gather_by(piece, xr, x_bits)
                for e in range(X):
                    start = [0, 0]
                    start[axis] = (f ^ d) * size
                    start[0] = start[0] + (xi ^ e) * part
                    full = lax.dynamic_update_slice(full, pieces[e], start)
            else:
                full = lax.dynamic_update_slice_in_dim(full, xf(held, d), (f ^ d) * size, axis=axis)
        return full

    def fetch_text(weight, axis):
        rows, cols = weight.shape
        part = rows // R
        mine = lax.dynamic_slice_in_dim(weight, r * part, part, axis=0)
        full_shape = (rows * F, cols) if axis == 0 else (rows, cols * F)
        size = weight.shape[axis]
        full = place(full_shape, [(weight, f * size)], axis)
        for d in range(1, F):
            pieces = gather_by(xf(mine, d), xr, x_bits + [1])
            order = [0]
            for bit in x_bits + [1]:
                order = order + [o ^ bit for o in order]
            for e in range(R):
                start = [0, 0]
                start[axis] = (f ^ d) * size
                start[0] = start[0] + (r ^ order[e]) * part
                full = lax.dynamic_update_slice(full, pieces[e], start)
        return full

    qkv_native = query_key_value_weight.reshape(2, rows_d, 3 * wq)
    image = stream(rows_img, cols_img, mod_img, img, img_cot, alive_img, gather_group, scatter_group)
    text = stream(rows_txt, cols_txt, mod_txt, txt, txt_cot, alive_txt, gather_text, scatter_text)
    streams = (image, text)
    image.w_qkv = fetch_image(qkv_native[0], 0, False)
    image.w_out = fetch_image(output_weight[0], 1, True)
    image.w_fc1 = fetch_image(first_feed_weight[0], 0, True)
    image.w_fc2 = fetch_image(second_feed_weight[0], 1, True)
    text.w_qkv = fetch_text(qkv_native[1], 0)
    text.w_out = fetch_text(output_weight[1], 1)
    text.w_fc1 = fetch_text(first_feed_weight[1], 0)
    text.w_fc2 = fetch_text(second_feed_weight[1], 1)

    for s in streams:
        mod = s.mod
        s.xf = s.x.astype(F32)
        s.hat1, s.inv1 = norm_rows(s.xf)
        normed = (s.hat1 * (1.0 + mod[1:2]) + mod[0:1]).astype(BF)
        s.n1 = s.gather(normed)
        s.g2 = s.cot.astype(F32) * s.live
        s.gb_mlp = s.gather((mod[5:6] * s.g2).astype(BF))
        s.rank_qkv = mm_t(s.n1, s.a_qkv).astype(BF)
        s.joint = (mm(s.n1, s.w_qkv) + mm(s.rank_qkv, s.b_qkv)).astype(BF)
    img_len = image.joint.shape[0]
    joint = jnp.concatenate([image.joint, exchange(text.joint)], axis=0)
    attended, lse = attend_forward(joint)
    image.att = attended[:img_len]
    text.att = exchange(attended[img_len:])
    for s in streams:
        mod = s.mod
        s.rank_out = mm_t(s.att, s.a_out).astype(BF)
        partial = mm(s.att, s.w_out) + mm(s.rank_out, s.b_out)
        s.br_attn = s.scatter(partial.astype(BF)).astype(F32)
        s.after = s.xf + mod[2:3] * s.br_attn
        s.hat2, s.inv2 = norm_rows(s.after)
        normed = (s.hat2 * (1.0 + mod[4:5]) + mod[3:4]).astype(BF)
        s.n2 = s.gather(normed)
        s.rank_fc1 = mm_t(s.n2, s.a_fc1).astype(BF)
        s.hidden = mm(s.n2, s.w_fc1) + mm(s.rank_fc1, s.b_fc1)
        s.act = gelu_tanh(s.hidden).astype(BF)
        s.rank_fc2 = mm_t(s.act, s.a_fc2).astype(BF)
        partial = mm(s.act, s.w_fc2) + mm(s.rank_fc2, s.b_fc2)
        s.br_mlp = s.scatter(partial.astype(BF)).astype(F32)
        s.out = ((s.after + mod[5:6] * s.br_mlp) * s.live).astype(BF)

    for s in streams:
        mod = s.mod
        s.gg_mlp = jnp.sum(s.g2 * s.br_mlp, axis=0)
        gb = s.gb_mlp
        gr_fc2 = mm_t(gb, s.b_fc2).astype(BF)
        s.t_back1 = t_mm(s.rank_fc2, gb)
        grad_act = mm_t(gb, s.w_fc2) + mm(gr_fc2, s.a_fc2)
        _, pull = jax.vjp(gelu_tanh, s.hidden)
        gh = pull(grad_act)[0].astype(BF)
        s.t_a_fc2 = t_mm(gr_fc2, s.act)
        s.t_b_fc1 = t_mm(s.rank_fc1, gh)
        gr_fc1 = mm_t(gh, s.b_fc1).astype(BF)
        s.t_in2 = t_mm(gr_fc1, s.n2)
        partial = mm_t(gh, s.w_fc1) + mm(gr_fc1, s.a_fc1)
        gn2 = s.scatter(partial.astype(BF)).astype(F32)
        s.gs_mlp = jnp.sum(gn2, axis=0)
        s.gc_mlp = jnp.sum(gn2 * s.hat2, axis=0)
        s.g_after = s.g2 + norm_back(gn2 * (1.0 + mod[4:5]), s.hat2, s.inv2)
        s.gg_attn = jnp.sum(s.g_after * s.br_attn, axis=0)
        gb = s.gather((mod[2:3] * s.g_after).astype(BF))
        gr_out = mm_t(gb, s.b_out).astype(BF)
        s.t_back0 = t_mm(s.rank_out, gb)
        s.g_att = (mm_t(gb, s.w_out) + mm(gr_out, s.a_out)).astype(BF)
        s.t_a_out = t_mm(gr_out, s.att)

    def combine(pieces):
        blocks = gather_by(gather_by(pieces, xf, f_bits), xr, [1] + x_bits)
        flat = blocks.reshape(R * F * RANK, pieces.shape[-1])
        slots = (ids_all[:, :, None] * RANK + jnp.arange(RANK, dtype=jnp.int32)).reshape(1, -1)
        place_rows = (row_ids[:, None] == slots).astype(BF)
        return mm(place_rows, flat)

    def reduce_rows(img_rows, txt_rows):
        def fold(rows, index, scatter):
            blocks = to_relative(rows, index)
            n = blocks.shape[1]
            return scatter(blocks.reshape(T * n, wq)).reshape(n, wq)

        return exchange(fold(img_rows, shard, scatter_group)), fold(txt_rows, z, scatter_text)

    def rows_home(rows):
        kinds = rows.shape[1]
        blocks = rows.astype(BF).reshape(T, Rq, kinds, wq)
        blocks = jnp.take(blocks, jnp.bitwise_xor(z, arange_t), axis=0)
        got = jnp.stack([blocks[0]] + [xz(blocks[d], d) for d in range(1, T)])
        got = jnp.take(got, jnp.bitwise_xor(z, arange_t), axis=0)
        return jnp.moveaxis(got, 0, 2).reshape(Rq, kinds, W).astype(F32)

    early_rows = reduce_rows(
        *[jnp.concatenate([s.t_back1, s.t_in2, s.t_back0], axis=0).astype(BF) for s in streams]
    )
    early_img = exchange(
        jnp.concatenate([image.t_b_fc1, image.t_a_fc2, image.t_a_out], axis=1).astype(BF)
    )
    early_txt = jnp.concatenate([text.t_b_fc1, text.t_a_fc2, text.t_a_out], axis=1).astype(BF)

    def lay(rows, kinds):
        return [rows[i * RANK : (i + 1) * RANK] for i in range(kinds)]

    early = combine(
        jnp.concatenate([early_img, early_txt] + lay(early_rows[0], 3) + lay(early_rows[1], 3), axis=1)
    )
    span = 2 * ffq + wq
    grad_b_fc1 = jnp.stack([early[:, 0:ffq], early[:, span : span + ffq]])
    grad_a_fc2 = jnp.stack([early[:, ffq : 2 * ffq], early[:, span + ffq : span + 2 * ffq]])
    grad_a_out = jnp.stack([early[:, 2 * ffq : span], early[:, span + 2 * ffq : 2 * span]])
    home = rows_home(early[:, 2 * span :].reshape(Rf, 6, wq))

    g_att = jnp.concatenate([image.g_att, exchange(text.g_att)], axis=0)
    g_joint = attend_backward(joint, g_att, lse)
    image.g_joint = g_joint[:img_len]
    text.g_joint = exchange(g_joint[img_len:])
    for s in streams:
        mod = s.mod
        gj = s.g_joint
        gr_qkv = mm_t(gj, s.b_qkv).astype(BF)
        partial = mm_t(gj, s.w_qkv) + mm(gr_qkv, s.a_qkv)
        gn1 = s.scatter(partial.astype(BF)).astype(F32)
        s.t_b_qkv = t_mm(s.rank_qkv, gj)
        s.t_in1 = t_mm(gr_qkv, s.n1)
        s.gs_attn = jnp.sum(gn1, axis=0)
        s.gc_attn = jnp.sum(gn1 * s.hat1, axis=0)
        dx = s.g_after + norm_back(gn1 * (1.0 + mod[1:2]), s.hat1, s.inv1)
        s.dx = dx.astype(BF)
    late_rows = reduce_rows(
        *[
            jnp.concatenate(
                [
                    s.t_in1,
                    jnp.stack(
                        [s.gs_attn, s.gc_attn, s.gg_attn, s.gs_mlp, s.gc_mlp, s.gg_mlp]
                    ),
                ],
                axis=0,
            )
            for s in streams
        ]
    )
    gm = jnp.stack([rows[RANK:] for rows in late_rows]).astype(BF)
    gm_f = gather_by(gm, xf, f_bits)
    gm_all = gather_by(gm_f, xr, [1] + x_bits)

    late = combine(
        jnp.concatenate(
            [exchange(image.t_b_qkv.astype(BF)), text.t_b_qkv.astype(BF)]
            + [rows[:RANK].astype(BF) for rows in late_rows],
            axis=1,
        )
    )
    grad_b_qkv = jnp.stack([late[:, : 3 * wq], late[:, 3 * wq : 6 * wq]]).reshape(2, Rf, 3, wq)
    home_late = rows_home(late[:, 6 * wq :].reshape(Rf, 2, wq))

    seqs = R * F
    match = (row_adapter[None, :] == ids_all.reshape(seqs)[:, None]).astype(F32)
    gm_seq = gm_all.reshape(seqs, 2, 6, wq)
    rank_seq_rel = jnp.einsum(
        "sd,tkid->stki", silu_all.reshape(seqs, W), down_rel, preferred_element_type=F32
    )
    rank_seq = jnp.take(rank_seq_rel, jnp.bitwise_xor(z, arange_t), axis=1)
    rank_seq = jnp.moveaxis(rank_seq, 1, 2).reshape(seqs, 2, Rf)
    rank_seq = (rank_seq * match[:, None, :]).astype(BF)
    grad_b_ada, gcr = [], []
    for k in range(2):
        grad_b_ada.append(
            jnp.einsum("sr,scj->rcj", rank_seq[:, k], gm_seq[:, k], preferred_element_type=F32)
        )
        gcr.append(
            jnp.einsum(
                "scj,rcj->sr", gm_seq[:, k], modulation_up_factor[k], preferred_element_type=F32
            )
            * match
        )
    grad_b_ada = jnp.stack(grad_b_ada)
    gcr = jnp.stack(gcr, axis=1)
    gcr_rel = jnp.take(
        jnp.moveaxis(gcr.reshape(seqs, 2, T, Rq), 2, 0), jnp.bitwise_xor(z, arange_t), axis=0
    )
    gcr_own = gcr_rel[0]
    for d in range(1, T):
        gcr_own = gcr_own + xz(gcr_rel[d], d)
    grad_in0 = jnp.einsum(
        "ski,sd->kid",
        gcr_own,
        silu_all.reshape(seqs, W).astype(F32),
        precision=lax.Precision.HIGHEST,
    )
    gm_pair = gm_f
    dpart = jnp.zeros((F, rows_d), F32)
    for k in range(2):
        dpart = dpart + jnp.einsum(
            "fcj,dcj->fd", gm_pair[:, k], modulation_weight[k], preferred_element_type=F32
        )
    dfull = lax.dynamic_update_slice_in_dim(jnp.zeros((F, W), F32), dpart, f * rows_d, axis=1)
    gcr_pair = gcr.reshape(R, F, 2, T, Rq)[0]
    gcr_pair = jnp.take(gcr_pair, jnp.bitwise_xor(z, arange_t), axis=2)
    dfull = dfull + jnp.einsum(
        "fkti,tkid->fd",
        gcr_pair,
        down_rel.astype(F32),
        precision=lax.Precision.HIGHEST,
    )
    dsum = dfull[0]
    for d in range(1, F):
        dsum = dsum + xf(dfull[d], d)
    for bit in t_bits:
        dsum = dsum + xz(dsum, bit)
    sigmoid = jax.nn.sigmoid(cond)
    dcond = dsum[None] * sigmoid * (1.0 + cond * (1.0 - sigmoid))

    grad_in = jnp.stack(
        [
            grad_in0,
            jnp.moveaxis(home_late, 1, 0),
            jnp.stack([home[:, 1], home[:, 4]]),
        ]
    )
    grad_back = jnp.stack(
        [jnp.stack([home[:, 2], home[:, 5]]), jnp.stack([home[:, 0], home[:, 3]])]
    )
    return (
        exchange(image.out)[None],
        text.out[None],
        exchange(image.dx)[None],
        text.dx[None],
        dcond,
        grad_in,
        grad_back,
        grad_b_ada,
        grad_b_qkv,
        grad_b_fc1,
        grad_a_out,
        grad_a_fc2,
    )


def solution(mesh):
    tokens = P(("rep", "fsdp"), "tp", None)
    table = P(None, None, ("fsdp", "tp"), None)
    columns4 = P(None, "fsdp", None, "tp")
    columns3 = P(None, "fsdp", "tp")
    rows3 = P(None, "tp", "fsdp")
    slot = P(("rep", "fsdp"))
    in_specs = (
        tokens, tokens, P(("rep", "fsdp"), None), tokens, tokens, slot, slot,
        columns4, columns4, rows3, columns3, rows3, table, table,
        columns4, columns4, columns3, columns3, columns3,
    )
    out_specs = (
        tokens, tokens, tokens, tokens, P(("rep", "fsdp"), None),
        table, table, columns4, columns4, columns3, columns3, columns3,
    )
    sizes = (mesh.shape["rep"], mesh.shape["fsdp"], mesh.shape["tp"])
    return jax.shard_map(
        functools.partial(body, sizes), mesh=mesh, in_specs=in_specs, out_specs=out_specs, check_vma=False
    )
```

profile of v0, /device:TPU:0, one launch (start us, length us, event | category | flops | bytes accessed | tf_op | source)
XLA Modules:
  0.0 893.3 jit_solution(9134751751673669946)
XLA Ops:
  8.5 8.2 collective-permute-start.11
  135.5 6.8 collective-permute-done.14
  148.5 6.7 dynamic_update_slice.125
  163.5 11.5 %collective-permute-done.58 = bf16[384,768]{1,0:T(8,128)(2,1)} collective-permute-done((bf16[384,768]{1,0:T(8,128)(2,1)}, bf16[384,768]{1,0:T(8,128)(2,1)}, u32[]{:S(2)}, u32[]{:S(2)}) %collective-permute-start.58) | collective-permute-done | bytes 589856 | tf_op jit(solution)/shard_map/ppermute | solution.py:247
  193.7 6.6 collective-permute-done.15
  200.3 10.4 %collective-permute-start.35 = (bf16[384,1536]{1,0:T(8,128)(2,1)}, bf16[384,1536]{1,0:T(8,128)(2,1)}, u32[]{:S(2)}, u32[]{:S(2)}) collective-permute-start(bf16[384,1536]{1,0:T(8,128)(2,1)} %dynamic-slice_bitcast_fusion.1), channel_id=1, source_target_pairs={{0,0},{1,1},{2,8},{3,9},{8,2},{9,3},{10,10},{11,11},{16,16},{17,17... | collective-permute-start | bytes 3538952 | tf_op jit(solution)/shard_map/ppermute | solution.py:260
  211.5 10.4 %collective-permute-start.39 = (bf16[768,768]{1,0:T(8,128)(2,1)}, bf16[768,768]{1,0:T(8,128)(2,1)}, u32[]{:S(2)}, u32[]{:S(2)}) collective-permute-start(bf16[768,768]{1,0:T(8,128)(2,1)} %dynamic-slice_bitcast_fusion), channel_id=1, source_target_pairs={{0,0},{1,1},{2,8},{3,9},{8,2},{9,3},{10,10},{11,11},{16,16},{17,17... | collective-permute-start | bytes 3538952 | tf_op jit(solution)/shard_map/ppermute | solution.py:260
  231.8 6.5 dynamic_update_slice.126
  257.1 13.3 %collective-permute-start.16 = (bf16[4,2,16,1536]{3,2,1,0:T(8,128)(2,1)S(1)}, bf16[4,2,16,1536]{3,2,1,0:T(8,128)(2,1)S(1)}, u32[]{:S(2)}, u32[]{:S(2)}) collective-permute-start(bf16[4,2,16,1536]{3,2,1,0:T(8,128)(2,1)S(1)} %copy-done.43), channel_id=1, source_target_pairs={{0,2},{1,3},{2,0},{3,1},{4,6},{5,7},{6,4},{7,5},{8,10},{9,11},{10,... | collective-permute-start | bytes 1179656 | tf_op jit(solution)/shard_map/ppermute | solution.py:244
  273.0 20.5 %collective-permute-done.16 = bf16[4,2,16,1536]{3,2,1,0:T(8,128)(2,1)S(1)} collective-permute-done((bf16[4,2,16,1536]{3,2,1,0:T(8,128)(2,1)S(1)}, bf16[4,2,16,1536]{3,2,1,0:T(8,128)(2,1)S(1)}, u32[]{:S(2)}, u32[]{:S(2)}) %collective-permute-start.16) | collective-permute-done | bytes 393248 | tf_op jit(solution)/shard_map/ppermute | solution.py:244
  302.2 7.4 dynamic_update_slice.127
  309.6 7.1 dynamic_update_slice.128
  344.7 13.2 %collective-permute-done.36 = bf16[1,384,1536]{2,1,0:T(8,128)(2,1)S(1)} collective-permute-done((bf16[1,384,1536]{2,1,0:T(8,128)(2,1)}, bf16[1,384,1536]{2,1,0:T(8,128)(2,1)S(1)}, u32[]{:S(2)}, u32[]{:S(2)}) %collective-permute-start.36) | collective-permute-done | bytes 1179680 | tf_op jit(solution)/shard_map/ppermute | solution.py:250
  361.9 20.7 %collective-permute-done.40 = bf16[1,768,768]{2,1,0:T(8,128)(2,1)S(1)} collective-permute-done((bf16[1,768,768]{2,1,0:T(8,128)(2,1)}, bf16[1,768,768]{2,1,0:T(8,128)(2,1)S(1)}, u32[]{:S(2)}, u32[]{:S(2)}) %collective-permute-start.40) | collective-permute-done | bytes 1179680 | tf_op jit(solution)/shard_map/ppermute | solution.py:250
  394.4 6.4 fusion.7
  402.0 12.6 %attend_forward.1 = (bf16[1024,384]{1,0:T(8,128)(2,1)S(1)}, f32[1024,6]{1,0:T(8,128)S(1)}) custom-call(bf16[1024,1152]{1,0:T(8,128)(2,1)S(1)} %pad_maximum_fusion.4.q_ref.kv_ref, bf16[1024,1152]{1,0:T(8,128)(2,1)S(1)} %pad_maximum_fusion.4.q_ref.kv_ref), custom_call_target="tpu_custom_call" | custom-call | flops 1610612736 | bytes 4718592 | tf_op jit(solution)/shard_map/attend_forward/pallas_call | solution.py:139
  426.2 8.7 collective-permute-done.51
  443.8 14.3 %dynamic_update_slice.142 = bf16[1536,1536]{1,0:T(8,128)(2,1)S(1)} dynamic-update-slice(bf16[1536,1536]{1,0:T(8,128)(2,1)S(1)} %get-tuple-element.96, bf16[768,768]{1,0:T(8,128)(2,1)} %collective-permute-done.41, s32[]{:T(128)S(6)} %select_n.315, s32[]{:T(128)S(6)} %select_n.290) | dynamic-update-slice | bytes 2359300 | tf_op jit(solution)/shard_map/dynamic_update_slice | solution.py:435
  461.1 9.1 %collective-permute-done.54 = bf16[64,1536]{1,0:T(8,128)(2,1)S(1)} collective-permute-done((bf16[64,1536]{1,0:T(8,128)(2,1)S(1)}, bf16[64,1536]{1,0:T(8,128)(2,1)S(1)}, u32[]{:S(2)}, u32[]{:S(2)}) %collective-permute-start.54) | collective-permute-done | bytes 196640 | tf_op jit(solution)/shard_map/ppermute | solution.py:244
  486.6 9.5 %collective-permute-done.74 = bf16[64,1536]{1,0:T(8,128)(2,1)S(1)} collective-permute-done((bf16[64,1536]{1,0:T(8,128)(2,1)S(1)}, bf16[64,1536]{1,0:T(8,128)(2,1)S(1)}, u32[]{:S(2)}, u32[]{:S(2)}) %collective-permute-start.74) | collective-permute-done | bytes 196640 | tf_op jit(solution)/shard_map/ppermute | solution.py:244
  514.7 9.3 %collective-permute-done.31 = bf16[224,1536]{1,0:T(8,128)(2,1)} collective-permute-done((bf16[224,1536]{1,0:T(8,128)(2,1)}, bf16[224,1536]{1,0:T(8,128)(2,1)}, u32[]{:S(2)}, u32[]{:S(2)}) %collective-permute-start.31) | collective-permute-done | bytes 688160 | tf_op jit(solution)/shard_map/ppermute | solution.py:244
  534.5 13.9 %collective-permute-done.32 = bf16[224,1536]{1,0:T(8,128)(2,1)} collective-permute-done((bf16[224,1536]{1,0:T(8,128)(2,1)}, bf16[224,1536]{1,0:T(8,128)(2,1)}, u32[]{:S(2)}, u32[]{:S(2)}) %collective-permute-start.32) | collective-permute-done | bytes 688160 | tf_op jit(solution)/shard_map/ppermute | solution.py:244
  562.0 9.7 %multiply_convert_fusion = (bf16[896,1536]{1,0:T(8,128)(2,1)S(1)}, f32[896,1536]{1,0:T(8,128)}) fusion(f32[896,1536]{1,0:T(8,128)S(1)} %fusion.168, bf16[1536,1536]{1,0:T(8,128)(2,1)S(1)} %bitcast.578, bf16[224,1536]{1,0:T(8,128)(2,1)} %collective-permute-done.34, bf16[224,1536]{1,0:T(8,128)(2,1)} %collective-permute-done.33, ...), kind=kOutput, calls=%fused_computation.25 | convolution fusion | flops 4252631040 | bytes 21233664 | tf_op jit(solution)/shard_map/dot_general | solution.py:19
  572.1 12.2 %fusion.6 = bf16[896,1536]{1,0:T(8,128)(2,1)S(1)} fusion(f32[896,1536]{1,0:T(8,128)} %get-tuple-element.174, f32[896,1536]{1,0:T(8,128)S(1)} %bitcast.574, bf16[1536,1536]{1,0:T(8,128)(2,1)} %bitcast_dynamic-update-slice_fusion.2, bf16[224,1536]{1,0:T(8,128)(2,1)S(1)} %copy-done.159, bf16[224,1536]{1,0:T(8,128)(2,1)S(1)} %copy-done.156, ...), kind=kOutput, calls=%fused_computation.21 | convolution fusion | flops 4267769856 | bytes 21233664 | tf_op jit(solution)/shard_map/dot_general | solution.py:19
  587.0 7.1 add_convert_fusion.1
  612.1 12.9 %collective-permute-done.68 = bf16[224,1536]{1,0:T(8,128)(2,1)S(1)} collective-permute-done((bf16[224,1536]{1,0:T(8,128)(2,1)S(1)}, bf16[224,1536]{1,0:T(8,128)(2,1)S(1)}, u32[]{:S(2)}, u32[]{:S(2)}) %collective-permute-start.68) | collective-permute-done | bytes 688160 | tf_op jit(solution)/shard_map/ppermute | solution.py:244
  626.6 13.3 %collective-permute-done.44 = bf16[224,1536]{1,0:T(8,128)(2,1)S(1)} collective-permute-done((bf16[224,1536]{1,0:T(8,128)(2,1)S(1)}, bf16[224,1536]{1,0:T(8,128)(2,1)S(1)}, u32[]{:S(2)}, u32[]{:S(2)}) %collective-permute-start.44) | collective-permute-done | bytes 688160 | tf_op jit(solution)/shard_map/ppermute | solution.py:244
  653.7 6.9 collective-permute-start.46
  681.9 23.3 %attend_backward.1 = bf16[1024,1152]{1,0:T(8,128)(2,1)S(1)} custom-call(bf16[1024,1152]{1,0:T(8,128)(2,1)S(1)} %pad_maximum_fusion.4.q_ref.kv_ref, bf16[1024,1152]{1,0:T(8,128)(2,1)S(1)} %pad_maximum_fusion.4.q_ref.kv_ref, bf16[1024,384]{1,0:T(8,128)(2,1)S(1)} %pad_maximum_fusion.11.grad_ref, f32[1024,6]{1,0:T(8,128)S(1)} %copy-done.3), custom_call_target="tpu_custom_call" | custom-call | flops 4026531840 | bytes 9437184 | tf_op jit(solution)/shard_map/attend_backward/pallas_call | solution.py:170
  748.6 7.7 collective-permute-start.83
  756.4 9.2 %collective-permute-done.83 = bf16[64,1536]{1,0:T(8,128)(2,1)S(1)} collective-permute-done((bf16[64,1536]{1,0:T(8,128)(2,1)S(1)}, bf16[64,1536]{1,0:T(8,128)(2,1)S(1)}, u32[]{:S(2)}, u32[]{:S(2)}) %collective-permute-start.83) | collective-permute-done | bytes 196640 | tf_op jit(solution)/shard_map/ppermute | solution.py:244
  786.7 12.9 %collective-permute-done.80 = bf16[224,1536]{1,0:T(8,128)(2,1)S(1)} collective-permute-done((bf16[224,1536]{1,0:T(8,128)(2,1)S(1)}, bf16[224,1536]{1,0:T(8,128)(2,1)S(1)}, u32[]{:S(2)}, u32[]{:S(2)}) %collective-permute-start.80) | collective-permute-done | bytes 688160 | tf_op jit(solution)/shard_map/ppermute | solution.py:244
  (1020 shorter events, 536.7 us)
Async XLA Ops:
  8.5 215.5 %collective-permute-start.11 = (bf16[384,1152]{0,1:T(8,128)(2,1)}, bf16[384,1152]{0,1:T(8,128)(2,1)}, u32[]{:S(2)}, u32[]{:S(2)}) collective-permute-start(bf16[384,1152]{0,1:T(8,128)(2,1)} %constant_dynamic-slice_fusion.5), channel_id=1, source_target_pairs={{0,0},{1,1},{2,8},{3,9},{8,2},{9,3},{10,10},{11,11},{16,16},{17,17... | collective-permute-start | bytes 2654216 | tf_op jit(solution)/shard_map/ppermute | solution.py:260
  18.8 52.4 %collective-permute-start.1 = (f32[1,1664]{1,0:T(1,128)S(1)}, f32[1,1664]{1,0:T(1,128)S(1)}, u32[]{:S(2)}, u32[]{:S(2)}) collective-permute-start(f32[1,1664]{1,0:T(1,128)S(1)} %concatenate.202), channel_id=1, source_target_pairs={{0,4},{4,0},{1,5},{5,1},{2,6},{6,2},{3,7},{7,3},{8,12},{12,8},{9,1... | collective-permute-start | bytes 19976 | tf_op jit(solution)/shard_map/ppermute | solution.py:247
  22.6 61.6 %collective-permute-start.2 = (bf16[1,2,16,1536]{3,2,1,0:T(8,128)(2,1)S(1)}, bf16[1,2,16,1536]{3,2,1,0:T(8,128)(2,1)S(1)}, u32[]{:S(2)}, u32[]{:S(2)}) collective-permute-start(bf16[1,2,16,1536]{3,2,1,0:T(8,128)(2,1)S(1)} %slice.574), channel_id=1, source_target_pairs={{0,1},{1,0},{2,3},{3,2},{4,5},{5,4},{6,7},{7,6},{8,9},{9,8},{10,11... | collective-permute-start | bytes 294920 | tf_op jit(solution)/shard_map/ppermute | solution.py:244
  24.2 162.9 %collective-permute-start = (bf16[224,1536]{1,0:T(8,128)(2,1)}, bf16[224,1536]{1,0:T(8,128)(2,1)S(1)}, u32[]{:S(2)}, u32[]{:S(2)}) collective-permute-start(bf16[224,1536]{1,0:T(8,128)(2,1)} %bitcast.622), channel_id=1, source_target_pairs={{0,0},{1,1},{2,8},{3,9},{8,2},{9,3},{10,10},{11,11},{16,16},{17,17... | collective-permute-start | bytes 2064392 | tf_op jit(solution)/shard_map/ppermute | solution.py:260
  32.3 113.4 %collective-permute-start.22 = (bf16[192,1152]{1,0:T(8,128)(2,1)}, bf16[192,1152]{1,0:T(8,128)(2,1)}, u32[]{:S(2)}, u32[]{:S(2)}) collective-permute-start(bf16[192,1152]{1,0:T(8,128)(2,1)} %copy.112), channel_id=1, source_target_pairs={{0,4},{4,0},{1,5},{5,1},{2,6},{6,2},{3,7},{7,3},{8,12},{12,8},{9,1... | collective-permute-start | bytes 1327112 | tf_op jit(solution)/shard_map/ppermute | solution.py:247
  119.4 65.8 %collective-permute-start.55 = (bf16[192,1536]{1,0:T(8,128)(2,1)}, bf16[192,1536]{1,0:T(8,128)(2,1)}, u32[]{:S(2)}, u32[]{:S(2)}) collective-permute-start(bf16[192,1536]{1,0:T(8,128)(2,1)} %dynamic-slice_bitcast_fusion.3), channel_id=1, source_target_pairs={{0,4},{4,0},{1,5},{5,1},{2,6},{6,2},{3,7},{7,3},{8,12},{12,8},{9,1... | collective-permute-start | bytes 1769480 | tf_op jit(solution)/shard_map/ppermute | solution.py:247
  187.1 55.1 %collective-permute-start.59 = (bf16[1,384,768]{2,1,0:T(8,128)(2,1)}, bf16[1,384,768]{2,1,0:T(8,128)(2,1)}, u32[]{:S(2)}, u32[]{:S(2)}) collective-permute-start(bf16[1,384,768]{2,1,0:T(8,128)(2,1)} %bitcast.75), channel_id=1, source_target_pairs={{0,16},{8,24},{16,0},{24,8},{1,17},{9,25},{17,1},{25,9},{2,18},{10... | collective-permute-start | bytes 1769480 | tf_op jit(solution)/shard_map/ppermute | solution.py:250
  190.9 36.0 %collective-permute-start.28 = (bf16[192,768]{1,0:T(8,128)(2,1)S(1)}, bf16[192,768]{1,0:T(8,128)(2,1)}, u32[]{:S(2)}, u32[]{:S(2)}) collective-permute-start(bf16[192,768]{1,0:T(8,128)(2,1)S(1)} %constant_dynamic-slice_fusion.3), channel_id=1, source_target_pairs={{0,4},{4,0},{1,5},{5,1},{2,6},{6,2},{3,7},{7,3},{8,12},{12,8},{9,1... | collective-permute-start | bytes 884744 | tf_op jit(solution)/shard_map/ppermute | solution.py:247
  200.3 55.2 %collective-permute-start.35 = (bf16[384,1536]{1,0:T(8,128)(2,1)}, bf16[384,1536]{1,0:T(8,128)(2,1)}, u32[]{:S(2)}, u32[]{:S(2)}) collective-permute-start(bf16[384,1536]{1,0:T(8,128)(2,1)} %dynamic-slice_bitcast_fusion.1), channel_id=1, source_target_pairs={{0,0},{1,1},{2,8},{3,9},{8,2},{9,3},{10,10},{11,11},{16,16},{17,17... | collective-permute-start | bytes 3538952 | tf_op jit(solution)/shard_map/ppermute | solution.py:260
  211.5 45.5 %collective-permute-start.39 = (bf16[768,768]{1,0:T(8,128)(2,1)}, bf16[768,768]{1,0:T(8,128)(2,1)}, u32[]{:S(2)}, u32[]{:S(2)}) collective-permute-start(bf16[768,768]{1,0:T(8,128)(2,1)} %dynamic-slice_bitcast_fusion), channel_id=1, source_target_pairs={{0,0},{1,1},{2,8},{3,9},{8,2},{9,3},{10,10},{11,11},{16,16},{17,17... | collective-permute-start | bytes 3538952 | tf_op jit(solution)/shard_map/ppermute | solution.py:260
  224.0 109.3 %collective-permute-start.19 = (bf16[16,4608]{1,0:T(8,128)(2,1)}, bf16[16,4608]{1,0:T(8,128)(2,1)}, u32[]{:S(2)}, u32[]{:S(2)}) collective-permute-start(bf16[16,4608]{1,0:T(8,128)(2,1)} %get-tuple-element.144), channel_id=1, source_target_pairs={{0,0},{1,1},{2,8},{3,9},{8,2},{9,3},{10,10},{11,11},{16,16},{17,17... | collective-permute-start | bytes 442376 | tf_op jit(solution)/shard_map/ppermute | solution.py:260
  246.7 48.9 %collective-permute-start.21 = (bf16[64,1536]{1,0:T(8,128)(2,1)}, bf16[64,1536]{1,0:T(8,128)(2,1)S(1)}, u32[]{:S(2)}, u32[]{:S(2)}) collective-permute-start(bf16[64,1536]{1,0:T(8,128)(2,1)} %pad_maximum_fusion.28), channel_id=1, source_target_pairs={{0,2},{1,3},{2,0},{3,1},{4,6},{5,7},{6,4},{7,5},{8,10},{9,11},{10,... | collective-permute-start | bytes 589832 | tf_op jit(solution)/shard_map/ppermute | solution.py:244
  252.4 41.2 %collective-permute-start.73 = (bf16[64,1536]{1,0:T(8,128)(2,1)}, bf16[64,1536]{1,0:T(8,128)(2,1)S(1)}, u32[]{:S(2)}, u32[]{:S(2)}) collective-permute-start(bf16[64,1536]{1,0:T(8,128)(2,1)} %pad_maximum_fusion.30), channel_id=1, source_target_pairs={{0,2},{1,3},{2,0},{3,1},{4,6},{5,7},{6,4},{7,5},{8,10},{9,11},{10,... | collective-permute-start | bytes 589832 | tf_op jit(solution)/shard_map/ppermute | solution.py:244
  255.5 64.7 %collective-permute-start.8 = (bf16[224,1536]{1,0:T(8,128)(2,1)}, bf16[224,1536]{1,0:T(8,128)(2,1)}, u32[]{:S(2)}, u32[]{:S(2)}) collective-permute-start(bf16[224,1536]{1,0:T(8,128)(2,1)} %fusion.42), channel_id=1, source_target_pairs={{0,1},{1,0},{2,3},{3,2},{4,5},{5,4},{6,7},{7,6},{8,9},{9,8},{10,11... | collective-permute-start | bytes 2064392 | tf_op jit(solution)/shard_map/ppermute | solution.py:244
  257.1 36.4 %collective-permute-start.16 = (bf16[4,2,16,1536]{3,2,1,0:T(8,128)(2,1)S(1)}, bf16[4,2,16,1536]{3,2,1,0:T(8,128)(2,1)S(1)}, u32[]{:S(2)}, u32[]{:S(2)}) collective-permute-start(bf16[4,2,16,1536]{3,2,1,0:T(8,128)(2,1)S(1)} %copy-done.43), channel_id=1, source_target_pairs={{0,2},{1,3},{2,0},{3,1},{4,6},{5,7},{6,4},{7,5},{8,10},{9,11},{10,... | collective-permute-start | bytes 1179656 | tf_op jit(solution)/shard_map/ppermute | solution.py:244
  293.5 33.9 %collective-permute-start.9 = (bf16[224,1536]{1,0:T(8,128)(2,1)}, bf16[224,1536]{1,0:T(8,128)(2,1)}, u32[]{:S(2)}, u32[]{:S(2)}) collective-permute-start(bf16[224,1536]{1,0:T(8,128)(2,1)} %fusion.42), channel_id=1, source_target_pairs={{0,8},{8,0},{16,24},{24,16},{1,9},{9,1},{17,25},{25,17},{2,10},{10... | collective-permute-start | bytes 2064392 | tf_op jit(solution)/shard_map/ppermute | solution.py:250
  327.4 61.7 %collective-permute-start.57 = (bf16[2,192,1536]{2,1,0:T(8,128)(2,1)}, bf16[2,192,1536]{2,1,0:T(8,128)(2,1)}, u32[]{:S(2)}, u32[]{:S(2)}) collective-permute-start(bf16[2,192,1536]{2,1,0:T(8,128)(2,1)} %pad_maximum_fusion.6), channel_id=1, source_target_pairs={{0,8},{8,0},{16,24},{24,16},{1,9},{9,1},{17,25},{25,17},{2,10},{10... | collective-permute-start | bytes 3538952 | tf_op jit(solution)/shard_map/ppermute | solution.py:250
  333.4 54.2 %collective-permute-start.60 = (bf16[2,384,768]{2,1,0:T(8,128)(2,1)}, bf16[2,384,768]{2,1,0:T(8,128)(2,1)}, u32[]{:S(2)}, u32[]{:S(2)}) collective-permute-start(bf16[2,384,768]{2,1,0:T(8,128)(2,1)} %pad_maximum_fusion.7), channel_id=1, source_target_pairs={{0,8},{8,0},{16,24},{24,16},{1,9},{9,1},{17,25},{25,17},{2,10},{10... | collective-permute-start | bytes 3538952 | tf_op jit(solution)/shard_map/ppermute | solution.py:250
  335.2 47.4 %collective-permute-start.40 = (bf16[1,768,768]{2,1,0:T(8,128)(2,1)}, bf16[1,768,768]{2,1,0:T(8,128)(2,1)S(1)}, u32[]{:S(2)}, u32[]{:S(2)}) collective-permute-start(bf16[1,768,768]{2,1,0:T(8,128)(2,1)} %bitcast.51), channel_id=1, source_target_pairs={{0,16},{8,24},{16,0},{24,8},{1,17},{9,25},{17,1},{25,9},{2,18},{10... | collective-permute-start | bytes 3538952 | tf_op jit(solution)/shard_map/ppermute | solution.py:250
  335.3 57.7 %collective-permute-start.13 = (bf16[768,1152]{0,1:T(8,128)(2,1)}, bf16[768,1152]{0,1:T(8,128)(2,1)S(1)}, u32[]{:S(2)}, u32[]{:S(2)}) collective-permute-start(bf16[768,1152]{0,1:T(8,128)(2,1)} %get-tuple-element.172), channel_id=1, source_target_pairs={{0,4},{4,0},{1,5},{5,1},{2,6},{6,2},{3,7},{7,3},{8,12},{12,8},{9,1... | collective-permute-start | bytes 5308424 | tf_op jit(solution)/shard_map/ppermute | solution.py:247
  357.9 43.0 %collective-permute-start.25 = (bf16[128,1152]{1,0:T(8,128)(2,1)S(1)}, bf16[128,1152]{1,0:T(8,128)(2,1)}, u32[]{:S(2)}, u32[]{:S(2)}) collective-permute-start(bf16[128,1152]{1,0:T(8,128)(2,1)S(1)} %fusion.20), channel_id=1, source_target_pairs={{0,0},{1,1},{2,8},{3,9},{8,2},{9,3},{10,10},{11,11},{16,16},{17,17... | collective-permute-start | bytes 884744 | tf_op jit(solution)/shard_map/ppermute | solution.py:260
  382.6 33.8 %collective-permute-start.37 = (bf16[384,1536]{1,0:T(8,128)(2,1)}, bf16[384,1536]{1,0:T(8,128)(2,1)}, u32[]{:S(2)}, u32[]{:S(2)}) collective-permute-start(bf16[384,1536]{1,0:T(8,128)(2,1)} %constant_dynamic-slice_fusion.2), channel_id=1, source_target_pairs={{0,4},{4,0},{1,5},{5,1},{2,6},{6,2},{3,7},{7,3},{8,12},{12,8},{9,1... | collective-permute-start | bytes 3538952 | tf_op jit(solution)/shard_map/ppermute | solution.py:247
  387.6 54.9 %collective-permute-start.41 = (bf16[768,768]{1,0:T(8,128)(2,1)}, bf16[768,768]{1,0:T(8,128)(2,1)}, u32[]{:S(2)}, u32[]{:S(2)}) collective-permute-start(bf16[768,768]{1,0:T(8,128)(2,1)} %constant_dynamic-slice_fusion.1), channel_id=1, source_target_pairs={{0,4},{4,0},{1,5},{5,1},{2,6},{6,2},{3,7},{7,3},{8,12},{12,8},{9,1... | collective-permute-start | bytes 3538952 | tf_op jit(solution)/shard_map/ppermute | solution.py:247
  416.4 115.7 %collective-permute-start.38 = (bf16[1,384,1536]{2,1,0:T(8,128)(2,1)}, bf16[1,384,1536]{2,1,0:T(8,128)(2,1)}, u32[]{:S(2)}, u32[]{:S(2)}) collective-permute-start(bf16[1,384,1536]{2,1,0:T(8,128)(2,1)} %bitcast.46), channel_id=1, source_target_pairs={{0,16},{8,24},{16,0},{24,8},{1,17},{9,25},{17,1},{25,9},{2,18},{10... | collective-permute-start | bytes 3538952 | tf_op jit(solution)/shard_map/ppermute | solution.py:250
  442.4 60.7 %collective-permute-start.30 = (bf16[448,1536]{1,0:T(8,128)(2,1)S(1)}, bf16[448,1536]{1,0:T(8,128)(2,1)S(1)}, u32[]{:S(2)}, u32[]{:S(2)}) collective-permute-start(bf16[448,1536]{1,0:T(8,128)(2,1)S(1)} %slice.795), channel_id=1, source_target_pairs={{0,8},{8,0},{16,24},{24,16},{1,9},{9,1},{17,25},{25,17},{2,10},{10... | collective-permute-start | bytes 4128776 | tf_op jit(solution)/shard_map/ppermute | solution.py:250
  442.5 105.9 %collective-permute-start.42 = (bf16[1,768,768]{2,1,0:T(8,128)(2,1)}, bf16[1,768,768]{2,1,0:T(8,128)(2,1)}, u32[]{:S(2)}, u32[]{:S(2)}) collective-permute-start(bf16[1,768,768]{2,1,0:T(8,128)(2,1)} %bitcast.53), channel_id=1, source_target_pairs={{0,16},{8,24},{16,0},{24,8},{1,17},{9,25},{17,1},{25,9},{2,18},{10... | collective-permute-start | bytes 3538952 | tf_op jit(solution)/shard_map/ppermute | solution.py:250
  609.7 40.0 %collective-permute-start.112 = (bf16[48,384]{1,0:T(8,128)(2,1)S(1)}, bf16[48,384]{1,0:T(8,128)(2,1)S(1)}, u32[]{:S(2)}, u32[]{:S(2)}) collective-permute-start(bf16[48,384]{1,0:T(8,128)(2,1)S(1)} %slice.893), channel_id=1, source_target_pairs={{0,1},{1,0},{2,3},{3,2},{4,5},{5,4},{6,7},{7,6},{8,9},{9,8},{10,11... | collective-permute-start | bytes 110600 | tf_op jit(solution)/shard_map/ppermute | solution.py:244
  647.6 33.3 %collective-permute-start.78 = (bf16[128,384]{1,0:T(8,128)(2,1)}, bf16[128,384]{1,0:T(8,128)(2,1)}, u32[]{:S(2)}, u32[]{:S(2)}) collective-permute-start(bf16[128,384]{1,0:T(8,128)(2,1)} %fusion.60), channel_id=1, source_target_pairs={{0,0},{1,1},{2,8},{3,9},{8,2},{9,3},{10,10},{11,11},{16,16},{17,17... | collective-permute-start | bytes 294920 | tf_op jit(solution)/shard_map/ppermute | solution.py:260
  713.4 106.0 %collective-permute-start.100 = (bf16[16,1152]{1,0:T(8,128)(2,1)}, bf16[16,1152]{1,0:T(8,128)(2,1)}, u32[]{:S(2)}, u32[]{:S(2)}) collective-permute-start(bf16[16,1152]{1,0:T(8,128)(2,1)} %convolution_convert_fusion.11), channel_id=1, source_target_pairs={{0,0},{1,1},{2,8},{3,9},{8,2},{9,3},{10,10},{11,11},{16,16},{17,17... | collective-permute-start | bytes 110600 | tf_op jit(solution)/shard_map/ppermute | solution.py:260
  730.9 51.4 %collective-permute-start.79 = (bf16[448,1536]{1,0:T(8,128)(2,1)}, bf16[448,1536]{1,0:T(8,128)(2,1)}, u32[]{:S(2)}, u32[]{:S(2)}) collective-permute-start(bf16[448,1536]{1,0:T(8,128)(2,1)} %slice.844), channel_id=1, source_target_pairs={{0,8},{8,0},{16,24},{24,16},{1,9},{9,1},{17,25},{25,17},{2,10},{10... | collective-permute-start | bytes 4128776 | tf_op jit(solution)/shard_map/ppermute | solution.py:250
  786.3 42.6 %collective-permute-start.115 = (bf16[2,2,16,9216]{3,2,1,0:T(8,128)(2,1)}, bf16[2,2,16,9216]{3,2,1,0:T(8,128)(2,1)}, u32[]{:S(2)}, u32[]{:S(2)}) collective-permute-start(bf16[2,2,16,9216]{3,2,1,0:T(8,128)(2,1)} %pad_maximum_fusion.8), channel_id=1, source_target_pairs={{0,16},{8,24},{16,0},{24,8},{1,17},{9,25},{17,1},{25,9},{2,18},{10... | collective-permute-start | bytes 3538952 | tf_op jit(solution)/shard_map/ppermute | solution.py:250
  816.4 56.8 %collective-permute-start.81 = (bf16[224,1536]{1,0:T(8,128)(2,1)}, bf16[224,1536]{1,0:T(8,128)(2,1)S(1)}, u32[]{:S(2)}, u32[]{:S(2)}) collective-permute-start(bf16[224,1536]{1,0:T(8,128)(2,1)} %fusion.46), channel_id=1, source_target_pairs={{0,0},{1,1},{2,8},{3,9},{8,2},{9,3},{10,10},{11,11},{16,16},{17,17... | collective-permute-start | bytes 2064392 | tf_op jit(solution)/shard_map/ppermute | solution.py:260
  (269 other events, 3463.1 us)
where the time goes:
time: 910 us; the launch traced here: 893 us
  waiting for transfers between devices  250 us (27%)
  local copies, waits for them, and re-layouts  200 us (22%)
  starting transfers between devices  175 us (19%)
  matrix products  146 us (16%)
  other arithmetic  78.6 us (9%)
  Pallas kernels  35.9 us (4%)
    ppermute x47, waiting for transfers between devices, xz(): return lax.ppermute(v, 'tp', [(i, i ^ bit) for i in range(T)])  184 us
    dot_general x66, matrix products, dot(): lax.dot_general(left, right, (dims, ((), ())), preferred_element_type=F32)  127 us
    ppermute x47, starting transfers between devices, xz(): return lax.ppermute(v, 'tp', [(i, i ^ bit) for i in range(T)])  66.5 us
    ppermute x17, starting transfers between devices, exchange(): return lax.ppermute(v, ('rep', 'tp'), swap_pairs)  56.5 us
    dynamic_update_slice x16, local copies, waits for them, and re-layouts, fetch_text(): full = lax.dynamic_update_slice(full, pieces[e], start)  50.8 us
    ppermute x39, waiting for transfers between devices, xr(): return lax.ppermute(v, 'rep', [(i, i ^ bit) for i in range(R)])  42.7 us
    ppermute x39, starting transfers between devices, xr(): return lax.ppermute(v, 'rep', [(i, i ^ bit) for i in range(R)])  30.3 us
    dynamic_update_slice x6, local copies, waits for them, and re-layouts, fetch_image(): full = lax.dynamic_update_slice(full, pieces[e], start)  26.2 us
  transfers between devices with their start and end apart: 119, of which 40 were waited for; matrix products, arithmetic and copies ran while one was open for 41% of the time, Pallas kernels for 1%

commit v1 on v0

v1 whole, which is shorter than its diff:
```python
import functools

import jax
import jax.numpy as jnp
from jax import lax
from jax.experimental import pallas as pl
from jax.experimental.pallas import tpu as pltpu
from jax.sharding import PartitionSpec as P

HD = 64
RANK = 16
EPSILON = 1e-06
BF = jnp.bfloat16
F32 = jnp.float32
CORES = 2


def dot(left, right, dims):
    return lax.dot_general(left, right, (dims, ((), ())), preferred_element_type=F32)


def mm(left, right):
    return dot(left, right, ((left.ndim - 1,), (0,)))


def mm_t(left, right):
    return dot(left, right, ((left.ndim - 1,), (right.ndim - 1,)))


def t_mm(left, right):
    return dot(left, right, ((0,), (0,)))


def norm_rows(values):
    centred = values - jnp.mean(values, axis=-1, keepdims=True)
    inverse = lax.rsqrt(jnp.mean(centred * centred, axis=-1, keepdims=True) + EPSILON)
    return centred * inverse, inverse


def norm_back(grad_hat, hat, inverse):
    first = jnp.mean(grad_hat, axis=-1, keepdims=True)
    second = jnp.mean(grad_hat * hat, axis=-1, keepdims=True)
    return inverse * (grad_hat - first - hat * second)


def gelu_tanh(values):
    return jax.nn.gelu(values, approximate=True)


class Slot(int):
    pass


def spot(offs, where, step):
    if isinstance(where, Slot):
        return pl.multiple_of(offs[int(where)], step)
    return where


def copies(offs, plan, sources, targets, sems):
    def make(i):
        source, lead, rows, cols, target, row, col, _ = plan[i]
        ref = sources[source] if lead is None else sources[source].at[lead]
        dst = targets[target].at[pl.ds(spot(offs, row, 16), rows), pl.ds(spot(offs, col, 128), cols)]
        return pltpu.make_async_copy(ref, dst, sems.at[i])

    def each(action, chosen):
        for i in range(len(plan)):
            if chosen is not None and plan[i][4] not in chosen:
                continue
            case = plan[i][7]
            if case is None:
                action(make(i))
            else:

                @pl.when(offs[0] == case)
                def _(i=i):
                    action(make(i))

    return (
        lambda chosen=None: each(lambda c: c.start(), chosen),
        lambda chosen=None: each(lambda c: c.wait(), chosen),
    )


ANY = pl.BlockSpec(memory_space=pl.ANY)
SCALARS = pl.BlockSpec(memory_space=pltpu.SMEM)


def head_tiles(width):
    if width % 128 == 0:
        return [(p * 128, 128, 2) for p in range(width // 128)]
    return [(h * HD, HD, 1) for h in range(width // HD)]


def head_masks(rows, count):
    if count == 1:
        return [None]
    lane = lax.broadcasted_iota(jnp.int32, (rows, 128), 1)
    return [lane < HD, lane >= HD]


def pick(mask, values):
    return values if mask is None else jnp.where(mask, values, jnp.zeros_like(values))


def attend_forward_kernel(width, plan, offs, *refs):
    *sources, out_ref, lse_ref, kv_ref, sems = refs
    start_all, wait_all = copies(offs, plan, sources, [kv_ref], sems)
    step = pl.program_id(0)

    @pl.when(step == 0)
    def _():
        start_all()
        wait_all()

    rows = out_ref.shape[0]
    here = pl.ds(pl.multiple_of(step * rows, rows), rows)
    lses = []
    for start, size, count in head_tiles(width):
        queries = kv_ref[here, start : start + size] * jnp.asarray(HD ** (-0.5), BF)
        keys = kv_ref[:, width + start : width + start + size]
        values = kv_ref[:, 2 * width + start : 2 * width + start + size]
        total = None
        for mask in head_masks(rows, count):
            scores = mm_t(pick(mask, queries), keys)
            top = jnp.max(scores, axis=-1, keepdims=True)
            weights = jnp.exp(scores - top)
            norm = jnp.sum(weights, axis=-1, keepdims=True)
            part = mm(weights.astype(BF), values) * (1.0 / norm)
            part = pick(mask, part)
            total = part if total is None else total + part
            lses.append(top + jnp.log(norm))
        out_ref[:, start : start + size] = total.astype(BF)
    lse_ref[...] = jnp.concatenate(lses, axis=1)


def attend_backward_kernel(width, blocks, plan, offs, lse_ref, *refs):
    *sources, out_ref, kv_ref, grad_ref, dk_ref, dv_ref, sems = refs
    start_all, wait_all = copies(offs, plan, sources, [kv_ref, grad_ref], sems)
    step = pl.program_id(0)

    @pl.when(step == 0)
    def _():
        start_all()
        dk_ref[...] = jnp.zeros_like(dk_ref)
        dv_ref[...] = jnp.zeros_like(dv_ref)
        wait_all()

    rows = lse_ref.shape[0]
    here = pl.ds(pl.multiple_of(step * rows, rows), rows)
    head = 0
    for start, size, count in head_tiles(width):
        queries = kv_ref[here, start : start + size] * jnp.asarray(HD ** (-0.5), BF)
        keys = kv_ref[:, width + start : width + start + size]
        values = kv_ref[:, 2 * width + start : 2 * width + start + size]
        grads = grad_ref[here, start : start + size]
        grad_q = None
        for mask in head_masks(rows, count):
            queries_m = pick(mask, queries)
            grads_m = pick(mask, grads)
            scores = mm_t(queries_m, keys)
            probs = jnp.exp(scores - lse_ref[:, head : head + 1])
            grad_probs = mm_t(grads_m, values)
            product = probs * grad_probs
            inner = jnp.sum(product, axis=-1, keepdims=True)
            grad_scores = (product - probs * inner).astype(BF)
            part = pick(mask, mm(grad_scores, keys))
            grad_q = part if grad_q is None else grad_q + part
            dk_ref[:, start : start + size] += t_mm(grad_scores, queries_m)
            dv_ref[:, start : start + size] += t_mm(probs.astype(BF), grads_m)
            head += 1
        out_ref[here, start : start + size] = (grad_q * HD ** (-0.5)).astype(BF)

    @pl.when(step == blocks - 1)
    def _():
        out_ref[:, width : 2 * width] = dk_ref[...].astype(BF)
        out_ref[:, 2 * width :] = dv_ref[...].astype(BF)


def query_block(length):
    for rows in (256, 128, 64, 32, 16):
        if length % rows == 0:
            return rows
    return length


def stack_plan(arrays, target, first):
    plan, row = [], 0
    for i, (array, case) in enumerate(arrays):
        plan.append((first + i, None, array.shape[0], array.shape[1], target, row, 0, case))
        if case != 1:
            row += array.shape[0]
    return plan, row


def attend_forward(offs, joints):
    plan, length = stack_plan(joints, 0, 0)
    width3 = joints[0][0].shape[1]
    width = width3 // 3
    heads = width // HD
    rows = query_block(length)
    return pl.pallas_call(
        functools.partial(attend_forward_kernel, width, plan),
        grid=(length // rows,),
        in_specs=[SCALARS] + [ANY] * len(joints),
        out_specs=[
            pl.BlockSpec((rows, width), lambda i: (i, 0)),
            pl.BlockSpec((rows, heads), lambda i: (i, 0)),
        ],
        out_shape=[
            jax.ShapeDtypeStruct((length, width), BF),
            jax.ShapeDtypeStruct((length, heads), F32),
        ],
        scratch_shapes=[pltpu.VMEM((length, width3), BF), pltpu.SemaphoreType.DMA((len(plan),))],
        compiler_params=pltpu.CompilerParams(vmem_limit_bytes=40 * 1024 * 1024),
        cost_estimate=pl.CostEstimate(
            flops=16 * length * length * width,
            transcendentals=length * length * heads,
            bytes_accessed=length * width3 * 4,
        ),
        name="attend_forward",
    )(offs, *[a for a, _ in joints])


def attend_backward(offs, joints, grads, lse):
    plan, length = stack_plan(joints, 0, 0)
    more, _ = stack_plan(grads, 1, len(joints))
    plan = plan + more
    width3 = joints[0][0].shape[1]
    width = width3 // 3
    heads = width // HD
    rows = query_block(length)
    blocks = length // rows
    return pl.pallas_call(
        functools.partial(attend_backward_kernel, width, blocks, plan),
        grid=(blocks,),
        in_specs=[SCALARS, pl.BlockSpec((rows, heads), lambda i: (i, 0))] + [ANY] * len(plan),
        out_specs=pl.BlockSpec((length, width3), lambda i: (0, 0)),
        out_shape=jax.ShapeDtypeStruct((length, width3), BF),
        scratch_shapes=[
            pltpu.VMEM((length, width3), BF),
            pltpu.VMEM((length, width), BF),
            pltpu.VMEM((length, width), F32),
            pltpu.VMEM((length, width), F32),
            pltpu.SemaphoreType.DMA((len(plan),)),
        ],
        compiler_params=pltpu.CompilerParams(vmem_limit_bytes=48 * 1024 * 1024),
        cost_estimate=pl.CostEstimate(
            flops=32 * length * length * width,
            transcendentals=length * length * heads,
            bytes_accessed=length * width3 * 8,
        ),
        name="attend_backward",
    )(offs, lse, *[a for a, _ in joints], *[a for a, _ in grads])


class Matrix:
    def __init__(self, shape, sources, plan):
        self.shape, self.sources, self.plan = shape, sources, plan


def join(refs):
    if len(refs) == 1:
        return refs[0][...]
    return jnp.concatenate([r[...] for r in refs], axis=0)


def split(value, refs):
    row = 0
    for ref in refs:
        ref[...] = value[row : row + ref.shape[0]].astype(ref.dtype)
        row += ref.shape[0]


def qkv_forward_kernel(ws, ins, outs, need):
    (x_refs, (a,), (b,)), ((out,), (rank_out,)) = ins, outs
    x = join(x_refs)
    rank = mm_t(x, a[...]).astype(BF)
    rank_out[...] = rank
    low = mm(rank, b[...])
    need(0)
    out[...] = (mm(x, ws[0][...]) + low).astype(BF)


def qkv_backward_kernel(ws, ins, outs, need):
    ((g,), x_refs, ranks, (a,), (b,)), (out, (t_b,), (t_a,)) = ins, outs
    grad = g[...]
    low = mm_t(grad, b[...]).astype(BF)
    t_b[...] = t_mm(join(ranks), grad)
    t_a[...] = t_mm(low, join(x_refs))
    need(0)
    split(mm_t(grad, ws[0][...]) + mm(low, a[...]), out)


def out_forward_kernel(ws, ins, outs, need):
    ((att,), (a,), (b,)), (out, (rank_out,)) = ins, outs
    act = att[...]
    rank = mm_t(act, a[...]).astype(BF)
    rank_out[...] = rank
    need(0)
    split(mm(act, ws[0][...]) + mm(rank, b[...]), out)


def out_backward_kernel(ws, ins, outs, need):
    (g_refs, (att,), (rank,), (a,), (b,)), ((out,), (t_b,), (t_a,)) = ins, outs
    grad = join(g_refs)
    low = mm_t(grad, b[...]).astype(BF)
    t_b[...] = t_mm(rank[...], grad)
    t_a[...] = t_mm(low, att[...])
    need(0)
    out[...] = (mm_t(grad, ws[0][...]) + mm(low, a[...])).astype(BF)


def mlp_forward_kernel(ws, ins, outs, need):
    x_refs, (a1,), (b1,), (a2,), (b2,) = ins
    out, (act_out,), (slope_out,), (rank1_out,), (rank2_out,) = outs
    x = join(x_refs)
    rank1 = mm_t(x, a1[...]).astype(BF)
    rank1_out[...] = rank1
    low1 = mm(rank1, b1[...])
    need(0)
    hidden = mm(x, ws[0][...]) + low1
    square = hidden * hidden
    bend = jnp.tanh(0.7978845608028654 * hidden * (1.0 + 0.044715 * square))
    half = 0.5 * (1.0 + bend)
    act = (hidden * half).astype(BF)
    act_out[...] = act
    slope = half + 0.5 * hidden * (1.0 - bend * bend) * (
        0.7978845608028654 * (1.0 + 0.134145 * square)
    )
    slope_out[...] = slope.astype(BF)
    rank2 = mm_t(act, a2[...]).astype(BF)
    rank2_out[...] = rank2
    need(1)
    split(mm(act, ws[1][...]) + mm(rank2, b2[...]), out)


def mlp_backward_kernel(ws, ins, outs, need):
    g_refs, x_refs, (act,), (slope,), (rank1,), (rank2,), (a1,), (b1,), (a2,), (b2,) = ins
    out, (t_b1,), (t_a2,), (t_b2,), (t_a1,) = outs
    grad = join(g_refs)
    low2 = mm_t(grad, b2[...]).astype(BF)
    t_b2[...] = t_mm(rank2[...], grad)
    t_a2[...] = t_mm(low2, act[...])
    need(1)
    grad_act = mm_t(grad, ws[1][...]) + mm(low2, a2[...])
    gh = (grad_act * slope[...].astype(F32)).astype(BF)
    low1 = mm_t(gh, b1[...]).astype(BF)
    t_b1[...] = t_mm(rank1[...], gh)
    t_a1[...] = t_mm(low1, join(x_refs))
    need(0)
    split(mm_t(gh, ws[0][...]) + mm(low1, a1[...]), out)


def project(kernel, offs, matrices, ins, outs, first):
    arrays, specs, counts = [], [], []
    for group in ins:
        counts.append(len(group))
        for item in group:
            if isinstance(item, tuple):
                array, row, rows = item
                arrays.append(array)
                specs.append(pl.BlockSpec((rows, array.shape[1]), lambda i, at=row // rows: (at, 0)))
            else:
                arrays.append(item)
                specs.append(pl.BlockSpec(item.shape, lambda i: (0, 0)))
    sources, plan = [], []
    order = [first] + [m for m in range(len(matrices)) if m != first]
    for m in order:
        base = len(sources)
        sources += matrices[m].sources
        plan += [(base + p[0],) + p[1:4] + (m,) + p[4:] for p in matrices[m].plan]
    shapes = [jax.ShapeDtypeStruct(*o) for group in outs for o in group]
    n_in, n_src, n_out, n_mat = len(arrays), len(sources), len(shapes), len(matrices)

    def groups(refs, sizes):
        result, i = [], 0
        for n in sizes:
            result.append(list(refs[i : i + n]))
            i += n
        return result

    def body(offs_ref, *refs):
        in_refs, refs = refs[:n_in], refs[n_in:]
        src_refs, refs = refs[:n_src], refs[n_src:]
        out_refs, refs = refs[:n_out], refs[n_out:]
        w_refs, sems = refs[:n_mat], refs[n_mat]
        start, wait = copies(offs_ref, plan, src_refs, w_refs, sems)
        start()
        kernel(w_refs, groups(in_refs, counts), groups(out_refs, [len(g) for g in outs]), lambda m: wait([m]))

    flops = sum(4 * outs[0][0][0][0] * len(outs[0]) * m.shape[0] * m.shape[1] for m in matrices)
    moved = sum(2 * m.shape[0] * m.shape[1] for m in matrices) + sum(2 * s.size for s in shapes)
    results = pl.pallas_call(
        body,
        grid=(1,),
        in_specs=[SCALARS] + specs + [ANY] * n_src,
        out_specs=[pl.BlockSpec(s.shape, lambda i: (0, 0)) for s in shapes],
        out_shape=shapes,
        scratch_shapes=[pltpu.VMEM(m.shape, BF) for m in matrices] + [pltpu.SemaphoreType.DMA((len(plan),))],
        compiler_params=pltpu.CompilerParams(vmem_limit_bytes=56 * 1024 * 1024),
        cost_estimate=pl.CostEstimate(flops=flops, transcendentals=0, bytes_accessed=moved),
    )(offs, *arrays, *sources)
    return groups(results, [len(g) for g in outs])


class Stream:
    pass


def powers(size):
    bits, bit = [], 1
    while bit < size:
        bits.append(bit)
        bit *= 2
    return bits


def body(
    mesh_shape,
    image_input,
    text_input,
    cond,
    image_cotangent,
    text_cotangent,
    live,
    slot_adapter_index,
    modulation_weight,
    query_key_value_weight,
    output_weight,
    first_feed_weight,
    second_feed_weight,
    adapter_down_table,
    adapter_up_table,
    modulation_up_factor,
    query_key_value_up,
    first_feed_up,
    output_down_factor,
    second_feed_down,
):
    R, F, T = mesh_shape
    H = T // CORES
    X = R // CORES
    W = image_input.shape[-1]
    wq = W // T
    Rf = modulation_up_factor.shape[1]
    Rq = adapter_down_table.shape[2]
    ffq = first_feed_weight.shape[-1]
    r = lax.axis_index("rep")
    f = lax.axis_index("fsdp")
    z = lax.axis_index("tp")
    core = lax.rem(r, CORES)
    xi = lax.div(r, CORES)
    high = lax.div(z, H)
    native = core == high

    def xz(v, bit):
        return lax.ppermute(v, "tp", [(i, i ^ bit) for i in range(T)])

    def xf(v, bit):
        return lax.ppermute(v, "fsdp", [(i, i ^ bit) for i in range(F)])

    def xr(v, bit):
        return lax.ppermute(v, "rep", [(i, i ^ bit) for i in range(R)])

    swap_pairs, across_pairs = [], []
    for a in range(R):
        for b in range(T):
            if a % CORES != b // H:
                swap_pairs.append((a * T + b, (a ^ 1) * T + (b ^ H)))
                across_pairs.append((a * T + b, (a ^ 2) * T + b))

    def swap(v):
        return lax.ppermute(v, ("rep", "tp"), swap_pairs)

    def swap_across(v):
        return lax.ppermute(v, ("rep", "tp"), across_pairs)

    def exchange(v):
        return jnp.where(native, v, swap(v))

    lanes = {}

    def queue(lane, step, value, *more):
        if lane in lanes:
            _, value = lax.optimization_barrier((lanes[lane], value))
        lanes[lane] = step(value, *more)
        return lanes[lane]

    LX, LY, LZ = range(3)

    def due(value, *arrived):
        return lax.optimization_barrier((value, arrived))[0]

    def gather_by(v, step, bits):
        return gather_by_more(v[None], step, bits)

    def gather_by_more(blocks, step, bits):
        for bit in bits:
            blocks = jnp.concatenate([blocks, step(blocks, bit)], axis=0)
        return blocks

    x_bits = [b for b in powers(R) if b > 1]
    h_bits = powers(H)
    t_bits = powers(T)
    f_bits = powers(F)
    arange_t = jnp.arange(T, dtype=jnp.int32)

    def gather_group(v):
        blocks = [v]
        for bit in h_bits:
            blocks = blocks + [xz(b, bit) for b in blocks]
        return blocks + [xr(b, 1) for b in blocks]

    def fold_cores(blocks):
        return [blocks[i].astype(F32) + xr(blocks[H + i], 1).astype(F32) for i in range(H)]

    def fold_chips(keep):
        sent = None
        for bit in reversed(h_bits):
            out = [k.astype(BF) for k in keep[bit:]]
            sent = out if sent is None else sent
            keep = [keep[i] + xz(out[i], bit).astype(F32) for i in range(bit)]
        return keep[0], sent

    def gather_texts(pair):
        rows = pair[0].shape[0]
        blocks = gather_by(jnp.concatenate(pair, axis=0), xz, t_bits)
        blocks = jnp.take(blocks, jnp.bitwise_xor(z, arange_t), axis=0)
        return [blocks[:, i * rows : (i + 1) * rows].reshape(T * rows, W) for i in range(2)]

    def bit_of(index, bit):
        return lax.rem(lax.div(index, bit), 2)

    def sum_text(v):
        for bit in t_bits:
            v = v + xz(v, bit)
        return v

    def own_rows_of(v):
        rows = v.shape[0] // T
        return lax.dynamic_slice_in_dim(v, z * rows, rows, axis=0)

    def scatter_rows(v):
        for bit in reversed(t_bits):
            half = v.shape[0] // 2
            mine = bit_of(z, bit) == 0
            low, high_part = v[:half], v[half:]
            out = jnp.where(mine, high_part, low).astype(BF)
            v = jnp.where(mine, low, high_part).astype(F32) + xz(out, bit).astype(F32)
        return v

    def scatter_columns(rows, steps):
        for step, bit, mine in steps:
            half = rows.shape[1] // 2
            low, high_part = rows[:, :half], rows[:, half:]
            rows = jnp.where(mine == 0, low, high_part) + step(jnp.where(mine == 0, high_part, low), bit)
        return rows

    img_steps = [(xr, 1, core)] + [(xz, bit, bit_of(z, bit)) for bit in reversed(h_bits)]
    txt_steps = [(xz, bit, bit_of(z, bit)) for bit in reversed(t_bits)]

    silu = jax.nn.silu(cond).astype(BF)
    info = jnp.concatenate(
        [
            silu.astype(F32),
            jnp.broadcast_to(slot_adapter_index.astype(F32)[:, None], (1, 64)),
            jnp.broadcast_to(live.astype(F32)[:, None], (1, 64)),
        ],
        axis=1,
    )
    info_f = gather_by(info[0], xf, f_bits)
    silu_f = info_f[:, :W].astype(BF)
    ids_f = info_f[:, W].astype(jnp.int32)

    row_ids = f * Rf + jnp.arange(Rf, dtype=jnp.int32)
    row_adapter = lax.div(row_ids, RANK)
    rows_d = modulation_weight.shape[1]

    def condition_ranks(silu_rows):
        held = jnp.einsum("fd,kid->fki", silu_rows, adapter_down_table[0], preferred_element_type=F32)
        spread = jnp.take(gather_by(held, xz, t_bits), jnp.bitwise_xor(z, arange_t), axis=0)
        return jnp.moveaxis(spread, 0, 2).reshape(silu_rows.shape[0], 2, Rf)

    def partial_modulation(ranks):
        own_rows = (row_adapter[None] == ids_f[:, None])[:, None, :]
        rank_rows = jnp.where(own_rows, ranks, 0.0).astype(BF)
        silu_rows = lax.dynamic_slice_in_dim(silu_f, f * rows_d, rows_d, axis=1)
        parts = []
        for k in range(2):
            parts.append(
                jnp.einsum("fd,dcj->fcj", silu_rows, modulation_weight[k], preferred_element_type=F32)
                + jnp.einsum(
                    "fr,rcj->fcj", rank_rows[:, k], modulation_up_factor[k], preferred_element_type=F32
                )
            )
        return jnp.stack(parts, axis=1)

    def modulation_shard(partial_mod):
        total_mod = partial_mod[0]
        for d in range(1, F):
            total_mod = total_mod + xf(partial_mod[d], d)
        return total_mod

    def modulation(mod_shard):
        mod_rel = gather_by(mod_shard, xz, t_bits)
        mod_abs = jnp.take(mod_rel, jnp.bitwise_xor(z, arange_t), axis=0)
        return jnp.moveaxis(mod_abs, 0, 2).reshape(2, 6, W)

    def both_modulations(mod_all):
        mine = jnp.concatenate([mod_all[0], jnp.broadcast_to(text.live, (1, W))], axis=0)
        both = jnp.where(native, mine, xr(mine, 1))
        image.live = both[6:7]
        return both[:6], mod_all[1]

    base_row = f * Rf + z * Rq

    def own_table_rows(ident, kinds):
        table = jnp.concatenate(kinds, axis=2)
        wanted = ident * RANK + jnp.arange(RANK, dtype=jnp.int32)
        held = base_row + jnp.arange(Rq, dtype=jnp.int32)
        if Rq == RANK:
            return jnp.where(ident * RANK == base_row, table, jnp.zeros_like(table))
        match = (wanted[:, None] == held[None, :]).astype(BF)
        return jnp.einsum("ir,srw->siw", match, table, preferred_element_type=F32).astype(BF)

    def own_columns(ident, kinds):
        start = ident * RANK - f * Rf
        inside = (start >= 0) & (start <= Rf - RANK)
        first = jnp.clip(start, 0, Rf - RANK)
        taken = jnp.concatenate(
            [lax.dynamic_slice_in_dim(k, first, RANK, axis=1) for k in kinds], axis=2
        )
        return jnp.where(inside, taken, jnp.zeros_like(taken))

    def fetch_adapters(tables, columns, after):
        tables, columns = due((tables, columns), after)
        both = [
            jnp.concatenate([own_table_rows(ids_f[d], tables), own_columns(ids_f[d], columns)], axis=2)
            for d in range(F)
        ]
        rows = both[0]
        for d in range(1, F):
            rows = rows + queue(LY, xf, both[d], d)
        yield rows
        cut = len(tables) * W
        table_rows, column_rows = rows[:, :, :cut], rows[:, :, cut:]
        for bit in t_bits:
            if bit < H:
                table_rows = table_rows + xz(table_rows, bit)
            else:
                table_rows = table_rows + queue(LZ, xz, table_rows, bit)
        rows_img = jnp.where(native, table_rows[0], xr(table_rows[0], 1))
        cols_img = jnp.where(native, column_rows[0], queue(LZ, swap, column_rows[0]))

        def pieces(array, widths):
            result, at = [], 0
            for n in widths:
                result.append(array[:, at : at + n])
                at += n
            return result

        table_widths = [t.shape[2] for t in tables]
        column_widths = [c.shape[2] for c in columns]
        yield (
            pieces(rows_img, table_widths) + pieces(cols_img, column_widths),
            pieces(table_rows[1], table_widths) + pieces(column_rows[1], column_widths),
        )

    image, text = Stream(), Stream()
    text.live = live.astype(F32)[0]
    qkv_planes = lax.optimization_barrier(jnp.moveaxis(query_key_value_weight, 2, 1))
    sub, ffh, wh = rows_d // 2, ffq // 2, wq // 2
    xb, cb = lax.rem(xi, 2), core
    entries = [native.astype(jnp.int32)]

    def slot(value):
        entries.append(value)
        return Slot(len(entries) - 1)

    def fetch_first(after):
        return fetch_adapters(
            [adapter_down_table[1], adapter_up_table[0], adapter_down_table[2], adapter_up_table[1]],
            [query_key_value_up.reshape(2, Rf, 3 * wq), output_down_factor, first_feed_up, second_feed_down],
            after,
        )

    def norm_first():
        for s, mod, tokens in ((image, mods[0], img), (text, mods[1], text_tokens)):
            s.xf = tokens.astype(F32)
            s.hat1, s.inv1 = norm_rows(s.xf)
            s.normed = (s.hat1 * (1.0 + mod[1:2]) + mod[0:1]).astype(BF)

    if F == 2 and X == 2 and rows_d % 128 == 0 and wh % 16 == 0 and sub % 16 == 0:
        own, other = slot(f * rows_d), slot((1 - f) * rows_d)
        own_x, own_y = slot(f * rows_d + xb * sub), slot(f * rows_d + (1 - xb) * sub)
        other_x, other_y = slot((1 - f) * rows_d + xb * sub), slot((1 - f) * rows_d + (1 - xb) * sub)
        other_c, other_d = slot((1 - f) * rows_d + cb * sub), slot((1 - f) * rows_d + (1 - cb) * sub)
        half_x, half_y = slot(xb * ffh), slot((1 - xb) * ffh)
        half_c, half_d = slot(cb * ffh), slot((1 - cb) * ffh)
        att_c, att_d = slot(cb * wh), slot((1 - cb) * wh)

        def piece(weight, k, which, rows):
            start = (k,) + (0,) * (weight.ndim - 3) + (which * rows, 0)
            return lax.dynamic_slice(weight, start, (1,) + weight.shape[1:-2] + (rows, weight.shape[-1]))[0]

        def planes(weight, plan, k):
            if weight.ndim == 3:
                return plan
            n = weight.shape[-1]
            return [
                (p[0], c if p[1] is None else (k, c)) + p[2:5] + (c * n,) + p[6:]
                for p in plan
                for c in range(weight.shape[1])
            ]

        def width(weight):
            return weight.shape[-1] * (1 if weight.ndim == 3 else weight.shape[1])

        def image_pieces(weight, rows):
            mine = piece(weight, 0, xb, rows)
            a0 = queue(LZ, swap, mine)
            after = yield a0
            if after is not None:
                a0 = due(a0, after)
            a1 = queue(LX, swap_across, a0)
            b0 = queue(LY, xf, jnp.where(native, mine, a0), 1)
            after = yield a1, b0
            if after is not None:
                b0 = due(b0, after)
            yield [weight, a0, a1, b0, queue(LX, xr, b0, 2)]

        def image_in(weight, sources):
            n = weight.shape[-1]
            plan = [
                (0, 0, rows_d, n, own, 0, 1),
                (1, None, sub, n, own_x, 0, 0),
                (2, None, sub, n, own_y, 0, 0),
                (3, None, sub, n, other_x, 0, None),
                (4, None, sub, n, other_y, 0, None),
            ]
            return Matrix((W, width(weight)), sources, planes(weight, plan, 0))

        def image_out(sources):
            plan = [
                (0, 0, ffq, rows_d, 0, own, 1),
                (1, None, ffh, rows_d, half_x, own, 0),
                (2, None, ffh, rows_d, half_y, own, 0),
                (3, None, ffh, rows_d, half_x, other, None),
                (4, None, ffh, rows_d, half_y, other, None),
            ]
            return Matrix((ffq, W), sources, plan)

        def text_piece(weight, rows):
            b0 = queue(LY, xf, piece(weight, 1, cb, rows), 1)
            return [weight, b0, xr(b0, 1)]

        def text_in(weight):
            n = weight.shape[-1]
            plan = [
                (0, 1, rows_d, n, own, 0, None),
                (1, None, sub, n, other_c, 0, None),
                (2, None, sub, n, other_d, 0, None),
            ]
            return Matrix((W, width(weight)), text_piece(weight, sub), planes(weight, plan, 1))

        def text_out(weight, rows, slot_c, slot_d):
            plan = [
                (0, 1, 2 * rows, rows_d, 0, own, None),
                (1, None, rows, rows_d, slot_c, other, None),
                (2, None, rows, rows_d, slot_d, other, None),
            ]
            return Matrix((2 * rows, W), text_piece(weight, rows), plan)

        get_qkv = image_pieces(qkv_planes, sub)
        a0_qkv = next(get_qkv)
        text.w_qkv = text_in(due(qkv_planes, info_f))
        ranks = due(condition_ranks(silu_f), a0_qkv)
        img_swap = queue(LZ, swap, due(image_input[0], ranks))
        img = jnp.where(native, image_input[0], img_swap)
        shard = modulation_shard(due(partial_modulation(ranks), text.w_qkv.sources[1]))
        text_tokens, text.cot = gather_texts(due((text_input[0], text_cotangent[0]), shard))
        get_first = fetch_first(shard)
        next(get_first)
        a1_qkv, b0_qkv = get_qkv.send(shard)
        mods = both_modulations(due(modulation(shard), img_swap))
        norm_first()
        first_img, first_txt = next(get_first)
        image.w_qkv = image_in(qkv_planes, next(get_qkv))
        image.n1 = gather_group(image.normed)
        image.n1[1] = due(image.n1[1], a1_qkv, b0_qkv)
        rest = (output_weight, first_feed_weight, second_feed_weight, image_cotangent)
        _, rest = lax.optimization_barrier((image.normed, rest))
        text.w_out = text_out(rest[0], wh, att_c, att_d)
        text.w_fc1 = text_in(rest[1])
        text.w_fc2 = text_out(rest[2], ffh, half_c, half_d)
        rest = due(rest, image.n1[1])
        output_weight, first_feed_weight, second_feed_weight, image_cotangent = rest
        flight = Stream()

        def bulk(stage, value):
            if stage == 0:
                flight.out = output_weight[0]
                flight.a_out = queue(LZ, swap, flight.out)
                flight.get_fc1 = image_pieces(first_feed_weight, sub)
                flight.a0_fc1 = next(flight.get_fc1)
            elif stage == 1:
                flight.a_out, flight.a0_fc1 = due((flight.a_out, flight.a0_fc1), value)
                b_out = queue(LY, xf, jnp.where(native, flight.out, flight.a_out), 1)
                image.w_out = Matrix(
                    (wq, W),
                    [output_weight, flight.a_out, b_out],
                    [
                        (0, 0, wq, rows_d, 0, own, 1),
                        (1, None, wq, rows_d, 0, own, 0),
                        (2, None, wq, rows_d, 0, other, None),
                    ],
                )
                flight.part_fc1 = flight.get_fc1.send(value)
                flight.get_fc2 = image_pieces(due(second_feed_weight, value), ffh)
                flight.a0_fc2 = next(flight.get_fc2)
                return [flight.a_out]
            elif stage == 2:
                image.w_fc1 = image_in(first_feed_weight, flight.get_fc1.send(value))
                return [flight.part_fc1[0]]
            elif stage == 3:
                flight.part_fc2 = flight.get_fc2.send(value)
                return [flight.part_fc1[1], flight.a0_fc2]
            else:
                image.w_fc2 = image_out(flight.get_fc2.send(value))
                image.cot = jnp.where(
                    native, image_cotangent[0], queue(LZ, swap, due(image_cotangent[0], value))
                )
                return list(flight.part_fc2) + [image.w_fc1.sources[4]]
            return []

    else:

        def bulk(stage, value):
            return []

        def place(shape, pieces, axis):
            full = jnp.zeros(shape, BF)
            for piece, offset in pieces:
                full = lax.dynamic_update_slice_in_dim(full, piece, offset, axis=axis)
            return full

        def fetch_image(weight, axis):
            rows, cols = weight.shape
            part = rows // X
            mine = lax.dynamic_slice_in_dim(weight, xi * part, part, axis=0)
            moved = gather_by(exchange(mine), xr, x_bits)
            held = place((rows, cols), [(moved[e], (xi ^ e) * part) for e in range(X)], 0)
            held = jnp.where(native, weight, held)
            full_shape = (rows * F, cols) if axis == 0 else (rows, cols * F)
            size = weight.shape[axis]
            full = place(full_shape, [(held, f * size)], axis)
            for d in range(1, F):
                full = lax.dynamic_update_slice_in_dim(full, xf(held, d), (f ^ d) * size, axis=axis)
            return full

        def fetch_text(weight, axis):
            rows, cols = weight.shape
            part = rows // R
            mine = lax.dynamic_slice_in_dim(weight, r * part, part, axis=0)
            full_shape = (rows * F, cols) if axis == 0 else (rows, cols * F)
            size = weight.shape[axis]
            full = place(full_shape, [(weight, f * size)], axis)
            for d in range(1, F):
                pieces = gather_by(xf(mine, d), xr, x_bits + [1])
                order = [0]
                for bit in x_bits + [1]:
                    order = order + [o ^ bit for o in order]
                for e in range(R):
                    start = [0, 0]
                    start[axis] = (f ^ d) * size
                    start[0] = start[0] + (r ^ order[e]) * part
                    full = lax.dynamic_update_slice(full, pieces[e], start)
            return full

        def whole(full):
            rows, cols = full.shape
            return Matrix(full.shape, [full], [(0, None, rows, cols, 0, 0, None)])

        qkv_native = query_key_value_weight.reshape(2, rows_d, 3 * wq)
        img = exchange(image_input[0])
        image.cot = exchange(image_cotangent[0])
        shard = modulation_shard(partial_modulation(condition_ranks(silu_f)))
        text_tokens, text.cot = gather_texts((text_input[0], text_cotangent[0]))
        mods = both_modulations(modulation(shard))
        _, (first_img, first_txt) = fetch_first(shard)
        norm_first()
        image.n1 = gather_group(image.normed)
        for s, k, fetch in ((image, 0, fetch_image), (text, 1, fetch_text)):
            s.w_qkv = whole(fetch(qkv_native[k], 0))
            s.w_out = whole(fetch(output_weight[k], 1))
            s.w_fc1 = whole(fetch(first_feed_weight[k], 0))
            s.w_fc2 = whole(fetch(second_feed_weight[k], 1))
    offs = jnp.stack(entries).astype(jnp.int32)
    streams = (image, text)
    for s, mod, tokens, first in (
        (image, mods[0], img, first_img),
        (text, mods[1], text_tokens, first_txt),
    ):
        s.mod, s.x = mod, tokens
        s.a_qkv, s.b_out, s.a_fc1, s.b_fc2, s.b_qkv, s.a_out, s.b_fc1, s.a_fc2 = first

    near = [0, H]
    far = [i for i in range(T) if i not in near]
    flow = near + far
    image.size, text.size = image.x.shape[0], text.x.shape[0]
    image.once, image.twice = [flow], [near, far]
    text.once = text.twice = [[0]]
    img_len = T * image.size

    def scatter_image(blocks, parts):
        placed = [None] * T
        for i, v in zip([i for part in parts for i in part], blocks):
            placed[i] = v
        return fold_chips(fold_cores(placed))

    def windows(s, array, parts):
        result, row = [], 0
        for part in parts:
            rows = len(part) * s.size
            result.append((array, row, rows))
            row += rows
        return result

    def own_part(s, v):
        return own_rows_of(v) if s is text else v

    def total(results):
        value = results[0]
        for more in results[1:]:
            value = value + more
        return value

    def blocks_out(s, part):
        return [((s.size, W), BF)] * len(part)

    def qkv_forward(s):
        s.joint, s.rank_qkv = [], []
        for part in s.twice:
            rows = len(part) * s.size
            (out,), (rank,) = project(
                qkv_forward_kernel, offs, [s.w_qkv],
                [[s.n1[i] for i in part], [s.a_qkv], [s.b_qkv]],
                [[((rows, 3 * wq), BF)], [((rows, RANK), BF)]], 0,
            )
            s.joint.append(out)
            s.rank_qkv.append(rank)

    def out_forward(s):
        rows = len(s.once[0]) * s.size
        partial, (s.rank_out,) = project(
            out_forward_kernel, offs, [s.w_out], [windows(s, s.att, s.once), [s.a_out], [s.b_out]],
            [blocks_out(s, s.once[0]), [((rows, RANK), BF)]], 0,
        )
        return partial

    def second_norm(s, branch):
        mod = s.mod
        s.br_attn = branch
        s.after = s.xf + mod[2:3] * branch
        s.hat2, s.inv2 = norm_rows(s.after)
        return (s.hat2 * (1.0 + mod[4:5]) + mod[3:4]).astype(BF)

    def mlp_forward(s):
        s.saved, partial = [], []
        for part in s.twice:
            rows = len(part) * s.size
            out, *saved = project(
                mlp_forward_kernel, offs, [s.w_fc1, s.w_fc2],
                [[s.n2[i] for i in part], [s.a_fc1], [s.b_fc1], [s.a_fc2], [s.b_fc2]],
                [
                    blocks_out(s, part), [((rows, ffq), BF)], [((rows, ffq), BF)],
                    [((rows, RANK), BF)], [((rows, RANK), BF)],
                ],
                0,
            )
            partial += out
            s.saved.append([v[0] for v in saved])
        return partial

    def mlp_backward(s):
        partial, sums = [], []
        for part, (act, slope, rank1, rank2) in zip(s.twice, s.saved):
            out, *more = project(
                mlp_backward_kernel, offs, [s.w_fc1, s.w_fc2],
                [
                    [s.gb_mlp[i] for i in part], [s.n2[i] for i in part], [act], [slope], [rank1], [rank2],
                    [s.a_fc1], [s.b_fc1], [s.a_fc2], [s.b_fc2],
                ],
                [blocks_out(s, part)] + [[((RANK, n), F32)] for n in (ffq, ffq, W, W)],
                1,
            )
            partial += out
            sums.append([m[0] for m in more])
        s.t_b_fc1, s.t_a_fc2, s.t_back1, s.t_in2 = [total(t) for t in zip(*sums)]
        return partial

    def second_norm_back(s, gn2):
        mod = s.mod
        s.gs_mlp = jnp.sum(own_part(s, gn2), axis=0)
        s.gc_mlp = jnp.sum(own_part(s, gn2 * s.hat2), axis=0)
        s.g_after = s.g2 + norm_back(gn2 * (1.0 + mod[4:5]), s.hat2, s.inv2)
        s.gg_attn = jnp.sum(own_part(s, s.g_after * s.br_attn), axis=0)
        return (mod[2:3] * s.g_after).astype(BF)

    def out_backward(s, gb):
        s.g_att, sums = [], []
        atts, ranks = windows(s, s.att, s.twice), windows(s, s.rank_out, s.twice)
        for part, att, rank in zip(s.twice, atts, ranks):
            rows = len(part) * s.size
            (out,), *more = project(
                out_backward_kernel, offs, [s.w_out],
                [[gb[i] for i in part], [att], [rank], [s.a_out], [s.b_out]],
                [[((rows, wq), BF)], [((RANK, W), F32)], [((RANK, wq), F32)]], 0,
            )
            s.g_att.append(out)
            sums.append([m[0] for m in more])
        s.t_back0, s.t_a_out = [total(t) for t in zip(*sums)]

    def qkv_backward(s):
        partial, (s.t_b_qkv,), (s.t_in1,) = project(
            qkv_backward_kernel, offs, [s.w_qkv],
            [windows(s, s.g_joint, s.once), [s.n1[i] for i in s.once[0]], s.rank_qkv, [s.a_qkv], [s.b_qkv]],
            [blocks_out(s, s.once[0]), [((RANK, 3 * wq), F32)], [((RANK, W), F32)]], 0,
        )
        return partial

    text.n1 = [due(text.normed, image.normed)]
    qkv_forward(text)
    bulk(0, image.n1[1])
    qkv_forward(image)
    arrived = bulk(1, image.joint[0])
    joints = [(j, None) for j in image.joint] + [(text.joint[0], 1), (swap(text.joint[0]), 0)]
    joints[0] = (due(joints[0][0], *arrived), None)
    attended, lse = attend_forward(offs, joints)
    attended = due(attended, *bulk(2, attended))
    image.att = attended
    img_partial = out_forward(image)
    arrived = bulk(3, img_partial[0])
    text.att = exchange(attended[img_len:])
    txt_partial = out_forward(text)
    branch, sent = scatter_image(img_partial, image.once)
    branch = due(branch, *arrived)
    txt_branch = sum_text(txt_partial[0]).astype(F32)
    normed = second_norm(image, branch)
    image.n2 = gather_group(normed)
    arrived = bulk(4, normed)
    late = image.w_fc2.sources[-1]
    image.g2 = image.cot.astype(F32) * image.live
    image.gb_mlp = gather_group(due((image.mod[5:6] * image.g2).astype(BF), image.n2[1]))
    text.n2 = [second_norm(text, txt_branch)]
    text.g2 = text.cot.astype(F32) * text.live
    text.gb_mlp = [(text.mod[5:6] * text.g2).astype(BF)]
    txt_done = mlp_forward(text)
    txt_partial = mlp_backward(text)
    txt_gn2 = sum_text(txt_partial[0]).astype(F32)
    image.n2[0] = due(image.n2[0], txt_partial)
    image.n2[1] = due(image.n2[1], *arrived)

    info_f = due(info_f, normed, late)
    info_all = gather_by(info_f, xr, [1] + x_bits)
    ids_all = info_all[:, :, W].astype(jnp.int32)
    silu_all = info_all[:, :, :W].astype(BF)
    rank_all = condition_ranks(silu_all.reshape(R * F, W))

    img_done = mlp_forward(image)
    out_backward(text, [second_norm_back(text, txt_gn2)])
    txt_grad = swap(text.g_att[0])
    image.gb_mlp[0] = due(image.gb_mlp[0], txt_grad)
    img_partial = mlp_backward(image)
    gn2, sent = scatter_image(img_partial, image.twice)

    gb = second_norm_back(image, gn2)
    gb_img = gather_group(gb)
    out_backward(image, gb_img)
    img_done, txt_done = due((img_done, txt_done), image.g_att)
    image.br_mlp, _ = scatter_image(img_done, image.twice)
    text.br_mlp = lax.psum_scatter(txt_done[0], "tp", scatter_dimension=0, tiled=True).astype(F32)
    for s in streams:
        s.out = ((own_part(s, s.after) + s.mod[5:6] * s.br_mlp) * s.live).astype(BF)
        s.gg_mlp = jnp.sum(own_part(s, s.g2) * s.br_mlp, axis=0)

    def combine_input(img_cols, txt_cols, rows):
        kinds = rows[0].shape[0] // RANK
        img_cols = exchange(jnp.concatenate(img_cols, axis=1).astype(BF))
        return jnp.concatenate(
            [img_cols] + [c.astype(BF) for c in txt_cols]
            + [r[i * RANK : (i + 1) * RANK] for r in rows for i in range(kinds)],
            axis=1,
        )

    def gather_all(pieces):
        return gather_by(gather_by(pieces, xf, f_bits), xr, [1] + x_bits)

    def combine(blocks, idents):
        flat = blocks.reshape(R * F * RANK, blocks.shape[-1])
        slots = (idents.reshape(R * F, 1) * RANK + jnp.arange(RANK, dtype=jnp.int32)).reshape(1, -1)
        place_rows = (row_ids[:, None] == slots).astype(BF)
        return mm(place_rows, flat)

    def reduce_rows(img_rows, txt_rows):
        return exchange(scatter_columns(img_rows, img_steps)), scatter_columns(txt_rows, txt_steps)

    def rows_home(rows):
        kinds = rows.shape[1]
        blocks = rows.astype(BF).reshape(T, Rq, kinds, wq)
        blocks = jnp.take(blocks, jnp.bitwise_xor(z, arange_t), axis=0)
        got = jnp.stack([blocks[0]] + [xz(blocks[d], d) for d in range(1, T)])
        got = jnp.take(got, jnp.bitwise_xor(z, arange_t), axis=0)
        return jnp.moveaxis(got, 0, 2).reshape(Rq, kinds, W).astype(F32)

    ids_in_order = jnp.take(
        jnp.take(ids_all, jnp.bitwise_xor(r, jnp.arange(R, dtype=jnp.int32)), axis=0),
        jnp.bitwise_xor(f, jnp.arange(F, dtype=jnp.int32)),
        axis=1,
    )
    early_blocks = lax.all_gather(
        combine_input(
            [image.t_b_fc1, image.t_a_fc2, image.t_a_out],
            [text.t_b_fc1, text.t_a_fc2, text.t_a_out],
            reduce_rows(
                *[jnp.concatenate([s.t_back1, s.t_in2, s.t_back0], axis=0).astype(BF) for s in streams]
            ),
        ),
        ("rep", "fsdp"),
    )

    grads = [(g, None) for g in image.g_att] + [(text.g_att[0], 1), (txt_grad, 0)]
    g_joint = attend_backward(offs, joints, grads, lse)
    g_joint = due(g_joint, image.br_mlp)
    out_swap = swap(image.out)
    image.g_joint = g_joint
    text.g_joint = exchange(g_joint[img_len:])
    img_partial = qkv_backward(image)
    keep = fold_cores([img_partial[flow.index(i)] for i in range(T)])
    gn1_img, sent = fold_chips(keep)
    text.g_joint = due(text.g_joint, sent)
    txt_partial = qkv_backward(text)
    late_in = combine_input(
        [image.t_b_qkv], [text.t_b_qkv], reduce_rows(image.t_in1.astype(BF), text.t_in1.astype(BF))
    )
    late_blocks = gather_all(late_in)
    gn1_img = due(gn1_img, out_swap)
    for s, gn1 in ((image, gn1_img), (text, scatter_rows(txt_partial[0]))):
        hat1, inv1, g_after = [own_part(s, v) for v in (s.hat1, s.inv1, s.g_after)]
        s.gs_attn = jnp.sum(gn1, axis=0)
        s.gc_attn = jnp.sum(gn1 * hat1, axis=0)
        dx = g_after + norm_back(gn1 * (1.0 + s.mod[1:2]), hat1, inv1)
        s.dx = dx.astype(BF)
    gm = jnp.stack(
        reduce_rows(
            *[
                jnp.stack([s.gs_attn, s.gc_attn, s.gg_attn, s.gs_mlp, s.gc_mlp, s.gg_mlp])
                for s in streams
            ]
        )
    ).astype(BF)
    gm_f = gather_by(gm, xf, f_bits)
    gm_all = gather_by(gm_f, xr, [1] + x_bits)
    early, late = combine(early_blocks, ids_in_order), combine(late_blocks, ids_all)
    span = 2 * ffq + wq
    grad_b_fc1 = jnp.stack([early[:, 0:ffq], early[:, span : span + ffq]])
    grad_a_fc2 = jnp.stack([early[:, ffq : 2 * ffq], early[:, span + ffq : span + 2 * ffq]])
    grad_a_out = jnp.stack([early[:, 2 * ffq : span], early[:, span + 2 * ffq : 2 * span]])
    grad_b_qkv = jnp.stack([late[:, : 3 * wq], late[:, 3 * wq : 6 * wq]]).reshape(2, Rf, 3, wq)
    home = rows_home(
        jnp.concatenate([early[:, 2 * span :], late[:, 6 * wq : 8 * wq]], axis=1).reshape(Rf, 8, wq)
    )

    seqs = R * F
    match = (row_adapter[None, :] == ids_all.reshape(seqs)[:, None]).astype(F32)
    gm_seq = gm_all.reshape(seqs, 2, 6, wq)
    rank_seq = (rank_all * match[:, None, :]).astype(BF)
    grad_b_ada, gcr = [], []
    for k in range(2):
        grad_b_ada.append(
            jnp.einsum("sr,scj->rcj", rank_seq[:, k], gm_seq[:, k], preferred_element_type=F32)
        )
        gcr.append(
            jnp.einsum(
                "scj,rcj->sr", gm_seq[:, k], modulation_up_factor[k], preferred_element_type=F32
            )
            * match
        )
    grad_b_ada = jnp.stack(grad_b_ada)
    gcr = jnp.stack(gcr, axis=1)
    gcr_rel = jnp.take(
        jnp.moveaxis(gcr.reshape(seqs, 2, T, Rq), 2, 0), jnp.bitwise_xor(z, arange_t), axis=0
    )
    gcr_own = gcr_rel[0]
    for d in range(1, T):
        gcr_own = gcr_own + xz(gcr_rel[d], d)
    grad_in0 = jnp.einsum(
        "ski,sd->kid",
        gcr_own,
        silu_all.reshape(seqs, W).astype(F32),
        precision=lax.Precision.HIGHEST,
    )
    gm_pair = gm_f
    dpart = jnp.zeros((F, rows_d), F32)
    for k in range(2):
        dpart = dpart + jnp.einsum(
            "fcj,dcj->fd", gm_pair[:, k], modulation_weight[k], preferred_element_type=F32
        )
    dfull = lax.dynamic_update_slice_in_dim(jnp.zeros((F, W), F32), dpart, f * rows_d, axis=1)
    dfull = dfull + jnp.einsum(
        "fki,kid->fd",
        gcr_own.reshape(R, F, 2, Rq)[0],
        adapter_down_table[0].astype(F32),
        precision=lax.Precision.HIGHEST,
    )
    dsum = dfull[0]
    for d in range(1, F):
        dsum = dsum + xf(dfull[d], d)
    for bit in t_bits:
        dsum = dsum + xz(dsum, bit)
    sigmoid = jax.nn.sigmoid(cond)
    dcond = dsum[None] * sigmoid * (1.0 + cond * (1.0 - sigmoid))

    grad_in = jnp.stack(
        [
            grad_in0,
            jnp.stack([home[:, 6], home[:, 7]]),
            jnp.stack([home[:, 1], home[:, 4]]),
        ]
    )
    grad_back = jnp.stack(
        [jnp.stack([home[:, 2], home[:, 5]]), jnp.stack([home[:, 0], home[:, 3]])]
    )
    return (
        jnp.where(native, image.out, out_swap)[None],
        text.out[None],
        exchange(image.dx)[None],
        text.dx[None],
        dcond,
        grad_in,
        grad_back,
        grad_b_ada,
        grad_b_qkv,
        grad_b_fc1,
        grad_a_out,
        grad_a_fc2,
    )


def solution(mesh):
    tokens = P(("rep", "fsdp"), "tp", None)
    table = P(None, None, ("fsdp", "tp"), None)
    columns4 = P(None, "fsdp", None, "tp")
    columns3 = P(None, "fsdp", "tp")
    rows3 = P(None, "tp", "fsdp")
    slot = P(("rep", "fsdp"))
    in_specs = (
        tokens, tokens, P(("rep", "fsdp"), None), tokens, tokens, slot, slot,
        columns4, columns4, rows3, columns3, rows3, table, table,
        columns4, columns4, columns3, columns3, columns3,
    )
    out_specs = (
        tokens, tokens, tokens, tokens, P(("rep", "fsdp"), None),
        table, table, columns4, columns4, columns3, columns3, columns3,
    )
    sizes = (mesh.shape["rep"], mesh.shape["fsdp"], mesh.shape["tp"])
    return jax.shard_map(
        functools.partial(body, sizes), mesh=mesh, in_specs=in_specs, out_specs=out_specs, check_vma=False
    )
```

time: 910 us -> 755 us (0.83)
  local copies, waits for them, and re-layouts: 200 us -> 50.3 us
  Pallas kernels: 35.9 us -> 169 us
  matrix products: 146 us -> 17.6 us
  waiting for transfers between devices: 250 us -> 189 us
  starting transfers between devices: 175 us -> 217 us
  between operations: 8.04 us -> 21.4 us
    pallas_call x2 -> x18, Pallas kernels: 35.9 us -> 169 us  [the longest x16 129 us: project(): pl.pallas_call(body, grid=(1,), in_specs=[SCALARS] + specs + [ANY] * n_sr...]
    dot_general x66 -> x2, matrix products: 127 us -> 2.5 us  [dot(): lax.dot_general(left, right, (dims, ((), ())), preferred_element_type=F32)]
    dynamic_update_slice x35 -> x0, local copies, waits for them, and re-layouts: 92.9 us -> none  [the longest x16 50.8 us: fetch_text(): full = lax.dynamic_update_slice(full, pieces[e], start)]
    ppermute x39 -> x34, starting transfers between devices: 30.3 us -> 91.8 us  [xr(): return lax.ppermute(v, 'rep', [(i, i ^ bit) for i in range(R)])]
    ppermute x39 -> x34, waiting for transfers between devices: 42.7 us -> 2.73 us  [xr(): return lax.ppermute(v, 'rep', [(i, i ^ bit) for i in range(R)])]
    ppermute x17 -> x21, starting transfers between devices: 56.5 us -> 22.7 us  [the longest x18 18.1 us: swap(): return lax.ppermute(v, ('rep', 'tp'), swap_pairs)]
    ppermute x47 -> x41, starting transfers between devices: 66.5 us -> 85.2 us  [xz(): return lax.ppermute(v, 'tp', [(i, i ^ bit) for i in range(T)])]
    ppermute x16 -> x14, waiting for transfers between devices: 22.8 us -> 5.59 us  [xf(): return lax.ppermute(v, 'fsdp', [(i, i ^ bit) for i in range(F)])]
  transfers between devices with their start and end apart: 119 -> 112, of which waited for: 40 -> 33; matrix products, arithmetic and copies ran while one was open for 41% -> 16% of each run, Pallas kernels for 1% -> 22%
where the time goes in v1:
time: 755 us; the launch traced here: 744 us
  starting transfers between devices  217 us (29%)
  waiting for transfers between devices  189 us (25%)
  Pallas kernels  169 us (22%)
  other arithmetic  79.6 us (11%)
  local copies, waits for them, and re-layouts  50.3 us (7%)
  between operations  21.4 us (3%)
  matrix products  17.6 us (2%)
    ppermute x41, waiting for transfers between devices, xz(): return lax.ppermute(v, 'tp', [(i, i ^ bit) for i in range(T)])  181 us
    pallas_call x16, Pallas kernels, project(): pl.pallas_call(body, grid=(1,), in_specs=[SCALARS] + specs + [ANY] * n_sr...  129 us
    ppermute x34, starting transfers between devices, xr(): return lax.ppermute(v, 'rep', [(i, i ^ bit) for i in range(R)])  91.8 us
    ppermute x41, starting transfers between devices, xz(): return lax.ppermute(v, 'tp', [(i, i ^ bit) for i in range(T)])  85.2 us
    pallas_call x1, Pallas kernels, attend_backward(): pl.pallas_call(functools.partial(attend_backward_kernel, width, blocks, p...  26.4 us
    ppermute x18, starting transfers between devices, swap(): return lax.ppermute(v, ('rep', 'tp'), swap_pairs)  18.1 us
    ppermute x14, starting transfers between devices, xf(): return lax.ppermute(v, 'fsdp', [(i, i ^ bit) for i in range(F)])  17.2 us
    unnamed x281, local copies, waits for them, and re-layouts  17 us
  transfers between devices with their start and end apart: 112, of which 33 were waited for; matrix products, arithmetic and copies ran while one was open for 16% of the time, Pallas kernels for 22%

profile of v1, /device:TPU:0, one launch (start us, length us, event | category | flops | bytes accessed | tf_op | source)
XLA Modules:
  0.0 744.4 jit_solution(2621946722992705388)
XLA Ops:
  25.4 6.9 collective-permute-start.3
  32.4 7.8 %collective-permute-done.3 = bf16[2,2,2,16]{3,2,1,0:T(2,128)(2,1)S(1)} collective-permute-done((bf16[2,2,2,16]{3,2,1,0:T(2,128)(2,1)S(1)}, bf16[2,2,2,16]{3,2,1,0:T(2,128)(2,1)S(1)}, u32[]{:S(2)}, u32[]{:S(2)}) %collective-permute-start.3) | collective-permute-done | bytes 288 | tf_op jit(solution)/shard_map/ppermute | solution.py:459
  60.8 5.0 collective-permute-start.8
  65.7 7.7 %collective-permute-done.23 = bf16[1,64,1536]{2,1,0:T(8,128)(2,1)S(1)} collective-permute-done((bf16[1,64,1536]{2,1,0:T(8,128)(2,1)S(1)}, bf16[1,64,1536]{2,1,0:T(8,128)(2,1)S(1)}, u32[]{:S(2)}, u32[]{:S(2)}) %collective-permute-start.23) | collective-permute-done | bytes 196640 | tf_op jit(solution)/shard_map/ppermute | solution.py:459
  76.8 16.5 %collective-permute-done.24 = bf16[2,64,1536]{2,1,0:T(8,128)(2,1)S(1)} collective-permute-done((bf16[2,64,1536]{2,1,0:T(8,128)(2,1)S(1)}, bf16[2,64,1536]{2,1,0:T(8,128)(2,1)S(1)}, u32[]{:S(2)}, u32[]{:S(2)}) %collective-permute-start.24) | collective-permute-done | bytes 393248 | tf_op jit(solution)/shard_map/ppermute | solution.py:459
  107.6 7.2 collective-permute-done.12
  118.9 16.2 %collective-permute-done.13 = bf16[2,16,6144]{2,1,0:T(8,128)(2,1)S(1)} collective-permute-done((bf16[2,16,6144]{2,1,0:T(8,128)(2,1)S(1)}, bf16[2,16,6144]{2,1,0:T(8,128)(2,1)S(1)}, u32[]{:S(2)}, u32[]{:S(2)}) %collective-permute-start.13) | collective-permute-done | bytes 393248 | tf_op jit(solution)/shard_map/ppermute | solution.py:459
  152.1 16.0 %collective-permute-start.22 = (bf16[224,1536]{1,0:T(8,128)(2,1)}, bf16[224,1536]{1,0:T(8,128)(2,1)S(1)}, u32[]{:S(2)}, u32[]{:S(2)}) collective-permute-start(bf16[224,1536]{1,0:T(8,128)(2,1)} %collective-permute-done.19.refs_0_.refs_3_), channel_id=1, source_target_pairs={{0,8},{8,0},{16,24},{24,16},{1,9},{9,1},{17,25},{25,17},{2,10},{10... | collective-permute-start | bytes 2064392 | tf_op jit(solution)/shard_map/ppermute | solution.py:465
  169.0 6.9 shard_map.274
  184.3 20.4 %collective-permute-start.38 = (bf16[192,768]{1,0:T(8,128)(2,1)}, bf16[192,768]{1,0:T(8,128)(2,1)}, u32[]{:S(2)}, u32[]{:S(2)}) collective-permute-start(bf16[192,768]{1,0:T(8,128)(2,1)} %collective-permute-done.28.refs_4_.refs_6_), channel_id=1, source_target_pairs={{0,8},{8,0},{16,24},{24,16},{1,9},{9,1},{17,25},{25,17},{2,10},{10... | collective-permute-start | bytes 884744 | tf_op jit(solution)/shard_map/ppermute | solution.py:465
  205.6 7.0 shard_map.275
  214.4 14.0 %attend_forward.1 = (bf16[1024,384]{1,0:T(8,128)(2,1)S(1)}, f32[1024,6]{1,0:T(8,128)S(1)}) custom-call(s32[15]{0:T(128)S(1)} %copy-done.1, bf16[448,1152]{1,0:T(8,128)(2,1)S(1)} %copy-done.7, bf16[448,1152]{1,0:T(8,128)(2,1)S(1)} %copy-done.8, bf16[128,1152]{1,0:T(8,128)(2,1)S(1)} %copy-done.5, bf16[128,1152]{1,0:T(8,128)(2,1)S(1)} %collective-permute-done.26.refs_3_), custom_call_target="tpu_custom_call" | custom-call | flops 6442450944 | bytes 4718592 | tf_op jit(solution)/shard_map/attend_forward/pallas_call | solution.py:203
  257.4 6.3 shard_map.277
  263.7 16.7 %collective-permute-done.40 = bf16[128,1536]{1,0:T(8,128)(2,1)S(1)} collective-permute-done((bf16[128,1536]{1,0:T(8,128)(2,1)S(1)}, bf16[128,1536]{1,0:T(8,128)(2,1)S(1)}, u32[]{:S(2)}, u32[]{:S(2)}) %collective-permute-start.40) | collective-permute-done | bytes 393248 | tf_op jit(solution)/shard_map/ppermute | solution.py:459
  287.0 7.3 shard_map.279
  294.4 8.5 %shard_map.280 = (bf16[128,1536]{1,0:T(8,128)(2,1)}, f32[16,1536]{1,0:T(8,128)}, f32[16,1536]{1,0:T(8,128)}, f32[16,1536]{1,0:T(8,128)}, f32[16,1536]{1,0:T(8,128)}) custom-call(s32[15]{0:T(128)} %stack.229.offs_ref.offs, bf16[128,1536]{1,0:T(8,128)(2,1)} %multiply_convert_fusion.4.refs_0_, bf16[128,1536]{1,0:T(8,128)(2,1)} %get-tuple-element.352.refs_0_.refs_1_, ...), custom_call_target="tpu_custom_call" | custom-call | flops 2415919104 | bytes 10027008 | tf_op jit(solution)/shard_map/pallas_call | solution.py:395
  306.9 10.7 %collective-permute-done.51 = bf16[128,1536]{1,0:T(8,128)(2,1)S(1)} collective-permute-done((bf16[128,1536]{1,0:T(8,128)(2,1)}, bf16[128,1536]{1,0:T(8,128)(2,1)S(1)}, u32[]{:S(2)}, u32[]{:S(2)}) %collective-permute-start.51) | collective-permute-done | bytes 393248 | tf_op jit(solution)/shard_map/ppermute | solution.py:459
  326.9 18.6 %collective-permute-done.52 = bf16[128,1536]{1,0:T(8,128)(2,1)S(1)} collective-permute-done((bf16[128,1536]{1,0:T(8,128)(2,1)S(1)}, bf16[128,1536]{1,0:T(8,128)(2,1)S(1)}, u32[]{:S(2)}, u32[]{:S(2)}) %collective-permute-start.52) | collective-permute-done | bytes 393248 | tf_op jit(solution)/shard_map/ppermute | solution.py:459
  363.0 10.9 %collective-permute-done.48.refs_0_.refs_2_ = bf16[224,1536]{1,0:T(8,128)(2,1)S(1)} collective-permute-done((bf16[224,1536]{1,0:T(8,128)(2,1)}, bf16[224,1536]{1,0:T(8,128)(2,1)S(1)}, u32[]{:S(2)}, u32[]{:S(2)}) %collective-permute-start.48) | collective-permute-done | bytes 688160 | tf_op jit(solution)/shard_map/ppermute | solution.py:459
  382.3 9.3 %collective-permute-start.54 = (bf16[224,1536]{1,0:T(8,128)(2,1)S(1)}, bf16[224,1536]{1,0:T(8,128)(2,1)S(1)}, u32[]{:S(2)}, u32[]{:S(2)}) collective-permute-start(bf16[224,1536]{1,0:T(8,128)(2,1)S(1)} %get-tuple-element.230.refs_0_), channel_id=1, source_target_pairs={{0,8},{8,0},{16,24},{24,16},{1,9},{9,1},{17,25},{25,17},{2,10},{10... | collective-permute-start | bytes 2064392 | tf_op jit(solution)/shard_map/ppermute | solution.py:465
  396.0 15.6 %shard_map.282 = (bf16[224,1536]{1,0:T(8,128)(2,1)}, bf16[224,1536]{1,0:T(8,128)(2,1)}, bf16[448,1536]{1,0:T(8,128)(2,1)}, bf16[448,1536]{1,0:T(8,128)(2,1)}, bf...) custom-call(s32[15]{0:T(128)} %stack.229.offs_ref.offs, bf16[224,1536]{1,0:T(8,128)(2,1)} %copy-done.127, ...), custom_call_target="tpu_custom_call" | custom-call | flops 8455716864 | bytes 13594624 | tf_op jit(solution)/shard_map/pallas_call | solution.py:395
  412.4 12.6 %shard_map.285 = (bf16[224,1536]{1,0:T(8,128)(2,1)}, bf16[224,1536]{1,0:T(8,128)(2,1)}, f32[16,1536]{1,0:T(8,128)}, f32[16,1536]{1,0:T(8,128)}, f32[16,1536]{1,0:T(8,128)}, /*index=5*/f32[16,1536]{1,0:T(8,128)}) custom-call(s32[15]{0:T(128)} %stack.229.offs_ref.offs, bf16[224,1536]{1,0:T(8,128)(2,1)} %collective-permute-done.56.refs_0_, ...), custom_call_target="tpu_custom_call" | custom-call | flops 8455716864 | bytes 11010048 | tf_op jit(solution)/shard_map/pallas_call | solution.py:395
  425.9 15.5 %shard_map.281 = (bf16[224,1536]{1,0:T(8,128)(2,1)}, bf16[224,1536]{1,0:T(8,128)(2,1)}, bf16[448,1536]{1,0:T(8,128)(2,1)}, bf16[448,1536]{1,0:T(8,128)(2,1)}, bf...) custom-call(s32[15]{0:T(128)} %stack.229.offs_ref.offs, bf16[224,1536]{1,0:T(8,128)(2,1)} %add_convert_fusion.3.refs_0_.refs_2_, ...), custom_call_target="tpu_custom_call" | custom-call | flops 8455716864 | bytes 13594624 | tf_op jit(solution)/shard_map/pallas_call | solution.py:395
  442.4 12.7 %shard_map.284 = (bf16[224,1536]{1,0:T(8,128)(2,1)}, bf16[224,1536]{1,0:T(8,128)(2,1)}, f32[16,1536]{1,0:T(8,128)}, f32[16,1536]{1,0:T(8,128)}, f32[16,1536]{1,0:T(8,128)}, /*index=5*/f32[16,1536]{1,0:T(8,128)}) custom-call(s32[15]{0:T(128)} %stack.229.offs_ref.offs, bf16[224,1536]{1,0:T(8,128)(2,1)} %copy-done.44, bf16[224,1536]{1,0:T(8,128)(2,1)} %copy-done.130, ...), custom_call_target="tpu_custom_call" | custom-call | flops 8455716864 | bytes 11010048 | tf_op jit(solution)/shard_map/pallas_call | solution.py:395
  466.9 14.6 %collective-permute-done.59 = bf16[224,1536]{1,0:T(8,128)(2,1)} collective-permute-done((bf16[224,1536]{1,0:T(8,128)(2,1)}, bf16[224,1536]{1,0:T(8,128)(2,1)}, u32[]{:S(2)}, u32[]{:S(2)}) %collective-permute-start.59) | collective-permute-done | bytes 688160 | tf_op jit(solution)/shard_map/ppermute | solution.py:459
  492.4 11.6 %collective-permute-done.61.refs_0_ = bf16[224,1536]{1,0:T(8,128)(2,1)S(1)} collective-permute-done((bf16[224,1536]{1,0:T(8,128)(2,1)S(1)}, bf16[224,1536]{1,0:T(8,128)(2,1)S(1)}, u32[]{:S(2)}, u32[]{:S(2)}) %collective-permute-start.61) | collective-permute-done | bytes 688160 | tf_op jit(solution)/shard_map/ppermute | solution.py:459
  532.9 26.4 %attend_backward.1.refs_0_ = bf16[1024,1152]{1,0:T(8,128)(2,1)} custom-call(s32[15]{0:T(128)S(1)} %copy-done.2, f32[1024,6]{1,0:T(8,128)S(1)} %copy-done.11, bf16[448,1152]{1,0:T(8,128)(2,1)S(1)} %copy-done.7, bf16[448,1152]{1,0:T(8,128)(2,1)S(1)} %copy-done.9, bf16[128,1152]{1,0:T(8,128)(2,1)S(1)} %copy-done.5, ...), custom_call_target="tpu_custom_call" | custom-call | flops 12884901888 | bytes 9437184 | tf_op jit(solution)/shard_map/attend_backward/pallas_call | solution.py:235
  562.0 13.0 %collective-permute-done.65 = bf16[224,1536]{1,0:T(8,128)(2,1)S(1)} collective-permute-done((bf16[224,1536]{1,0:T(8,128)(2,1)S(1)}, bf16[224,1536]{1,0:T(8,128)(2,1)S(1)}, u32[]{:S(2)}, u32[]{:S(2)}) %collective-permute-start.65) | collective-permute-done | bytes 688160 | tf_op jit(solution)/shard_map/ppermute | solution.py:459
  576.8 10.5 %shard_map.288 = (bf16[224,1536]{1,0:T(8,128)(2,1)}, bf16[224,1536]{1,0:T(8,128)(2,1)}, bf16[224,1536]{1,0:T(8,128)(2,1)}, bf16[224,1536]{1,0:T(8,128)(2,1)}, f32[16,1152]{1,0:T(8,128)}, /*index=5*/f32[16,1536]{1,0:T(8,128)}) custom-call(s32[15]{0:T(128)} %stack.229.offs_ref.offs, bf16[1024,1152]{1,0:T(8,128)(2,1)} %attend_backward.1.refs_0_, ...), custom_call_target="tpu_custom_call" | custom-call | flops 6341787648 | bytes 6377472 | tf_op jit(solution)/shard_map/pallas_call | solution.py:395
  608.8 5.2 shard_map.289
  615.0 23.4 %collective-permute-start.100 = (bf16[16,768]{1,0:T(8,128)(2,1)S(1)}, bf16[16,768]{1,0:T(8,128)(2,1)S(1)}, u32[]{:S(2)}, u32[]{:S(2)}) collective-permute-start(bf16[16,768]{1,0:T(8,128)(2,1)S(1)} %broadcast_select_fusion.21), channel_id=1, source_target_pairs={{0,2},{1,3},{2,0},{3,1},{4,6},{5,7},{6,4},{7,5},{8,10},{9,11},{10,... | collective-permute-start | bytes 73736 | tf_op jit(solution)/shard_map/ppermute | solution.py:459
  642.9 5.6 collective-permute-done.72
  (810 shorter events, 336.5 us)
Async XLA Ops:
  8.0 584.9 %reduce-scatter.2.cloned.1.call-start = ((), (), s32[]{:S(2)}) async-start(), calls=%async_computation.1 | async-start | bytes 491520 | tf_op jit(solution)/shard_map/reduce_scatter | solution.py:1084
  49.1 46.5 %collective-permute-start.4 = (bf16[224,1536]{1,0:T(8,128)(2,1)}, bf16[224,1536]{1,0:T(8,128)(2,1)}, u32[]{:S(2)}, u32[]{:S(2)}) collective-permute-start(bf16[224,1536]{1,0:T(8,128)(2,1)} %bitcast), channel_id=1, source_target_pairs={{2,8},{3,9},{8,2},{9,3},{18,24},{19,25},{24,18},{25,19},{6,12},{7,... | collective-permute-start | bytes 2064392 | tf_op jit(solution)/shard_map/ppermute | solution.py:475
  50.6 128.2 %collective-permute-start.25 = (bf16[3,384,384]{2,1,0:T(8,128)(2,1)}, bf16[3,384,384]{2,1,0:T(8,128)(2,1)}, u32[]{:S(2)}, u32[]{:S(2)}) collective-permute-start(bf16[3,384,384]{2,1,0:T(8,128)(2,1)} %collective-permute-done.5.refs_4_.refs_6_), channel_id=1, source_target_pairs={{0,8},{8,0},{16,24},{24,16},{1,9},{9,1},{17,25},{25,17},{2,10},{10... | collective-permute-start | bytes 2654216 | tf_op jit(solution)/shard_map/ppermute | solution.py:465
  55.3 80.7 %collective-permute-start.16 = (bf16[3,384,384]{2,1,0:T(8,128)(2,1)}, bf16[3,384,384]{2,1,0:T(8,128)(2,1)}, u32[]{:S(2)}, u32[]{:S(2)}) collective-permute-start(bf16[3,384,384]{2,1,0:T(8,128)(2,1)} %collective-permute-done.refs_5_.refs_10_), channel_id=1, source_target_pairs={{2,18},{3,19},{8,24},{9,25},{18,2},{19,3},{24,8},{25,9},{6,22},{7,... | collective-permute-start | bytes 2654216 | tf_op jit(solution)/shard_map/ppermute | solution.py:478
  102.8 32.4 %collective-permute-start.17 = (bf16[3,384,384]{2,1,0:T(8,128)(2,1)S(1)}, bf16[3,384,384]{2,1,0:T(8,128)(2,1)S(1)}, u32[]{:S(2)}, u32[]{:S(2)}) collective-permute-start(bf16[3,384,384]{2,1,0:T(8,128)(2,1)S(1)} %copy-done.39), channel_id=1, source_target_pairs={{0,4},{4,0},{1,5},{5,1},{2,6},{6,2},{3,7},{7,3},{8,12},{12,8},{9,1... | collective-permute-start | bytes 2654216 | tf_op jit(solution)/shard_map/ppermute | solution.py:462
  105.5 35.3 %collective-permute-start.19 = (bf16[224,1536]{1,0:T(8,128)(2,1)S(1)}, bf16[224,1536]{1,0:T(8,128)(2,1)}, u32[]{:S(2)}, u32[]{:S(2)}) collective-permute-start(bf16[224,1536]{1,0:T(8,128)(2,1)S(1)} %fusion.19.refs_0_.refs_1_), channel_id=1, source_target_pairs={{0,1},{1,0},{2,3},{3,2},{4,5},{5,4},{6,7},{7,6},{8,9},{9,8},{10,11... | collective-permute-start | bytes 2064392 | tf_op jit(solution)/shard_map/ppermute | solution.py:459
  149.9 62.7 %collective-permute-start.29 = (bf16[384,1536]{1,0:T(8,128)(2,1)}, bf16[384,1536]{1,0:T(8,128)(2,1)}, u32[]{:S(2)}, u32[]{:S(2)}) collective-permute-start(bf16[384,1536]{1,0:T(8,128)(2,1)} %dynamic-slice_bitcast_fusion.2), channel_id=1, source_target_pairs={{0,4},{4,0},{1,5},{5,1},{2,6},{6,2},{3,7},{7,3},{8,12},{12,8},{9,1... | collective-permute-start | bytes 3538952 | tf_op jit(solution)/shard_map/ppermute | solution.py:462
  152.1 52.6 %collective-permute-start.22 = (bf16[224,1536]{1,0:T(8,128)(2,1)}, bf16[224,1536]{1,0:T(8,128)(2,1)S(1)}, u32[]{:S(2)}, u32[]{:S(2)}) collective-permute-start(bf16[224,1536]{1,0:T(8,128)(2,1)} %collective-permute-done.19.refs_0_.refs_3_), channel_id=1, source_target_pairs={{0,8},{8,0},{16,24},{24,16},{1,9},{9,1},{17,25},{25,17},{2,10},{10... | collective-permute-start | bytes 2064392 | tf_op jit(solution)/shard_map/ppermute | solution.py:465
  175.9 53.2 %collective-permute-start.27 = (bf16[384,1536]{1,0:T(8,128)(2,1)}, bf16[384,1536]{1,0:T(8,128)(2,1)}, u32[]{:S(2)}, u32[]{:S(2)}) collective-permute-start(bf16[384,1536]{1,0:T(8,128)(2,1)} %collective-permute-done.21.refs_7_.refs_18_), channel_id=1, source_target_pairs={{2,18},{3,19},{8,24},{9,25},{18,2},{19,3},{24,8},{25,9},{6,22},{7,... | collective-permute-start | bytes 3538952 | tf_op jit(solution)/shard_map/ppermute | solution.py:478
  184.3 48.8 %collective-permute-start.38 = (bf16[192,768]{1,0:T(8,128)(2,1)}, bf16[192,768]{1,0:T(8,128)(2,1)}, u32[]{:S(2)}, u32[]{:S(2)}) collective-permute-start(bf16[192,768]{1,0:T(8,128)(2,1)} %collective-permute-done.28.refs_4_.refs_6_), channel_id=1, source_target_pairs={{0,8},{8,0},{16,24},{24,16},{1,9},{9,1},{17,25},{25,17},{2,10},{10... | collective-permute-start | bytes 884744 | tf_op jit(solution)/shard_map/ppermute | solution.py:465
  243.2 42.4 %collective-permute-start.41 = (bf16[384,1536]{1,0:T(8,128)(2,1)}, bf16[384,1536]{1,0:T(8,128)(2,1)S(1)}, u32[]{:S(2)}, u32[]{:S(2)}) collective-permute-start(bf16[384,1536]{1,0:T(8,128)(2,1)} %collective-permute-done.29.refs_6_.refs_14_), channel_id=1, source_target_pairs={{0,8},{8,0},{16,24},{24,16},{1,9},{9,1},{17,25},{25,17},{2,10},{10... | collective-permute-start | bytes 3538952 | tf_op jit(solution)/shard_map/ppermute | solution.py:465
  247.2 33.1 %collective-permute-start.40 = (bf16[128,1536]{1,0:T(8,128)(2,1)S(1)}, bf16[128,1536]{1,0:T(8,128)(2,1)S(1)}, u32[]{:S(2)}, u32[]{:S(2)}) collective-permute-start(bf16[128,1536]{1,0:T(8,128)(2,1)S(1)} %add.513), channel_id=1, source_target_pairs={{0,2},{1,3},{2,0},{3,1},{4,6},{5,7},{6,4},{7,5},{8,10},{9,11},{10,... | collective-permute-start | bytes 1179656 | tf_op jit(solution)/shard_map/ppermute | solution.py:459
  253.3 51.9 %collective-permute-start.36 = (bf16[768,768]{1,0:T(8,128)(2,1)}, bf16[768,768]{1,0:T(8,128)(2,1)}, u32[]{:S(2)}, u32[]{:S(2)}) collective-permute-start(bf16[768,768]{1,0:T(8,128)(2,1)} %dynamic-slice_bitcast_fusion), channel_id=1, source_target_pairs={{2,8},{3,9},{8,2},{9,3},{18,24},{19,25},{24,18},{25,19},{6,12},{7,... | collective-permute-start | bytes 3538952 | tf_op jit(solution)/shard_map/ppermute | solution.py:475
  256.0 62.7 %collective-permute-start.35 = (bf16[384,1536]{1,0:T(8,128)(2,1)}, bf16[384,1536]{1,0:T(8,128)(2,1)}, u32[]{:S(2)}, u32[]{:S(2)}) collective-permute-start(bf16[384,1536]{1,0:T(8,128)(2,1)} %broadcast_select_fusion.1), channel_id=1, source_target_pairs={{0,4},{4,0},{1,5},{5,1},{2,6},{6,2},{3,7},{7,3},{8,12},{12,8},{9,1... | collective-permute-start | bytes 3538952 | tf_op jit(solution)/shard_map/ppermute | solution.py:462
  285.0 35.9 %collective-permute-start.32 = (bf16[224,1536]{1,0:T(8,128)(2,1)}, bf16[224,1536]{1,0:T(8,128)(2,1)S(1)}, u32[]{:S(2)}, u32[]{:S(2)}) collective-permute-start(bf16[224,1536]{1,0:T(8,128)(2,1)} %get-tuple-element.196), channel_id=1, source_target_pairs={{0,8},{8,0},{16,24},{24,16},{1,9},{9,1},{17,25},{25,17},{2,10},{10... | collective-permute-start | bytes 2064392 | tf_op jit(solution)/shard_map/ppermute | solution.py:465
  285.6 35.3 %collective-permute-start.34 = (bf16[224,1536]{1,0:T(8,128)(2,1)S(1)}, bf16[224,1536]{1,0:T(8,128)(2,1)}, u32[]{:S(2)}, u32[]{:S(2)}) collective-permute-start(bf16[224,1536]{1,0:T(8,128)(2,1)S(1)} %add_convert_fusion.4), channel_id=1, source_target_pairs={{0,1},{1,0},{2,3},{3,2},{4,5},{5,4},{6,7},{7,6},{8,9},{9,8},{10,11... | collective-permute-start | bytes 2064392 | tf_op jit(solution)/shard_map/ppermute | solution.py:459
  318.6 33.0 %collective-permute-start.44 = (bf16[384,1536]{1,0:T(8,128)(2,1)}, bf16[384,1536]{1,0:T(8,128)(2,1)}, u32[]{:S(2)}, u32[]{:S(2)}) collective-permute-start(bf16[384,1536]{1,0:T(8,128)(2,1)} %collective-permute-done.35.refs_9_.refs_20_), channel_id=1, source_target_pairs={{0,16},{8,24},{16,0},{24,8},{1,17},{9,25},{17,1},{25,9},{2,18},{10... | collective-permute-start | bytes 3538952 | tf_op jit(solution)/shard_map/ppermute | solution.py:465
  319.8 40.0 %collective-permute-start.46 = (bf16[768,768]{1,0:T(8,128)(2,1)S(1)}, bf16[768,768]{1,0:T(8,128)(2,1)}, u32[]{:S(2)}, u32[]{:S(2)}) collective-permute-start(bf16[768,768]{1,0:T(8,128)(2,1)S(1)} %broadcast_select_fusion), channel_id=1, source_target_pairs={{0,4},{4,0},{1,5},{5,1},{2,6},{6,2},{3,7},{7,3},{8,12},{12,8},{9,1... | collective-permute-start | bytes 3538952 | tf_op jit(solution)/shard_map/ppermute | solution.py:462
  325.3 35.4 %collective-permute-start.50 = (bf16[224,1536]{1,0:T(8,128)(2,1)}, bf16[224,1536]{1,0:T(8,128)(2,1)}, u32[]{:S(2)}, u32[]{:S(2)}) collective-permute-start(bf16[224,1536]{1,0:T(8,128)(2,1)} %bitcast.59), channel_id=1, source_target_pairs={{2,8},{3,9},{8,2},{9,3},{18,24},{19,25},{24,18},{25,19},{6,12},{7,... | collective-permute-start | bytes 2064392 | tf_op jit(solution)/shard_map/ppermute | solution.py:475
  359.8 33.5 %collective-permute-start.47 = (bf16[768,768]{1,0:T(8,128)(2,1)}, bf16[768,768]{1,0:T(8,128)(2,1)S(1)}, u32[]{:S(2)}, u32[]{:S(2)}) collective-permute-start(bf16[768,768]{1,0:T(8,128)(2,1)} %collective-permute-done.46.refs_14_.refs_15_), channel_id=1, source_target_pairs={{0,16},{8,24},{16,0},{24,8},{1,17},{9,25},{17,1},{25,9},{2,18},{10... | collective-permute-start | bytes 3538952 | tf_op jit(solution)/shard_map/ppermute | solution.py:465
  379.1 46.0 %collective-permute-start.43 = (bf16[224,1536]{1,0:T(8,128)(2,1)S(1)}, bf16[224,1536]{1,0:T(8,128)(2,1)S(1)}, u32[]{:S(2)}, u32[]{:S(2)}) collective-permute-start(bf16[224,1536]{1,0:T(8,128)(2,1)S(1)} %copy-done.40), channel_id=1, source_target_pairs={{0,8},{8,0},{16,24},{24,16},{1,9},{9,1},{17,25},{25,17},{2,10},{10... | collective-permute-start | bytes 2064392 | tf_op jit(solution)/shard_map/ppermute | solution.py:465
  382.3 59.2 %collective-permute-start.54 = (bf16[224,1536]{1,0:T(8,128)(2,1)S(1)}, bf16[224,1536]{1,0:T(8,128)(2,1)S(1)}, u32[]{:S(2)}, u32[]{:S(2)}) collective-permute-start(bf16[224,1536]{1,0:T(8,128)(2,1)S(1)} %get-tuple-element.230.refs_0_), channel_id=1, source_target_pairs={{0,8},{8,0},{16,24},{24,16},{1,9},{9,1},{17,25},{25,17},{2,10},{10... | collective-permute-start | bytes 2064392 | tf_op jit(solution)/shard_map/ppermute | solution.py:465
  394.3 67.4 %collective-permute-start.74 = (f32[1,2,1664]{2,1,0:T(2,128)S(1)}, f32[1,2,1664]{2,1,0:T(2,128)S(1)}, u32[]{:S(2)}, u32[]{:S(2)}) collective-permute-start(f32[1,2,1664]{2,1,0:T(2,128)S(1)} %bitcast.346), channel_id=1, source_target_pairs={{0,8},{8,0},{16,24},{24,16},{1,9},{9,1},{17,25},{25,17},{2,10},{10... | collective-permute-start | bytes 39944 | tf_op jit(solution)/shard_map/ppermute | solution.py:465
  425.0 38.0 %collective-permute-start.58 = (bf16[224,1536]{1,0:T(8,128)(2,1)}, bf16[224,1536]{1,0:T(8,128)(2,1)S(1)}, u32[]{:S(2)}, u32[]{:S(2)}) collective-permute-start(bf16[224,1536]{1,0:T(8,128)(2,1)} %get-tuple-element.242), channel_id=1, source_target_pairs={{0,8},{8,0},{16,24},{24,16},{1,9},{9,1},{17,25},{25,17},{2,10},{10... | collective-permute-start | bytes 2064392 | tf_op jit(solution)/shard_map/ppermute | solution.py:465
  521.4 199.9 %all-gather.3.cloned.1.call-start = ((), (), s32[]{:S(2)}) async-start(), calls=%async_computation.2 | async-start | bytes 2654208 | tf_op jit(solution)/shard_map/all_gather | solution.py:1123
  525.0 35.3 %collective-permute-start.90 = (bf16[16,3456]{1,0:T(8,128)(2,1)S(1)}, bf16[16,3456]{1,0:T(8,128)(2,1)S(1)}, u32[]{:S(2)}, u32[]{:S(2)}) collective-permute-start(bf16[16,3456]{1,0:T(8,128)(2,1)S(1)} %pad_maximum_fusion.16), channel_id=1, source_target_pairs={{2,8},{3,9},{8,2},{9,3},{18,24},{19,25},{24,18},{25,19},{6,12},{7,... | collective-permute-start | bytes 331784 | tf_op jit(solution)/shard_map/ppermute | solution.py:475
  525.7 36.3 %collective-permute-start.63 = (bf16[224,1536]{1,0:T(8,128)(2,1)}, bf16[224,1536]{1,0:T(8,128)(2,1)}, u32[]{:S(2)}, u32[]{:S(2)}) collective-permute-start(bf16[224,1536]{1,0:T(8,128)(2,1)} %get-tuple-element.247), channel_id=1, source_target_pairs={{0,8},{8,0},{16,24},{24,16},{1,9},{9,1},{17,25},{25,17},{2,10},{10... | collective-permute-start | bytes 2064392 | tf_op jit(solution)/shard_map/ppermute | solution.py:465
  530.0 30.5 %collective-permute-start.64 = (bf16[224,1536]{1,0:T(8,128)(2,1)}, bf16[224,1536]{1,0:T(8,128)(2,1)S(1)}, u32[]{:S(2)}, u32[]{:S(2)}) collective-permute-start(bf16[224,1536]{1,0:T(8,128)(2,1)} %get-tuple-element.249), channel_id=1, source_target_pairs={{0,8},{8,0},{16,24},{24,16},{1,9},{9,1},{17,25},{25,17},{2,10},{10... | collective-permute-start | bytes 2064392 | tf_op jit(solution)/shard_map/ppermute | solution.py:465
  597.9 67.5 %collective-permute-start.67 = (bf16[224,1536]{1,0:T(8,128)(2,1)}, bf16[224,1536]{1,0:T(8,128)(2,1)S(1)}, u32[]{:S(2)}, u32[]{:S(2)}) collective-permute-start(bf16[224,1536]{1,0:T(8,128)(2,1)} %get-tuple-element.256), channel_id=1, source_target_pairs={{0,8},{8,0},{16,24},{24,16},{1,9},{9,1},{17,25},{25,17},{2,10},{10... | collective-permute-start | bytes 2064392 | tf_op jit(solution)/shard_map/ppermute | solution.py:465
  602.9 36.6 %collective-permute-start.66 = (bf16[224,1536]{1,0:T(8,128)(2,1)S(1)}, bf16[224,1536]{1,0:T(8,128)(2,1)S(1)}, u32[]{:S(2)}, u32[]{:S(2)}) collective-permute-start(bf16[224,1536]{1,0:T(8,128)(2,1)S(1)} %multiply_convert_fusion), channel_id=1, source_target_pairs={{2,8},{3,9},{8,2},{9,3},{18,24},{19,25},{24,18},{25,19},{6,12},{7,... | collective-permute-start | bytes 2064392 | tf_op jit(solution)/shard_map/ppermute | solution.py:475
  607.1 58.3 %collective-permute-start.69 = (bf16[224,1536]{1,0:T(8,128)(2,1)}, bf16[224,1536]{1,0:T(8,128)(2,1)}, u32[]{:S(2)}, u32[]{:S(2)}) collective-permute-start(bf16[224,1536]{1,0:T(8,128)(2,1)} %add_convert_fusion), channel_id=1, source_target_pairs={{0,1},{1,0},{2,3},{3,2},{4,5},{5,4},{6,7},{7,6},{8,9},{9,8},{10,11... | collective-permute-start | bytes 2064392 | tf_op jit(solution)/shard_map/ppermute | solution.py:459
  677.3 42.0 %collective-permute-start.70 = (bf16[224,1536]{1,0:T(8,128)(2,1)}, bf16[224,1536]{1,0:T(8,128)(2,1)S(1)}, u32[]{:S(2)}, u32[]{:S(2)}) collective-permute-start(bf16[224,1536]{1,0:T(8,128)(2,1)} %fusion.24), channel_id=1, source_target_pairs={{2,8},{3,9},{8,2},{9,3},{18,24},{19,25},{24,18},{25,19},{6,12},{7,... | collective-permute-start | bytes 2064392 | tf_op jit(solution)/shard_map/ppermute | solution.py:475
  (215 other events, 2562.5 us)
Sparse Core Ops, SparseCore 0:
  521.5 22.4 reduce-scatter.1
Sparse Core Ops, SparseCore 1:
  562.1 32.1 all-gather.2

commit v2 on v1

--- a/solution.py
+++ b/solution.py
@@ -215,7 +215,7 @@
         scratch_shapes=[pltpu.VMEM((length, width3), BF), pltpu.SemaphoreType.DMA((len(plan),))],
         compiler_params=pltpu.CompilerParams(vmem_limit_bytes=40 * 1024 * 1024),
         cost_estimate=pl.CostEstimate(
-            flops=16 * length * length * width,
+            flops= 64 * 2 * length * length * width,
             transcendentals=length * length * heads,
             bytes_accessed=length * width3 * 4,
         ),
@@ -247,7 +247,7 @@
         ],
         compiler_params=pltpu.CompilerParams(vmem_limit_bytes=48 * 1024 * 1024),
         cost_estimate=pl.CostEstimate(
-            flops=32 * length * length * width,
+            flops= 128 * 2 * length * length * width,
             transcendentals=length * length * heads,
             bytes_accessed=length * width3 * 8,
         ),
@@ -312,48 +312,101 @@
     out[...] = (mm_t(grad, ws[0][...]) + mm(low, a[...])).astype(BF)
 
 
-def mlp_forward_kernel(ws, ins, outs, need):
-    x_refs, (a1,), (b1,), (a2,), (b2,) = ins
-    out, (act_out,), (slope_out,), (rank1_out,), (rank2_out,) = outs
-    x = join(x_refs)
-    rank1 = mm_t(x, a1[...]).astype(BF)
-    rank1_out[...] = rank1
-    low1 = mm(rank1, b1[...])
+def row_tile(rows):
+    for tile in (224, 128, 112, 64, 32, 16):
+        if rows % tile == 0:
+            return tile
+    return rows
+
+
+def column_tiles(cols):
+    tile = 512 if cols % 512 == 0 else cols
+    return [(c, tile) for c in range(0, cols, tile)]
+
+
+def by_rows(rows, step):
+    tile = row_tile(rows)
+
+    def run(i, carry):
+        step(pl.ds(pl.multiple_of(i * tile, 16), tile))
+        return carry
+
+    lax.fori_loop(0, rows // tile, run, 0)
+
+
+def mlp_forward_kernel(ws, ins, outs, need, gathered):
+    (a1,), (b1,), (a2,), (b2,) = ins
+    out, (act_out,), (slope_out,), (rank1_out,), (rank2_out,), (spill,) = outs
+    (xs,) = gathered
+    need(len(ws))
     need(0)
-    hidden = mm(x, ws[0][...]) + low1
-    square = hidden * hidden
-    bend = jnp.tanh(0.7978845608028654 * hidden * (1.0 + 0.044715 * square))
-    half = 0.5 * (1.0 + bend)
-    act = (hidden * half).astype(BF)
-    act_out[...] = act
-    slope = half + 0.5 * hidden * (1.0 - bend * bend) * (
-        0.7978845608028654 * (1.0 + 0.134145 * square)
-    )
-    slope_out[...] = slope.astype(BF)
-    rank2 = mm_t(act, a2[...]).astype(BF)
-    rank2_out[...] = rank2
+
+    def first(here):
+        x = xs[here, :]
+        rank1 = mm_t(x, a1[...]).astype(BF)
+        rank1_out[here, :] = rank1
+        for c, tile in column_tiles(act_out.shape[1]):
+            hidden = mm(x, ws[0][:, c : c + tile]) + mm(rank1, b1[:, c : c + tile])
+            square = hidden * hidden
+            bend = jnp.tanh(hidden * (0.7978845608028654 + 0.035677408136300125 * square))
+            half = 0.5 + 0.5 * bend
+            act_out[here, c : c + tile] = (hidden * half).astype(BF)
+            slope = half + (half * (1.0 - bend)) * hidden * (
+                0.7978845608028654 + 0.10703222440890037 * square
+            )
+            slope_out[here, c : c + tile] = slope.astype(BF)
+
+    by_rows(xs.shape[0], first)
     need(1)
-    split(mm(act, ws[1][...]) + mm(rank2, b2[...]), out)
-
-
-def mlp_backward_kernel(ws, ins, outs, need):
-    g_refs, x_refs, (act,), (slope,), (rank1,), (rank2,), (a1,), (b1,), (a2,), (b2,) = ins
-    out, (t_b1,), (t_a2,), (t_b2,), (t_a1,) = outs
-    grad = join(g_refs)
-    low2 = mm_t(grad, b2[...]).astype(BF)
-    t_b2[...] = t_mm(rank2[...], grad)
-    t_a2[...] = t_mm(low2, act[...])
+
+    def second(here):
+        act = act_out[here, :]
+        rank2 = mm_t(act, a2[...]).astype(BF)
+        rank2_out[here, :] = rank2
+        for c, tile in column_tiles(spill.shape[1]):
+            spill[here, c : c + tile] = (mm(act, ws[1][:, c : c + tile]) + mm(rank2, b2[:, c : c + tile])).astype(BF)
+
+    by_rows(xs.shape[0], second)
+    split(spill, out)
+
+
+def mlp_backward_kernel(ws, ins, outs, need, gathered):
+    (act,), (slope,), (rank1,), (rank2,), (a1,), (b1,), (a2,), (b2,) = ins
+    out, (t_b1,), (t_a2,), (t_b2,), (t_a1,), (spill,) = outs
+    gs, xs = gathered
+    need(len(ws))
     need(1)
-    grad_act = mm_t(grad, ws[1][...]) + mm(low2, a2[...])
-    gh = (grad_act * slope[...].astype(F32)).astype(BF)
-    low1 = mm_t(gh, b1[...]).astype(BF)
-    t_b1[...] = t_mm(rank1[...], gh)
-    t_a1[...] = t_mm(low1, join(x_refs))
+    t_b1[...] = jnp.zeros_like(t_b1)
+    t_a2[...] = jnp.zeros_like(t_a2)
+    t_b2[...] = jnp.zeros_like(t_b2)
+    t_a1[...] = jnp.zeros_like(t_a1)
+
+    def first(here):
+        grad = gs[here, :]
+        low2 = mm_t(grad, b2[...]).astype(BF)
+        t_b2[...] += t_mm(rank2[here, :], grad)
+        t_a2[...] += t_mm(low2, act[here, :])
+        for c, tile in column_tiles(spill.shape[1]):
+            part = mm_t(grad, ws[1][c : c + tile, :]) + mm(low2, a2[:, c : c + tile])
+            spill[here, c : c + tile] = (part * slope[here, c : c + tile].astype(F32)).astype(BF)
+
+    by_rows(gs.shape[0], first)
+    need(len(ws) + 1)
     need(0)
-    split(mm_t(gh, ws[0][...]) + mm(low1, a1[...]), out)
-
-
-def project(kernel, offs, matrices, ins, outs, first):
+
+    def second(here):
+        gh = spill[here, :]
+        low1 = mm_t(gh, b1[...]).astype(BF)
+        t_b1[...] += t_mm(rank1[here, :], gh)
+        t_a1[...] += t_mm(low1, xs[here, :])
+        for c, tile in column_tiles(gs.shape[1]):
+            gs[here, c : c + tile] = (mm_t(gh, ws[0][c : c + tile, :]) + mm(low1, a1[:, c : c + tile])).astype(BF)
+
+    by_rows(gs.shape[0], second)
+    split(gs, out)
+
+
+def project(kernel, offs, matrices, ins, outs, first, blocks=(), spill=None):
     arrays, specs, counts = [], [], []
     for group in ins:
         counts.append(len(group))
@@ -371,6 +424,19 @@
         base = len(sources)
         sources += matrices[m].sources
         plan += [(base + p[0],) + p[1:4] + (m,) + p[4:] for p in matrices[m].plan]
+    scratch = []
+    for i, group in enumerate(blocks):
+        rows, cols = sum(g.shape[0] for g in group), group[0].shape[1]
+        more, row = [], 0
+        for g in group:
+            more.append((len(sources), None, g.shape[0], cols, len(matrices) + i, row, 0, None))
+            sources.append(g)
+            row += g.shape[0]
+        plan = more + plan if i == 0 else plan + more
+        scratch.append(pltpu.VMEM((rows, cols), BF))
+    n_blocks = len(scratch)
+    if spill is not None:
+        scratch.append(pltpu.VMEM(spill, BF))
     shapes = [jax.ShapeDtypeStruct(*o) for group in outs for o in group]
     n_in, n_src, n_out, n_mat = len(arrays), len(sources), len(shapes), len(matrices)
 
@@ -385,12 +451,18 @@
         in_refs, refs = refs[:n_in], refs[n_in:]
         src_refs, refs = refs[:n_src], refs[n_src:]
         out_refs, refs = refs[:n_out], refs[n_out:]
-        w_refs, sems = refs[:n_mat], refs[n_mat]
-        start, wait = copies(offs_ref, plan, src_refs, w_refs, sems)
+        *targets, sems = refs
+        w_refs, gathered = targets[:n_mat], targets[n_mat : n_mat + n_blocks]
+        start, wait = copies(offs_ref, plan, src_refs, targets[: n_mat + n_blocks], sems)
         start()
-        kernel(w_refs, groups(in_refs, counts), groups(out_refs, [len(g) for g in outs]), lambda m: wait([m]))
-
-    flops = sum(4 * outs[0][0][0][0] * len(outs[0]) * m.shape[0] * m.shape[1] for m in matrices)
+        results = groups(out_refs, [len(g) for g in outs])
+        if n_blocks:
+            results.append(targets[n_mat + n_blocks :])
+            kernel(w_refs, groups(in_refs, counts), results, lambda m: wait([m]), gathered)
+        else:
+            kernel(w_refs, groups(in_refs, counts), results, lambda m: wait([m]))
+
+    flops = sum(16 * outs[0][0][0][0] * len(outs[0]) * m.shape[0] * m.shape[1] for m in matrices)
     moved = sum(2 * m.shape[0] * m.shape[1] for m in matrices) + sum(2 * s.size for s in shapes)
     results = pl.pallas_call(
         body,
@@ -398,7 +470,7 @@
         in_specs=[SCALARS] + specs + [ANY] * n_src,
         out_specs=[pl.BlockSpec(s.shape, lambda i: (0, 0)) for s in shapes],
         out_shape=shapes,
-        scratch_shapes=[pltpu.VMEM(m.shape, BF) for m in matrices] + [pltpu.SemaphoreType.DMA((len(plan),))],
+        scratch_shapes=[pltpu.VMEM(m.shape, BF) for m in matrices] + scratch + [pltpu.SemaphoreType.DMA((len(plan),))],
         compiler_params=pltpu.CompilerParams(vmem_limit_bytes=56 * 1024 * 1024),
         cost_estimate=pl.CostEstimate(flops=flops, transcendentals=0, bytes_accessed=moved),
     )(offs, *arrays, *sources)
@@ -792,7 +864,11 @@
         image.n1[1] = due(image.n1[1], a1_qkv, b0_qkv)
         rest = (output_weight, first_feed_weight, second_feed_weight, image_cotangent)
         _, rest = lax.optimization_barrier((image.normed, rest))
-        text.w_out = text_out(rest[0], wh, att_c, att_d)
+        text.w_out = Matrix(
+            (wq, W),
+            [output_weight, queue(LY, xf, rest[0][1], 1)],
+            [(0, 1, wq, rows_d, 0, own, None), (1, None, wq, rows_d, 0, other, None)],
+        )
         text.w_fc1 = text_in(rest[1])
         text.w_fc2 = text_out(rest[2], ffh, half_c, half_d)
         rest = due(rest, image.n1[1])
@@ -969,16 +1045,16 @@
 
     def mlp_forward(s):
         s.saved, partial = [], []
-        for part in s.twice:
+        for part in s.once:
             rows = len(part) * s.size
             out, *saved = project(
                 mlp_forward_kernel, offs, [s.w_fc1, s.w_fc2],
-                [[s.n2[i] for i in part], [s.a_fc1], [s.b_fc1], [s.a_fc2], [s.b_fc2]],
+                [[s.a_fc1], [s.b_fc1], [s.a_fc2], [s.b_fc2]],
                 [
                     blocks_out(s, part), [((rows, ffq), BF)], [((rows, ffq), BF)],
                     [((rows, RANK), BF)], [((rows, RANK), BF)],
                 ],
-                0,
+                0, [[s.n2[i] for i in part]], (rows, W),
             )
             partial += out
             s.saved.append([v[0] for v in saved])
@@ -986,15 +1062,15 @@
 
     def mlp_backward(s):
         partial, sums = [], []
-        for part, (act, slope, rank1, rank2) in zip(s.twice, s.saved):
+        for part, (act, slope, rank1, rank2) in zip(s.once, s.saved):
             out, *more = project(
                 mlp_backward_kernel, offs, [s.w_fc1, s.w_fc2],
                 [
-                    [s.gb_mlp[i] for i in part], [s.n2[i] for i in part], [act], [slope], [rank1], [rank2],
+                    [act], [slope], [rank1], [rank2],
                     [s.a_fc1], [s.b_fc1], [s.a_fc2], [s.b_fc2],
                 ],
                 [blocks_out(s, part)] + [[((RANK, n), F32)] for n in (ffq, ffq, W, W)],
-                1,
+                1, [[s.gb_mlp[i] for i in part], [s.n2[i] for i in part]], (len(part) * s.size, ffq),
             )
             partial += out
             sums.append([m[0] for m in more])
@@ -1032,9 +1108,10 @@
         return partial
 
     text.n1 = [due(text.normed, image.normed)]
-    qkv_forward(text)
     bulk(0, image.n1[1])
     qkv_forward(image)
+    text.n1[0] = due(text.n1[0], image.joint[0])
+    qkv_forward(text)
     arrived = bulk(1, image.joint[0])
     joints = [(j, None) for j in image.joint] + [(text.joint[0], 1), (swap(text.joint[0]), 0)]
     joints[0] = (due(joints[0][0], *arrived), None)
@@ -1074,13 +1151,13 @@
     txt_grad = swap(text.g_att[0])
     image.gb_mlp[0] = due(image.gb_mlp[0], txt_grad)
     img_partial = mlp_backward(image)
-    gn2, sent = scatter_image(img_partial, image.twice)
+    gn2, sent = scatter_image(img_partial, image.once)
 
     gb = second_norm_back(image, gn2)
     gb_img = gather_group(gb)
     out_backward(image, gb_img)
-    img_done, txt_done = due((img_done, txt_done), image.g_att)
-    image.br_mlp, _ = scatter_image(img_done, image.twice)
+    img_done, txt_done = due((img_done, txt_done), gb_img[0])
+    image.br_mlp, _ = scatter_image(img_done, image.once)
     text.br_mlp = lax.psum_scatter(txt_done[0], "tp", scatter_dimension=0, tiled=True).astype(F32)
     for s in streams:
         s.out = ((own_part(s, s.after) + s.mod[5:6] * s.br_mlp) * s.live).astype(BF)

time: 755 us -> 722 us (0.956)
  starting transfers between devices: 217 us -> 185 us
  Pallas kernels: 169 us -> 161 us
    ppermute x34 -> x33, starting transfers between devices: 91.8 us -> 66.9 us  [xr(): return lax.ppermute(v, 'rep', [(i, i ^ bit) for i in range(R)])]
    ppermute x41, waiting for transfers between devices: 181 us -> 162 us  [xz(): return lax.ppermute(v, 'tp', [(i, i ^ bit) for i in range(T)])]
    ppermute x14, waiting for transfers between devices: 5.59 us -> 18.9 us  [xf(): return lax.ppermute(v, 'fsdp', [(i, i ^ bit) for i in range(F)])]
    pallas_call x16 -> x14, Pallas kernels: 129 us -> 120 us  [project(): pl.pallas_call(body, grid=(1,), in_specs=[SCALARS] + specs + [ANY] * n_sr...]
  transfers between devices with their start and end apart: 112 -> 111, of which waited for: 33 -> 35; matrix products, arithmetic and copies ran while one was open for 16% -> 19% of each run, Pallas kernels for 22% -> 23%
where the time goes in v2:
time: 722 us; the launch traced here: 713 us
  waiting for transfers between devices  190 us (26%)
  starting transfers between devices  185 us (26%)
  Pallas kernels  161 us (22%)
  other arithmetic  81.2 us (11%)
  local copies, waits for them, and re-layouts  53.5 us (7%)
  between operations  21.2 us (3%)
  matrix products  20.5 us (3%)
    ppermute x41, waiting for transfers between devices, xz(): return lax.ppermute(v, 'tp', [(i, i ^ bit) for i in range(T)])  162 us
    pallas_call x14, Pallas kernels, project(): pl.pallas_call(body, grid=(1,), in_specs=[SCALARS] + specs + [ANY] * n_sr...  120 us
    ppermute x41, starting transfers between devices, xz(): return lax.ppermute(v, 'tp', [(i, i ^ bit) for i in range(T)])  78.9 us
    ppermute x33, starting transfers between devices, xr(): return lax.ppermute(v, 'rep', [(i, i ^ bit) for i in range(R)])  66.9 us
    pallas_call x1, Pallas kernels, attend_backward(): pl.pallas_call(functools.partial(attend_backward_kernel, width, blocks, p...  26.3 us
    ppermute x18, starting transfers between devices, swap(): return lax.ppermute(v, ('rep', 'tp'), swap_pairs)  19.8 us
    ppermute x14, waiting for transfers between devices, xf(): return lax.ppermute(v, 'fsdp', [(i, i ^ bit) for i in range(F)])  18.9 us
    ppermute x14, starting transfers between devices, xf(): return lax.ppermute(v, 'fsdp', [(i, i ^ bit) for i in range(F)])  15.1 us
  transfers between devices with their start and end apart: 111, of which 35 were waited for; matrix products, arithmetic and copies ran while one was open for 19% of the time, Pallas kernels for 23%

profile of v2, /device:TPU:0, one launch (start us, length us, event | category | flops | bytes accessed | tf_op | source)
XLA Modules:
  0.0 712.5 jit_solution(13661685780482314952)
XLA Ops:
  50.4 5.3 collective-permute-done.5.refs_4_.refs_6_
  71.7 5.5 collective-permute-start.8
  77.2 6.4 collective-permute-done.23
  86.4 17.6 %collective-permute-done.24 = bf16[2,64,1536]{2,1,0:T(8,128)(2,1)S(1)} collective-permute-done((bf16[2,64,1536]{2,1,0:T(8,128)(2,1)S(1)}, bf16[2,64,1536]{2,1,0:T(8,128)(2,1)S(1)}, u32[]{:S(2)}, u32[]{:S(2)}) %collective-permute-start.24) | collective-permute-done | bytes 393248 | tf_op jit(solution)/shard_map/ppermute | solution.py:531
  118.8 7.7 %collective-permute-done.12 = bf16[2,16,6144]{2,1,0:T(8,128)(2,1)S(1)} collective-permute-done((bf16[2,16,6144]{2,1,0:T(8,128)(2,1)S(1)}, bf16[2,16,6144]{2,1,0:T(8,128)(2,1)S(1)}, u32[]{:S(2)}, u32[]{:S(2)}) %collective-permute-start.12) | collective-permute-done | bytes 393248 | tf_op jit(solution)/shard_map/ppermute | solution.py:531
  130.2 16.4 %collective-permute-done.13 = bf16[2,16,6144]{2,1,0:T(8,128)(2,1)S(1)} collective-permute-done((bf16[2,16,6144]{2,1,0:T(8,128)(2,1)S(1)}, bf16[2,16,6144]{2,1,0:T(8,128)(2,1)S(1)}, u32[]{:S(2)}, u32[]{:S(2)}) %collective-permute-start.13) | collective-permute-done | bytes 393248 | tf_op jit(solution)/shard_map/ppermute | solution.py:531
  159.8 8.4 %collective-permute-done.28.refs_4_.refs_6_ = bf16[384,768]{1,0:T(8,128)(2,1)S(1)} collective-permute-done((bf16[384,768]{1,0:T(8,128)(2,1)S(1)}, bf16[384,768]{1,0:T(8,128)(2,1)S(1)}, u32[]{:S(2)}, u32[]{:S(2)}) %collective-permute-start.28) | collective-permute-done | bytes 589856 | tf_op jit(solution)/shard_map/ppermute | solution.py:534
  171.8 5.9 collective-permute-done.18.refs_8_.refs_13_
  178.6 6.9 shard_map.274
  191.7 6.9 shard_map.275
  201.3 7.7 %collective-permute-start.41 = (bf16[384,1536]{1,0:T(8,128)(2,1)}, bf16[384,1536]{1,0:T(8,128)(2,1)}, u32[]{:S(2)}, u32[]{:S(2)}) collective-permute-start(bf16[384,1536]{1,0:T(8,128)(2,1)} %collective-permute-done.29.refs_5_.refs_12_), channel_id=1, source_target_pairs={{0,8},{8,0},{16,24},{24,16},{1,9},{9,1},{17,25},{25,17},{2,10},{10... | collective-permute-start | bytes 3538952 | tf_op jit(solution)/shard_map/ppermute | solution.py:537
  209.7 13.9 %attend_forward.1 = (bf16[1024,384]{1,0:T(8,128)(2,1)S(1)}, f32[1024,6]{1,0:T(8,128)S(1)}) custom-call(s32[15]{0:T(128)S(1)} %copy-done.1, bf16[448,1152]{1,0:T(8,128)(2,1)S(1)} %copy-done.13, bf16[448,1152]{1,0:T(8,128)(2,1)S(1)} %copy-done.15, bf16[128,1152]{1,0:T(8,128)(2,1)S(1)} %copy-done.3, bf16[128,1152]{1,0:T(8,128)(2,1)S(1)} %collective-permute-done.26.refs_3_), custom_call_target="tpu_custom_call" | custom-call | flops 51539607552 | bytes 4718592 | tf_op jit(solution)/shard_map/attend_forward/pallas_call | solution.py:203
  233.7 10.3 %collective-permute-start.42 = (bf16[768,768]{1,0:T(8,128)(2,1)}, bf16[768,768]{1,0:T(8,128)(2,1)}, u32[]{:S(2)}, u32[]{:S(2)}) collective-permute-start(bf16[768,768]{1,0:T(8,128)(2,1)} %collective-permute-done.30.refs_8_.refs_9_), channel_id=1, source_target_pairs={{0,8},{8,0},{16,24},{24,16},{1,9},{9,1},{17,25},{25,17},{2,10},{10... | collective-permute-start | bytes 3538952 | tf_op jit(solution)/shard_map/ppermute | solution.py:537
  244.2 14.1 %collective-permute-start.45 = (bf16[128,1536]{1,0:T(8,128)(2,1)S(1)}, bf16[128,1536]{1,0:T(8,128)(2,1)S(1)}, u32[]{:S(2)}, u32[]{:S(2)}) collective-permute-start(bf16[128,1536]{1,0:T(8,128)(2,1)S(1)} %add.497), channel_id=1, source_target_pairs={{0,2},{1,3},{2,0},{3,1},{4,6},{5,7},{6,4},{7,5},{8,10},{9,11},{10,... | collective-permute-start | bytes 1179656 | tf_op jit(solution)/shard_map/ppermute | solution.py:531
  259.1 6.3 shard_map.277
  265.3 14.7 %collective-permute-done.45 = bf16[128,1536]{1,0:T(8,128)(2,1)S(1)} collective-permute-done((bf16[128,1536]{1,0:T(8,128)(2,1)S(1)}, bf16[128,1536]{1,0:T(8,128)(2,1)S(1)}, u32[]{:S(2)}, u32[]{:S(2)}) %collective-permute-start.45) | collective-permute-done | bytes 393248 | tf_op jit(solution)/shard_map/ppermute | solution.py:531
  282.2 7.0 shard_map.279
  289.3 8.4 %shard_map.280 = (bf16[128,1536]{1,0:T(8,128)(2,1)}, f32[16,1536]{1,0:T(8,128)}, f32[16,1536]{1,0:T(8,128)}, f32[16,1536]{1,0:T(8,128)}, f32[16,1536]{1,0:T(8,128)}) custom-call(s32[15]{0:T(128)} %stack.229.offs_ref.offs, bf16[128,1536]{1,0:T(8,128)(2,1)} %get-tuple-element.206.refs_0_, bf16[128,1536]{1,0:T(8,128)(2,1)} %get-tuple-element.207.refs_1_, ...), custom_call_target="tpu_custom_call" | custom-call | flops 9663676416 | bytes 10027008 | tf_op jit(solution)/shard_map/pallas_call | solution.py:467
  303.3 6.6 collective-permute-done.50
  311.5 20.7 %collective-permute-done.34 = bf16[224,1536]{1,0:T(8,128)(2,1)S(1)} collective-permute-done((bf16[224,1536]{1,0:T(8,128)(2,1)S(1)}, bf16[224,1536]{1,0:T(8,128)(2,1)S(1)}, u32[]{:S(2)}, u32[]{:S(2)}) %collective-permute-start.34) | collective-permute-done | bytes 688160 | tf_op jit(solution)/shard_map/ppermute | solution.py:531
  351.7 6.5 collective-permute-done.47.refs_16_.refs_24_
  372.9 5.8 collective-permute-start.53
  382.1 23.1 %shard_map.281 = (bf16[224,1536]{1,0:T(8,128)(2,1)}, bf16[224,1536]{1,0:T(8,128)(2,1)}, bf16[224,1536]{1,0:T(8,128)(2,1)}, bf16[224,1536]{1,0:T(8,128)(2,1)}, bf...) custom-call(s32[15]{0:T(128)} %stack.229.offs_ref.offs, ...), custom_call_target="tpu_custom_call" | custom-call | flops 67645734912 | bytes 17752064 | tf_op jit(solution)/shard_map/pallas_call | solution.py:467
  406.4 25.3 %shard_map.283 = (bf16[224,1536]{1,0:T(8,128)(2,1)}, bf16[224,1536]{1,0:T(8,128)(2,1)}, bf16[224,1536]{1,0:T(8,128)(2,1)}, bf16[224,1536]{1,0:T(8,128)(2,1)}, f3...) custom-call(s32[15]{0:T(128)} %stack.229.offs_ref.offs, ...), custom_call_target="tpu_custom_call" | custom-call | flops 67645734912 | bytes 12386304 | tf_op jit(solution)/shard_map/pallas_call | solution.py:467
  447.6 10.6 %collective-permute-done.58 = bf16[224,1536]{1,0:T(8,128)(2,1)} collective-permute-done((bf16[224,1536]{1,0:T(8,128)(2,1)}, bf16[224,1536]{1,0:T(8,128)(2,1)}, u32[]{:S(2)}, u32[]{:S(2)}) %collective-permute-start.58) | collective-permute-done | bytes 688160 | tf_op jit(solution)/shard_map/ppermute | solution.py:531
  477.9 14.9 %collective-permute-done.64.refs_0_ = bf16[224,1536]{1,0:T(8,128)(2,1)} collective-permute-done((bf16[224,1536]{1,0:T(8,128)(2,1)S(1)}, bf16[224,1536]{1,0:T(8,128)(2,1)}, u32[]{:S(2)}, u32[]{:S(2)}) %collective-permute-start.64) | collective-permute-done | bytes 688160 | tf_op jit(solution)/shard_map/ppermute | solution.py:531
  499.2 7.6 %collective-permute-done.61 = bf16[224,1536]{1,0:T(8,128)(2,1)} collective-permute-done((bf16[224,1536]{1,0:T(8,128)(2,1)}, bf16[224,1536]{1,0:T(8,128)(2,1)}, u32[]{:S(2)}, u32[]{:S(2)}) %collective-permute-start.61) | collective-permute-done | bytes 688160 | tf_op jit(solution)/shard_map/ppermute | solution.py:531
  516.5 26.3 %attend_backward.1.refs_0_ = bf16[1024,1152]{1,0:T(8,128)(2,1)} custom-call(s32[15]{0:T(128)S(1)} %copy-done.2, f32[1024,6]{1,0:T(8,128)S(1)} %get-tuple-element.238.lse_ref, bf16[448,1152]{1,0:T(8,128)(2,1)S(1)} %copy-done.14, bf16[448,1152]{1,0:T(8,128)(2,1)S(1)} %copy-done.16, bf16[128,1152]{1,0:T(8,128)(2,1)S(1)} %copy-done.4, ...), custom_call_target="tpu_custom_call" | custom-call | flops 103079215104 | bytes 9437184 | tf_op jit(solution)/shard_map/attend_backward/pallas_call | solution.py:235
  544.6 10.4 %shard_map.286 = (bf16[224,1536]{1,0:T(8,128)(2,1)}, bf16[224,1536]{1,0:T(8,128)(2,1)}, bf16[224,1536]{1,0:T(8,128)(2,1)}, bf16[224,1536]{1,0:T(8,128)(2,1)}, f32[16,1152]{1,0:T(8,128)}, /*index=5*/f32[16,1536]{1,0:T(8,128)}) custom-call(s32[15]{0:T(128)} %stack.229.offs_ref.offs, bf16[1024,1152]{1,0:T(8,128)(2,1)} %attend_backward.1.refs_0_, ...), custom_call_target="tpu_custom_call" | custom-call | flops 25367150592 | bytes 6377472 | tf_op jit(solution)/shard_map/pallas_call | solution.py:467
  589.5 5.2 shard_map.287
  595.7 8.5 %collective-permute-start.99 = (bf16[16,768]{1,0:T(8,128)(2,1)S(1)}, bf16[16,768]{1,0:T(8,128)(2,1)S(1)}, u32[]{:S(2)}, u32[]{:S(2)}) collective-permute-start(bf16[16,768]{1,0:T(8,128)(2,1)S(1)} %broadcast_select_fusion.21), channel_id=1, source_target_pairs={{0,2},{1,3},{2,0},{3,1},{4,6},{5,7},{6,4},{7,5},{8,10},{9,11},{10,... | collective-permute-start | bytes 73736 | tf_op jit(solution)/shard_map/ppermute | solution.py:531
  606.4 6.9 collective-permute-start.100
  (806 shorter events, 343.1 us)
Async XLA Ops:
  8.0 489.4 %reduce-scatter.2.cloned.1.call-start = ((), (), s32[]{:S(2)}) async-start(), calls=%async_computation.1 | async-start | bytes 491520 | tf_op jit(solution)/shard_map/reduce_scatter | solution.py:1161
  16.0 26.8 %collective-permute-start = (bf16[3,384,384]{2,1,0:T(8,128)(2,1)}, bf16[3,384,384]{2,1,0:T(8,128)(2,1)}, u32[]{:S(2)}, u32[]{:S(2)}) collective-permute-start(bf16[3,384,384]{2,1,0:T(8,128)(2,1)} %dynamic-slice_bitcast_fusion.5), channel_id=1, source_target_pairs={{2,8},{3,9},{8,2},{9,3},{18,24},{19,25},{24,18},{25,19},{6,12},{7,... | collective-permute-start | bytes 2654216 | tf_op jit(solution)/shard_map/ppermute | solution.py:547
  59.3 46.9 %collective-permute-start.4 = (bf16[224,1536]{1,0:T(8,128)(2,1)}, bf16[224,1536]{1,0:T(8,128)(2,1)}, u32[]{:S(2)}, u32[]{:S(2)}) collective-permute-start(bf16[224,1536]{1,0:T(8,128)(2,1)} %bitcast.339), channel_id=1, source_target_pairs={{2,8},{3,9},{8,2},{9,3},{18,24},{19,25},{24,18},{25,19},{6,12},{7,... | collective-permute-start | bytes 2064392 | tf_op jit(solution)/shard_map/ppermute | solution.py:547
  60.9 124.7 %collective-permute-start.25 = (bf16[3,384,384]{2,1,0:T(8,128)(2,1)}, bf16[3,384,384]{2,1,0:T(8,128)(2,1)}, u32[]{:S(2)}, u32[]{:S(2)}) collective-permute-start(bf16[3,384,384]{2,1,0:T(8,128)(2,1)} %collective-permute-done.5.refs_4_.refs_6_), channel_id=1, source_target_pairs={{0,8},{8,0},{16,24},{24,16},{1,9},{9,1},{17,25},{25,17},{2,10},{10... | collective-permute-start | bytes 2654216 | tf_op jit(solution)/shard_map/ppermute | solution.py:537
  66.2 81.9 %collective-permute-start.16 = (bf16[3,384,384]{2,1,0:T(8,128)(2,1)}, bf16[3,384,384]{2,1,0:T(8,128)(2,1)}, u32[]{:S(2)}, u32[]{:S(2)}) collective-permute-start(bf16[3,384,384]{2,1,0:T(8,128)(2,1)} %collective-permute-done.refs_5_.refs_10_), channel_id=1, source_target_pairs={{2,18},{3,19},{8,24},{9,25},{18,2},{19,3},{24,8},{25,9},{6,22},{7,... | collective-permute-start | bytes 2654216 | tf_op jit(solution)/shard_map/ppermute | solution.py:550
  83.8 27.4 %collective-permute-start.11 = (bf16[2,16,10752]{2,1,0:T(8,128)(2,1)}, bf16[2,16,10752]{2,1,0:T(8,128)(2,1)}, u32[]{:S(2)}, u32[]{:S(2)}) collective-permute-start(bf16[2,16,10752]{2,1,0:T(8,128)(2,1)} %pad_maximum_fusion.6), channel_id=1, source_target_pairs={{0,4},{4,0},{1,5},{5,1},{2,6},{6,2},{3,7},{7,3},{8,12},{12,8},{9,1... | collective-permute-start | bytes 2064392 | tf_op jit(solution)/shard_map/ppermute | solution.py:534
  114.6 32.8 %collective-permute-start.17 = (bf16[3,384,384]{2,1,0:T(8,128)(2,1)S(1)}, bf16[3,384,384]{2,1,0:T(8,128)(2,1)S(1)}, u32[]{:S(2)}, u32[]{:S(2)}) collective-permute-start(bf16[3,384,384]{2,1,0:T(8,128)(2,1)S(1)} %copy-done.33), channel_id=1, source_target_pairs={{0,4},{4,0},{1,5},{5,1},{2,6},{6,2},{3,7},{7,3},{8,12},{12,8},{9,1... | collective-permute-start | bytes 2654216 | tf_op jit(solution)/shard_map/ppermute | solution.py:534
  116.8 36.1 %collective-permute-start.19 = (bf16[224,1536]{1,0:T(8,128)(2,1)S(1)}, bf16[224,1536]{1,0:T(8,128)(2,1)}, u32[]{:S(2)}, u32[]{:S(2)}) collective-permute-start(bf16[224,1536]{1,0:T(8,128)(2,1)S(1)} %fusion.19.refs_0_.refs_1_), channel_id=1, source_target_pairs={{0,1},{1,0},{2,3},{3,2},{4,5},{5,4},{6,7},{7,6},{8,9},{9,8},{10,11... | collective-permute-start | bytes 2064392 | tf_op jit(solution)/shard_map/ppermute | solution.py:531
  168.2 33.0 %collective-permute-start.29 = (bf16[384,1536]{1,0:T(8,128)(2,1)}, bf16[384,1536]{1,0:T(8,128)(2,1)}, u32[]{:S(2)}, u32[]{:S(2)}) collective-permute-start(bf16[384,1536]{1,0:T(8,128)(2,1)} %dynamic-slice_bitcast_fusion.2), channel_id=1, source_target_pairs={{0,4},{4,0},{1,5},{5,1},{2,6},{6,2},{3,7},{7,3},{8,12},{12,8},{9,1... | collective-permute-start | bytes 3538952 | tf_op jit(solution)/shard_map/ppermute | solution.py:534
  169.9 39.1 %collective-permute-start.21 = (bf16[384,1536]{1,0:T(8,128)(2,1)}, bf16[384,1536]{1,0:T(8,128)(2,1)}, u32[]{:S(2)}, u32[]{:S(2)}) collective-permute-start(bf16[384,1536]{1,0:T(8,128)(2,1)} %dynamic-slice_bitcast_fusion.3), channel_id=1, source_target_pairs={{2,8},{3,9},{8,2},{9,3},{18,24},{19,25},{24,18},{25,19},{6,12},{7,... | collective-permute-start | bytes 3538952 | tf_op jit(solution)/shard_map/ppermute | solution.py:547
  201.3 80.4 %collective-permute-start.41 = (bf16[384,1536]{1,0:T(8,128)(2,1)}, bf16[384,1536]{1,0:T(8,128)(2,1)}, u32[]{:S(2)}, u32[]{:S(2)}) collective-permute-start(bf16[384,1536]{1,0:T(8,128)(2,1)} %collective-permute-done.29.refs_5_.refs_12_), channel_id=1, source_target_pairs={{0,8},{8,0},{16,24},{24,16},{1,9},{9,1},{17,25},{25,17},{2,10},{10... | collective-permute-start | bytes 3538952 | tf_op jit(solution)/shard_map/ppermute | solution.py:537
  224.5 76.2 %collective-permute-start.36 = (bf16[768,768]{1,0:T(8,128)(2,1)}, bf16[768,768]{1,0:T(8,128)(2,1)}, u32[]{:S(2)}, u32[]{:S(2)}) collective-permute-start(bf16[768,768]{1,0:T(8,128)(2,1)} %dynamic-slice_bitcast_fusion), channel_id=1, source_target_pairs={{2,8},{3,9},{8,2},{9,3},{18,24},{19,25},{24,18},{25,19},{6,12},{7,... | collective-permute-start | bytes 3538952 | tf_op jit(solution)/shard_map/ppermute | solution.py:547
  226.4 31.9 %collective-permute-start.31 = (bf16[384,768]{1,0:T(8,128)(2,1)S(1)}, bf16[384,768]{1,0:T(8,128)(2,1)S(1)}, u32[]{:S(2)}, u32[]{:S(2)}) collective-permute-start(bf16[384,768]{1,0:T(8,128)(2,1)S(1)} %broadcast_select_fusion.6), channel_id=1, source_target_pairs={{0,4},{4,0},{1,5},{5,1},{2,6},{6,2},{3,7},{7,3},{8,12},{12,8},{9,1... | collective-permute-start | bytes 1769480 | tf_op jit(solution)/shard_map/ppermute | solution.py:534
  233.7 48.5 %collective-permute-start.42 = (bf16[768,768]{1,0:T(8,128)(2,1)}, bf16[768,768]{1,0:T(8,128)(2,1)}, u32[]{:S(2)}, u32[]{:S(2)}) collective-permute-start(bf16[768,768]{1,0:T(8,128)(2,1)} %collective-permute-done.30.refs_8_.refs_9_), channel_id=1, source_target_pairs={{0,8},{8,0},{16,24},{24,16},{1,9},{9,1},{17,25},{25,17},{2,10},{10... | collective-permute-start | bytes 3538952 | tf_op jit(solution)/shard_map/ppermute | solution.py:537
  244.2 35.9 %collective-permute-start.45 = (bf16[128,1536]{1,0:T(8,128)(2,1)S(1)}, bf16[128,1536]{1,0:T(8,128)(2,1)S(1)}, u32[]{:S(2)}, u32[]{:S(2)}) collective-permute-start(bf16[128,1536]{1,0:T(8,128)(2,1)S(1)} %add.497), channel_id=1, source_target_pairs={{0,2},{1,3},{2,0},{3,1},{4,6},{5,7},{6,4},{7,5},{8,10},{9,11},{10,... | collective-permute-start | bytes 1179656 | tf_op jit(solution)/shard_map/ppermute | solution.py:531
  258.2 52.1 %collective-permute-start.35 = (bf16[384,1536]{1,0:T(8,128)(2,1)S(1)}, bf16[384,1536]{1,0:T(8,128)(2,1)}, u32[]{:S(2)}, u32[]{:S(2)}) collective-permute-start(bf16[384,1536]{1,0:T(8,128)(2,1)S(1)} %broadcast_select_fusion.1), channel_id=1, source_target_pairs={{0,4},{4,0},{1,5},{5,1},{2,6},{6,2},{3,7},{7,3},{8,12},{12,8},{9,1... | collective-permute-start | bytes 3538952 | tf_op jit(solution)/shard_map/ppermute | solution.py:534
  280.0 31.5 %collective-permute-start.32 = (bf16[224,1536]{1,0:T(8,128)(2,1)}, bf16[224,1536]{1,0:T(8,128)(2,1)S(1)}, u32[]{:S(2)}, u32[]{:S(2)}) collective-permute-start(bf16[224,1536]{1,0:T(8,128)(2,1)} %get-tuple-element.190), channel_id=1, source_target_pairs={{0,8},{8,0},{16,24},{24,16},{1,9},{9,1},{17,25},{25,17},{2,10},{10... | collective-permute-start | bytes 2064392 | tf_op jit(solution)/shard_map/ppermute | solution.py:537
  298.0 34.2 %collective-permute-start.34 = (bf16[224,1536]{1,0:T(8,128)(2,1)S(1)}, bf16[224,1536]{1,0:T(8,128)(2,1)S(1)}, u32[]{:S(2)}, u32[]{:S(2)}) collective-permute-start(bf16[224,1536]{1,0:T(8,128)(2,1)S(1)} %add_convert_fusion.4), channel_id=1, source_target_pairs={{0,1},{1,0},{2,3},{3,2},{4,5},{5,4},{6,7},{7,6},{8,9},{9,8},{10,11... | collective-permute-start | bytes 2064392 | tf_op jit(solution)/shard_map/ppermute | solution.py:531
  310.3 27.5 %collective-permute-start.37 = (bf16[384,1536]{1,0:T(8,128)(2,1)}, bf16[384,1536]{1,0:T(8,128)(2,1)S(1)}, u32[]{:S(2)}, u32[]{:S(2)}) collective-permute-start(bf16[384,1536]{1,0:T(8,128)(2,1)} %collective-permute-done.35.refs_7_.refs_16_), channel_id=1, source_target_pairs={{0,16},{8,24},{16,0},{24,8},{1,17},{9,25},{17,1},{25,9},{2,18},{10... | collective-permute-start | bytes 3538952 | tf_op jit(solution)/shard_map/ppermute | solution.py:537
  310.9 34.9 %collective-permute-start.39 = (bf16[768,768]{1,0:T(8,128)(2,1)}, bf16[768,768]{1,0:T(8,128)(2,1)}, u32[]{:S(2)}, u32[]{:S(2)}) collective-permute-start(bf16[768,768]{1,0:T(8,128)(2,1)} %broadcast_select_fusion), channel_id=1, source_target_pairs={{0,4},{4,0},{1,5},{5,1},{2,6},{6,2},{3,7},{7,3},{8,12},{12,8},{9,1... | collective-permute-start | bytes 3538952 | tf_op jit(solution)/shard_map/ppermute | solution.py:534
  333.4 47.7 %collective-permute-start.46 = (bf16[224,1536]{1,0:T(8,128)(2,1)S(1)}, bf16[224,1536]{1,0:T(8,128)(2,1)}, u32[]{:S(2)}, u32[]{:S(2)}) collective-permute-start(bf16[224,1536]{1,0:T(8,128)(2,1)S(1)} %add_convert_fusion.3.refs_14_.refs_22_), channel_id=1, source_target_pairs={{0,8},{8,0},{16,24},{24,16},{1,9},{9,1},{17,25},{25,17},{2,10},{10... | collective-permute-start | bytes 2064392 | tf_op jit(solution)/shard_map/ppermute | solution.py:537
  348.0 30.7 %collective-permute-start.40 = (bf16[768,768]{1,0:T(8,128)(2,1)}, bf16[768,768]{1,0:T(8,128)(2,1)S(1)}, u32[]{:S(2)}, u32[]{:S(2)}) collective-permute-start(bf16[768,768]{1,0:T(8,128)(2,1)} %collective-permute-done.39.refs_12_.refs_11_), channel_id=1, source_target_pairs={{0,16},{8,24},{16,0},{24,8},{1,17},{9,25},{17,1},{25,9},{2,18},{10... | collective-permute-start | bytes 3538952 | tf_op jit(solution)/shard_map/ppermute | solution.py:537
  366.6 65.9 %collective-permute-start.94 = (bf16[48,384]{1,0:T(8,128)(2,1)S(1)}, bf16[48,384]{1,0:T(8,128)(2,1)S(1)}, u32[]{:S(2)}, u32[]{:S(2)}) collective-permute-start(bf16[48,384]{1,0:T(8,128)(2,1)S(1)} %broadcast_select_fusion.18), channel_id=1, source_target_pairs={{0,1},{1,0},{2,3},{3,2},{4,5},{5,4},{6,7},{7,6},{8,9},{9,8},{10,11... | collective-permute-start | bytes 110600 | tf_op jit(solution)/shard_map/ppermute | solution.py:531
  372.9 32.4 %collective-permute-start.53 = (bf16[224,1536]{1,0:T(8,128)(2,1)S(1)}, bf16[224,1536]{1,0:T(8,128)(2,1)S(1)}, u32[]{:S(2)}, u32[]{:S(2)}) collective-permute-start(bf16[224,1536]{1,0:T(8,128)(2,1)S(1)} %get-tuple-element.228.refs_18_), channel_id=1, source_target_pairs={{0,8},{8,0},{16,24},{24,16},{1,9},{9,1},{17,25},{25,17},{2,10},{10... | collective-permute-start | bytes 2064392 | tf_op jit(solution)/shard_map/ppermute | solution.py:537
  381.1 50.7 %collective-permute-start.73 = (f32[1,2,1664]{2,1,0:T(2,128)S(1)}, f32[1,2,1664]{2,1,0:T(2,128)S(1)}, u32[]{:S(2)}, u32[]{:S(2)}) collective-permute-start(f32[1,2,1664]{2,1,0:T(2,128)S(1)} %bitcast.347), channel_id=1, source_target_pairs={{0,8},{8,0},{16,24},{24,16},{1,9},{9,1},{17,25},{25,17},{2,10},{10... | collective-permute-start | bytes 39944 | tf_op jit(solution)/shard_map/ppermute | solution.py:537
  469.9 219.8 %all-gather.3.cloned.1.call-start = ((), (), s32[]{:S(2)}) async-start(), calls=%async_computation.2 | async-start | bytes 2654208 | tf_op jit(solution)/shard_map/all_gather | solution.py:1200
  469.9 29.3 %collective-permute-start.59 = (bf16[224,1536]{1,0:T(8,128)(2,1)}, bf16[224,1536]{1,0:T(8,128)(2,1)}, u32[]{:S(2)}, u32[]{:S(2)}) collective-permute-start(bf16[224,1536]{1,0:T(8,128)(2,1)} %get-tuple-element.234), channel_id=1, source_target_pairs={{0,8},{8,0},{16,24},{24,16},{1,9},{9,1},{17,25},{25,17},{2,10},{10... | collective-permute-start | bytes 2064392 | tf_op jit(solution)/shard_map/ppermute | solution.py:537
  472.6 34.2 %collective-permute-start.61 = (bf16[224,1536]{1,0:T(8,128)(2,1)}, bf16[224,1536]{1,0:T(8,128)(2,1)}, u32[]{:S(2)}, u32[]{:S(2)}) collective-permute-start(bf16[224,1536]{1,0:T(8,128)(2,1)} %add_convert_fusion.1), channel_id=1, source_target_pairs={{0,1},{1,0},{2,3},{3,2},{4,5},{5,4},{6,7},{7,6},{8,9},{9,8},{10,11... | collective-permute-start | bytes 2064392 | tf_op jit(solution)/shard_map/ppermute | solution.py:531
  509.1 96.3 %collective-permute-start.62 = (bf16[224,1536]{1,0:T(8,128)(2,1)S(1)}, bf16[224,1536]{1,0:T(8,128)(2,1)}, u32[]{:S(2)}, u32[]{:S(2)}) collective-permute-start(bf16[224,1536]{1,0:T(8,128)(2,1)S(1)} %multiply_convert_fusion), channel_id=1, source_target_pairs={{2,8},{3,9},{8,2},{9,3},{18,24},{19,25},{24,18},{25,19},{6,12},{7,... | collective-permute-start | bytes 2064392 | tf_op jit(solution)/shard_map/ppermute | solution.py:547
  567.5 65.7 %collective-permute-start.66 = (bf16[224,1536]{1,0:T(8,128)(2,1)}, bf16[224,1536]{1,0:T(8,128)(2,1)S(1)}, u32[]{:S(2)}, u32[]{:S(2)}) collective-permute-start(bf16[224,1536]{1,0:T(8,128)(2,1)} %get-tuple-element.246), channel_id=1, source_target_pairs={{0,8},{8,0},{16,24},{24,16},{1,9},{9,1},{17,25},{25,17},{2,10},{10... | collective-permute-start | bytes 2064392 | tf_op jit(solution)/shard_map/ppermute | solution.py:537
  588.8 44.4 %collective-permute-start.68 = (bf16[224,1536]{1,0:T(8,128)(2,1)S(1)}, bf16[224,1536]{1,0:T(8,128)(2,1)S(1)}, u32[]{:S(2)}, u32[]{:S(2)}) collective-permute-start(bf16[224,1536]{1,0:T(8,128)(2,1)S(1)} %add_convert_fusion), channel_id=1, source_target_pairs={{0,1},{1,0},{2,3},{3,2},{4,5},{5,4},{6,7},{7,6},{8,9},{9,8},{10,11... | collective-permute-start | bytes 2064392 | tf_op jit(solution)/shard_map/ppermute | solution.py:531
  645.5 42.1 %collective-permute-start.69 = (bf16[224,1536]{1,0:T(8,128)(2,1)}, bf16[224,1536]{1,0:T(8,128)(2,1)S(1)}, u32[]{:S(2)}, u32[]{:S(2)}) collective-permute-start(bf16[224,1536]{1,0:T(8,128)(2,1)} %fusion.24), channel_id=1, source_target_pairs={{2,8},{3,9},{8,2},{9,3},{18,24},{19,25},{24,18},{25,19},{6,12},{7,... | collective-permute-start | bytes 2064392 | tf_op jit(solution)/shard_map/ppermute | solution.py:547
  (214 other events, 2515.6 us)
Sparse Core Ops, SparseCore 0:
  470.0 20.7 reduce-scatter.1
Sparse Core Ops, SparseCore 1:
  585.0 34.4 all-gather.2

commit v3 on v2

--- a/solution.py
+++ b/solution.py
@@ -179,7 +179,7 @@
 
 
 def query_block(length):
-    for rows in (256, 128, 64, 32, 16):
+    for rows in (512, 256, 128, 64, 32, 16):
         if length % rows == 0:
             return rows
     return length
@@ -313,7 +313,7 @@
 
 
 def row_tile(rows):
-    for tile in (224, 128, 112, 64, 32, 16):
+    for tile in (448, 224, 128, 112, 64, 32, 16):
         if rows % tile == 0:
             return tile
     return rows
@@ -853,7 +853,7 @@
         img = jnp.where(native, image_input[0], img_swap)
         shard = modulation_shard(due(partial_modulation(ranks), text.w_qkv.sources[1]))
         text_tokens, text.cot = gather_texts(due((text_input[0], text_cotangent[0]), shard))
-        get_first = fetch_first(shard)
+        get_first = fetch_first(ranks)
         next(get_first)
         a1_qkv, b0_qkv = get_qkv.send(shard)
         mods = both_modulations(due(modulation(shard), img_swap))

time: 722 us -> 717 us (level)
  waiting for transfers between devices: 190 us -> 177 us
  other arithmetic: 81.2 us -> 89.3 us
  Pallas kernels: 161 us -> 153 us
    ppermute x41, waiting for transfers between devices: 162 us -> 153 us  [xz(): return lax.ppermute(v, 'tp', [(i, i ^ bit) for i in range(T)])]
  transfers between devices with their start and end apart: 111 -> 111, of which waited for: 35 -> 35; matrix products, arithmetic and copies ran while one was open for 19% -> 21% of each run, Pallas kernels for 23% -> 22%
where the time goes in v3:
time: 717 us; the launch traced here: 707 us
  starting transfers between devices  189 us (26%)
  waiting for transfers between devices  177 us (25%)
  Pallas kernels  153 us (21%)
  other arithmetic  89.3 us (12%)
  local copies, waits for them, and re-layouts  55.9 us (8%)
  matrix products  21.2 us (3%)
  between operations  21.2 us (3%)
    ppermute x41, waiting for transfers between devices, xz(): return lax.ppermute(v, 'tp', [(i, i ^ bit) for i in range(T)])  153 us
    pallas_call x14, Pallas kernels, project(): pl.pallas_call(body, grid=(1,), in_specs=[SCALARS] + specs + [ANY] * n_sr...  117 us
    ppermute x41, starting transfers between devices, xz(): return lax.ppermute(v, 'tp', [(i, i ^ bit) for i in range(T)])  81.2 us
    ppermute x33, starting transfers between devices, xr(): return lax.ppermute(v, 'rep', [(i, i ^ bit) for i in range(R)])  66.1 us
    pallas_call x1, Pallas kernels, attend_backward(): pl.pallas_call(functools.partial(attend_backward_kernel, width, blocks, p...  25.2 us
    ppermute x18, starting transfers between devices, swap(): return lax.ppermute(v, ('rep', 'tp'), swap_pairs)  20 us
    ppermute x14, starting transfers between devices, xf(): return lax.ppermute(v, 'fsdp', [(i, i ^ bit) for i in range(F)])  17.5 us
    ppermute x14, waiting for transfers between devices, xf(): return lax.ppermute(v, 'fsdp', [(i, i ^ bit) for i in range(F)])  14.7 us
  transfers between devices with their start and end apart: 111, of which 35 were waited for; matrix products, arithmetic and copies ran while one was open for 21% of the time, Pallas kernels for 22%

profile of v3, /device:TPU:0, one launch (start us, length us, event | category | flops | bytes accessed | tf_op | source)
XLA Modules:
  0.0 706.6 jit_solution(5342088393645850105)
XLA Ops:
  73.3 5.5 collective-permute-start.8
  82.8 11.7 %collective-permute-done.8 = f32[2,2,6,384]{3,1,2,0:T(2,128)S(1)} collective-permute-done((f32[2,2,6,384]{3,1,2,0:T(2,128)S(1)}, f32[2,2,6,384]{3,1,2,0:T(2,128)S(1)}, u32[]{:S(2)}, u32[]{:S(2)}) %collective-permute-start.8) | collective-permute-done | bytes 36896 | tf_op jit(solution)/shard_map/ppermute | solution.py:531
  116.9 7.7 %collective-permute-done.12 = bf16[2,16,6144]{2,1,0:T(8,128)(2,1)S(1)} collective-permute-done((bf16[2,16,6144]{2,1,0:T(8,128)(2,1)S(1)}, bf16[2,16,6144]{2,1,0:T(8,128)(2,1)S(1)}, u32[]{:S(2)}, u32[]{:S(2)}) %collective-permute-start.12) | collective-permute-done | bytes 393248 | tf_op jit(solution)/shard_map/ppermute | solution.py:531
  128.7 16.5 %collective-permute-done.13 = bf16[2,16,6144]{2,1,0:T(8,128)(2,1)S(1)} collective-permute-done((bf16[2,16,6144]{2,1,0:T(8,128)(2,1)S(1)}, bf16[2,16,6144]{2,1,0:T(8,128)(2,1)S(1)}, u32[]{:S(2)}, u32[]{:S(2)}) %collective-permute-start.13) | collective-permute-done | bytes 393248 | tf_op jit(solution)/shard_map/ppermute | solution.py:531
  158.4 8.5 %collective-permute-done.28.refs_4_.refs_6_ = bf16[384,768]{1,0:T(8,128)(2,1)S(1)} collective-permute-done((bf16[384,768]{1,0:T(8,128)(2,1)S(1)}, bf16[384,768]{1,0:T(8,128)(2,1)S(1)}, u32[]{:S(2)}, u32[]{:S(2)}) %collective-permute-start.28) | collective-permute-done | bytes 589856 | tf_op jit(solution)/shard_map/ppermute | solution.py:534
  170.4 5.5 collective-permute-done.18.refs_8_.refs_13_
  176.8 6.9 shard_map.274
  189.9 7.0 shard_map.275
  199.5 7.7 %collective-permute-start.41 = (bf16[384,1536]{1,0:T(8,128)(2,1)}, bf16[384,1536]{1,0:T(8,128)(2,1)}, u32[]{:S(2)}, u32[]{:S(2)}) collective-permute-start(bf16[384,1536]{1,0:T(8,128)(2,1)} %collective-permute-done.29.refs_5_.refs_12_), channel_id=1, source_target_pairs={{0,8},{8,0},{16,24},{24,16},{1,9},{9,1},{17,25},{25,17},{2,10},{10... | collective-permute-start | bytes 3538952 | tf_op jit(solution)/shard_map/ppermute | solution.py:537
  207.9 10.7 %attend_forward.1 = (bf16[1024,384]{1,0:T(8,128)(2,1)S(1)}, f32[1024,6]{1,0:T(8,128)S(1)}) custom-call(s32[15]{0:T(128)S(1)} %copy-done.1, bf16[448,1152]{1,0:T(8,128)(2,1)S(1)} %copy-done.13, bf16[448,1152]{1,0:T(8,128)(2,1)S(1)} %copy-done.15, bf16[128,1152]{1,0:T(8,128)(2,1)S(1)} %copy-done.3, bf16[128,1152]{1,0:T(8,128)(2,1)S(1)} %collective-permute-done.26.refs_3_), custom_call_target="tpu_custom_call" | custom-call | flops 51539607552 | bytes 4718592 | tf_op jit(solution)/shard_map/attend_forward/pallas_call | solution.py:203
  229.1 12.9 %collective-permute-start.42 = (bf16[768,768]{1,0:T(8,128)(2,1)}, bf16[768,768]{1,0:T(8,128)(2,1)}, u32[]{:S(2)}, u32[]{:S(2)}) collective-permute-start(bf16[768,768]{1,0:T(8,128)(2,1)} %collective-permute-done.30.refs_8_.refs_9_), channel_id=1, source_target_pairs={{0,8},{8,0},{16,24},{24,16},{1,9},{9,1},{17,25},{25,17},{2,10},{10... | collective-permute-start | bytes 3538952 | tf_op jit(solution)/shard_map/ppermute | solution.py:537
  242.1 14.4 %collective-permute-start.45 = (bf16[128,1536]{1,0:T(8,128)(2,1)S(1)}, bf16[128,1536]{1,0:T(8,128)(2,1)S(1)}, u32[]{:S(2)}, u32[]{:S(2)}) collective-permute-start(bf16[128,1536]{1,0:T(8,128)(2,1)S(1)} %add.497), channel_id=1, source_target_pairs={{0,2},{1,3},{2,0},{3,1},{4,6},{5,7},{6,4},{7,5},{8,10},{9,11},{10,... | collective-permute-start | bytes 1179656 | tf_op jit(solution)/shard_map/ppermute | solution.py:531
  257.4 6.2 shard_map.277
  263.6 14.7 %collective-permute-done.45 = bf16[128,1536]{1,0:T(8,128)(2,1)S(1)} collective-permute-done((bf16[128,1536]{1,0:T(8,128)(2,1)S(1)}, bf16[128,1536]{1,0:T(8,128)(2,1)S(1)}, u32[]{:S(2)}, u32[]{:S(2)}) %collective-permute-start.45) | collective-permute-done | bytes 393248 | tf_op jit(solution)/shard_map/ppermute | solution.py:531
  280.3 7.0 shard_map.279
  287.4 8.4 %shard_map.280 = (bf16[128,1536]{1,0:T(8,128)(2,1)}, f32[16,1536]{1,0:T(8,128)}, f32[16,1536]{1,0:T(8,128)}, f32[16,1536]{1,0:T(8,128)}, f32[16,1536]{1,0:T(8,128)}) custom-call(s32[15]{0:T(128)} %stack.229.offs_ref.offs, bf16[128,1536]{1,0:T(8,128)(2,1)} %get-tuple-element.206.refs_0_, bf16[128,1536]{1,0:T(8,128)(2,1)} %get-tuple-element.207.refs_1_, ...), custom_call_target="tpu_custom_call" | custom-call | flops 9663676416 | bytes 10027008 | tf_op jit(solution)/shard_map/pallas_call | solution.py:467
  301.5 6.6 collective-permute-done.50
  309.9 20.4 %collective-permute-done.34 = bf16[224,1536]{1,0:T(8,128)(2,1)S(1)} collective-permute-done((bf16[224,1536]{1,0:T(8,128)(2,1)S(1)}, bf16[224,1536]{1,0:T(8,128)(2,1)S(1)}, u32[]{:S(2)}, u32[]{:S(2)}) %collective-permute-start.34) | collective-permute-done | bytes 688160 | tf_op jit(solution)/shard_map/ppermute | solution.py:531
  349.3 7.7 %collective-permute-done.47.refs_16_.refs_24_ = bf16[224,1536]{1,0:T(8,128)(2,1)} collective-permute-done((bf16[224,1536]{1,0:T(8,128)(2,1)S(1)}, bf16[224,1536]{1,0:T(8,128)(2,1)}, u32[]{:S(2)}, u32[]{:S(2)}) %collective-permute-start.47) | collective-permute-done | bytes 688160 | tf_op jit(solution)/shard_map/ppermute | solution.py:531
  357.0 5.0 collective-permute-start.48
  371.4 6.1 collective-permute-start.53
  380.5 22.5 %shard_map.281 = (bf16[224,1536]{1,0:T(8,128)(2,1)}, bf16[224,1536]{1,0:T(8,128)(2,1)}, bf16[224,1536]{1,0:T(8,128)(2,1)}, bf16[224,1536]{1,0:T(8,128)(2,1)}, bf...) custom-call(s32[15]{0:T(128)} %stack.229.offs_ref.offs, ...), custom_call_target="tpu_custom_call" | custom-call | flops 67645734912 | bytes 17752064 | tf_op jit(solution)/shard_map/pallas_call | solution.py:467
  404.0 23.1 %shard_map.283 = (bf16[224,1536]{1,0:T(8,128)(2,1)}, bf16[224,1536]{1,0:T(8,128)(2,1)}, bf16[224,1536]{1,0:T(8,128)(2,1)}, bf16[224,1536]{1,0:T(8,128)(2,1)}, f3...) custom-call(s32[15]{0:T(128)} %stack.229.offs_ref.offs, ...), custom_call_target="tpu_custom_call" | custom-call | flops 67645734912 | bytes 12386304 | tf_op jit(solution)/shard_map/pallas_call | solution.py:467
  443.4 10.2 %collective-permute-done.58 = bf16[224,1536]{1,0:T(8,128)(2,1)} collective-permute-done((bf16[224,1536]{1,0:T(8,128)(2,1)}, bf16[224,1536]{1,0:T(8,128)(2,1)}, u32[]{:S(2)}, u32[]{:S(2)}) %collective-permute-start.58) | collective-permute-done | bytes 688160 | tf_op jit(solution)/shard_map/ppermute | solution.py:531
  473.3 14.8 %collective-permute-done.64.refs_0_ = bf16[224,1536]{1,0:T(8,128)(2,1)} collective-permute-done((bf16[224,1536]{1,0:T(8,128)(2,1)S(1)}, bf16[224,1536]{1,0:T(8,128)(2,1)}, u32[]{:S(2)}, u32[]{:S(2)}) %collective-permute-start.64) | collective-permute-done | bytes 688160 | tf_op jit(solution)/shard_map/ppermute | solution.py:531
  494.6 7.6 %collective-permute-done.61 = bf16[224,1536]{1,0:T(8,128)(2,1)} collective-permute-done((bf16[224,1536]{1,0:T(8,128)(2,1)}, bf16[224,1536]{1,0:T(8,128)(2,1)}, u32[]{:S(2)}, u32[]{:S(2)}) %collective-permute-start.61) | collective-permute-done | bytes 688160 | tf_op jit(solution)/shard_map/ppermute | solution.py:531
  511.7 25.2 %attend_backward.1.refs_0_ = bf16[1024,1152]{1,0:T(8,128)(2,1)} custom-call(s32[15]{0:T(128)S(1)} %copy-done.2, f32[1024,6]{1,0:T(8,128)S(1)} %get-tuple-element.238.lse_ref, bf16[448,1152]{1,0:T(8,128)(2,1)S(1)} %copy-done.14, bf16[448,1152]{1,0:T(8,128)(2,1)S(1)} %copy-done.16, bf16[128,1152]{1,0:T(8,128)(2,1)S(1)} %copy-done.4, ...), custom_call_target="tpu_custom_call" | custom-call | flops 103079215104 | bytes 9437184 | tf_op jit(solution)/shard_map/attend_backward/pallas_call | solution.py:235
  538.7 10.4 %shard_map.286 = (bf16[224,1536]{1,0:T(8,128)(2,1)}, bf16[224,1536]{1,0:T(8,128)(2,1)}, bf16[224,1536]{1,0:T(8,128)(2,1)}, bf16[224,1536]{1,0:T(8,128)(2,1)}, f32[16,1152]{1,0:T(8,128)}, /*index=5*/f32[16,1536]{1,0:T(8,128)}) custom-call(s32[15]{0:T(128)} %stack.229.offs_ref.offs, bf16[1024,1152]{1,0:T(8,128)(2,1)} %attend_backward.1.refs_0_, ...), custom_call_target="tpu_custom_call" | custom-call | flops 25367150592 | bytes 6377472 | tf_op jit(solution)/shard_map/pallas_call | solution.py:467
  561.7 5.1 collective-permute-start.66
  583.4 5.2 shard_map.287
  589.6 8.6 %collective-permute-start.99 = (bf16[16,768]{1,0:T(8,128)(2,1)S(1)}, bf16[16,768]{1,0:T(8,128)(2,1)S(1)}, u32[]{:S(2)}, u32[]{:S(2)}) collective-permute-start(bf16[16,768]{1,0:T(8,128)(2,1)S(1)} %broadcast_select_fusion.21), channel_id=1, source_target_pairs={{0,2},{1,3},{2,0},{3,1},{4,6},{5,7},{6,4},{7,5},{8,10},{9,11},{10,... | collective-permute-start | bytes 73736 | tf_op jit(solution)/shard_map/ppermute | solution.py:531
  600.4 6.8 collective-permute-start.100
  (812 shorter events, 348.6 us)
Async XLA Ops:
  8.0 484.7 %reduce-scatter.2.cloned.1.call-start = ((), (), s32[]{:S(2)}) async-start(), calls=%async_computation.1 | async-start | bytes 491520 | tf_op jit(solution)/shard_map/reduce_scatter | solution.py:1161
  16.1 36.2 %collective-permute-start = (bf16[3,384,384]{2,1,0:T(8,128)(2,1)}, bf16[3,384,384]{2,1,0:T(8,128)(2,1)}, u32[]{:S(2)}, u32[]{:S(2)}) collective-permute-start(bf16[3,384,384]{2,1,0:T(8,128)(2,1)} %dynamic-slice_bitcast_fusion.5), channel_id=1, source_target_pairs={{2,8},{3,9},{8,2},{9,3},{18,24},{19,25},{24,18},{25,19},{6,12},{7,... | collective-permute-start | bytes 2654216 | tf_op jit(solution)/shard_map/ppermute | solution.py:547
  60.7 44.3 %collective-permute-start.4 = (bf16[224,1536]{1,0:T(8,128)(2,1)}, bf16[224,1536]{1,0:T(8,128)(2,1)}, u32[]{:S(2)}, u32[]{:S(2)}) collective-permute-start(bf16[224,1536]{1,0:T(8,128)(2,1)} %bitcast), channel_id=1, source_target_pairs={{2,8},{3,9},{8,2},{9,3},{18,24},{19,25},{24,18},{25,19},{6,12},{7,... | collective-permute-start | bytes 2064392 | tf_op jit(solution)/shard_map/ppermute | solution.py:547
  70.3 39.0 %collective-permute-start.11 = (bf16[2,16,10752]{2,1,0:T(8,128)(2,1)}, bf16[2,16,10752]{2,1,0:T(8,128)(2,1)}, u32[]{:S(2)}, u32[]{:S(2)}) collective-permute-start(bf16[2,16,10752]{2,1,0:T(8,128)(2,1)} %pad_maximum_fusion.6), channel_id=1, source_target_pairs={{0,4},{4,0},{1,5},{5,1},{2,6},{6,2},{3,7},{7,3},{8,12},{12,8},{9,1... | collective-permute-start | bytes 2064392 | tf_op jit(solution)/shard_map/ppermute | solution.py:534
  71.8 111.9 %collective-permute-start.25 = (bf16[3,384,384]{2,1,0:T(8,128)(2,1)}, bf16[3,384,384]{2,1,0:T(8,128)(2,1)}, u32[]{:S(2)}, u32[]{:S(2)}) collective-permute-start(bf16[3,384,384]{2,1,0:T(8,128)(2,1)} %collective-permute-done.5.refs_4_.refs_6_), channel_id=1, source_target_pairs={{0,8},{8,0},{16,24},{24,16},{1,9},{9,1},{17,25},{25,17},{2,10},{10... | collective-permute-start | bytes 2654216 | tf_op jit(solution)/shard_map/ppermute | solution.py:537
  94.5 52.2 %collective-permute-start.16 = (bf16[3,384,384]{2,1,0:T(8,128)(2,1)}, bf16[3,384,384]{2,1,0:T(8,128)(2,1)}, u32[]{:S(2)}, u32[]{:S(2)}) collective-permute-start(bf16[3,384,384]{2,1,0:T(8,128)(2,1)} %collective-permute-done.refs_5_.refs_10_), channel_id=1, source_target_pairs={{2,18},{3,19},{8,24},{9,25},{18,2},{19,3},{24,8},{25,9},{6,22},{7,... | collective-permute-start | bytes 2654216 | tf_op jit(solution)/shard_map/ppermute | solution.py:550
  112.8 33.3 %collective-permute-start.17 = (bf16[3,384,384]{2,1,0:T(8,128)(2,1)S(1)}, bf16[3,384,384]{2,1,0:T(8,128)(2,1)S(1)}, u32[]{:S(2)}, u32[]{:S(2)}) collective-permute-start(bf16[3,384,384]{2,1,0:T(8,128)(2,1)S(1)} %copy-done.36), channel_id=1, source_target_pairs={{0,4},{4,0},{1,5},{5,1},{2,6},{6,2},{3,7},{7,3},{8,12},{12,8},{9,1... | collective-permute-start | bytes 2654216 | tf_op jit(solution)/shard_map/ppermute | solution.py:534
  114.9 36.7 %collective-permute-start.19 = (bf16[224,1536]{1,0:T(8,128)(2,1)S(1)}, bf16[224,1536]{1,0:T(8,128)(2,1)}, u32[]{:S(2)}, u32[]{:S(2)}) collective-permute-start(bf16[224,1536]{1,0:T(8,128)(2,1)S(1)} %fusion.19.refs_0_.refs_1_), channel_id=1, source_target_pairs={{0,1},{1,0},{2,3},{3,2},{4,5},{5,4},{6,7},{7,6},{8,9},{9,8},{10,11... | collective-permute-start | bytes 2064392 | tf_op jit(solution)/shard_map/ppermute | solution.py:531
  166.9 32.6 %collective-permute-start.29 = (bf16[384,1536]{1,0:T(8,128)(2,1)}, bf16[384,1536]{1,0:T(8,128)(2,1)}, u32[]{:S(2)}, u32[]{:S(2)}) collective-permute-start(bf16[384,1536]{1,0:T(8,128)(2,1)} %dynamic-slice_bitcast_fusion.2), channel_id=1, source_target_pairs={{0,4},{4,0},{1,5},{5,1},{2,6},{6,2},{3,7},{7,3},{8,12},{12,8},{9,1... | collective-permute-start | bytes 3538952 | tf_op jit(solution)/shard_map/ppermute | solution.py:534
  168.4 38.7 %collective-permute-start.21 = (bf16[384,1536]{1,0:T(8,128)(2,1)}, bf16[384,1536]{1,0:T(8,128)(2,1)}, u32[]{:S(2)}, u32[]{:S(2)}) collective-permute-start(bf16[384,1536]{1,0:T(8,128)(2,1)} %dynamic-slice_bitcast_fusion.3), channel_id=1, source_target_pairs={{2,8},{3,9},{8,2},{9,3},{18,24},{19,25},{24,18},{25,19},{6,12},{7,... | collective-permute-start | bytes 3538952 | tf_op jit(solution)/shard_map/ppermute | solution.py:547
  199.5 80.4 %collective-permute-start.41 = (bf16[384,1536]{1,0:T(8,128)(2,1)}, bf16[384,1536]{1,0:T(8,128)(2,1)}, u32[]{:S(2)}, u32[]{:S(2)}) collective-permute-start(bf16[384,1536]{1,0:T(8,128)(2,1)} %collective-permute-done.29.refs_5_.refs_12_), channel_id=1, source_target_pairs={{0,8},{8,0},{16,24},{24,16},{1,9},{9,1},{17,25},{25,17},{2,10},{10... | collective-permute-start | bytes 3538952 | tf_op jit(solution)/shard_map/ppermute | solution.py:537
  219.4 79.4 %collective-permute-start.36 = (bf16[768,768]{1,0:T(8,128)(2,1)}, bf16[768,768]{1,0:T(8,128)(2,1)}, u32[]{:S(2)}, u32[]{:S(2)}) collective-permute-start(bf16[768,768]{1,0:T(8,128)(2,1)} %dynamic-slice_bitcast_fusion), channel_id=1, source_target_pairs={{2,8},{3,9},{8,2},{9,3},{18,24},{19,25},{24,18},{25,19},{6,12},{7,... | collective-permute-start | bytes 3538952 | tf_op jit(solution)/shard_map/ppermute | solution.py:547
  221.9 34.7 %collective-permute-start.31 = (bf16[384,768]{1,0:T(8,128)(2,1)S(1)}, bf16[384,768]{1,0:T(8,128)(2,1)S(1)}, u32[]{:S(2)}, u32[]{:S(2)}) collective-permute-start(bf16[384,768]{1,0:T(8,128)(2,1)S(1)} %broadcast_select_fusion.6), channel_id=1, source_target_pairs={{0,4},{4,0},{1,5},{5,1},{2,6},{6,2},{3,7},{7,3},{8,12},{12,8},{9,1... | collective-permute-start | bytes 1769480 | tf_op jit(solution)/shard_map/ppermute | solution.py:534
  229.1 51.3 %collective-permute-start.42 = (bf16[768,768]{1,0:T(8,128)(2,1)}, bf16[768,768]{1,0:T(8,128)(2,1)}, u32[]{:S(2)}, u32[]{:S(2)}) collective-permute-start(bf16[768,768]{1,0:T(8,128)(2,1)} %collective-permute-done.30.refs_8_.refs_9_), channel_id=1, source_target_pairs={{0,8},{8,0},{16,24},{24,16},{1,9},{9,1},{17,25},{25,17},{2,10},{10... | collective-permute-start | bytes 3538952 | tf_op jit(solution)/shard_map/ppermute | solution.py:537
  242.1 36.2 %collective-permute-start.45 = (bf16[128,1536]{1,0:T(8,128)(2,1)S(1)}, bf16[128,1536]{1,0:T(8,128)(2,1)S(1)}, u32[]{:S(2)}, u32[]{:S(2)}) collective-permute-start(bf16[128,1536]{1,0:T(8,128)(2,1)S(1)} %add.497), channel_id=1, source_target_pairs={{0,2},{1,3},{2,0},{3,1},{4,6},{5,7},{6,4},{7,5},{8,10},{9,11},{10,... | collective-permute-start | bytes 1179656 | tf_op jit(solution)/shard_map/ppermute | solution.py:531
  256.6 52.1 %collective-permute-start.35 = (bf16[384,1536]{1,0:T(8,128)(2,1)S(1)}, bf16[384,1536]{1,0:T(8,128)(2,1)}, u32[]{:S(2)}, u32[]{:S(2)}) collective-permute-start(bf16[384,1536]{1,0:T(8,128)(2,1)S(1)} %broadcast_select_fusion.1), channel_id=1, source_target_pairs={{0,4},{4,0},{1,5},{5,1},{2,6},{6,2},{3,7},{7,3},{8,12},{12,8},{9,1... | collective-permute-start | bytes 3538952 | tf_op jit(solution)/shard_map/ppermute | solution.py:534
  278.3 31.6 %collective-permute-start.32 = (bf16[224,1536]{1,0:T(8,128)(2,1)}, bf16[224,1536]{1,0:T(8,128)(2,1)S(1)}, u32[]{:S(2)}, u32[]{:S(2)}) collective-permute-start(bf16[224,1536]{1,0:T(8,128)(2,1)} %get-tuple-element.190), channel_id=1, source_target_pairs={{0,8},{8,0},{16,24},{24,16},{1,9},{9,1},{17,25},{25,17},{2,10},{10... | collective-permute-start | bytes 2064392 | tf_op jit(solution)/shard_map/ppermute | solution.py:537
  296.1 34.2 %collective-permute-start.34 = (bf16[224,1536]{1,0:T(8,128)(2,1)S(1)}, bf16[224,1536]{1,0:T(8,128)(2,1)S(1)}, u32[]{:S(2)}, u32[]{:S(2)}) collective-permute-start(bf16[224,1536]{1,0:T(8,128)(2,1)S(1)} %add_convert_fusion.4), channel_id=1, source_target_pairs={{0,1},{1,0},{2,3},{3,2},{4,5},{5,4},{6,7},{7,6},{8,9},{9,8},{10,11... | collective-permute-start | bytes 2064392 | tf_op jit(solution)/shard_map/ppermute | solution.py:531
  308.6 27.5 %collective-permute-start.37 = (bf16[384,1536]{1,0:T(8,128)(2,1)}, bf16[384,1536]{1,0:T(8,128)(2,1)S(1)}, u32[]{:S(2)}, u32[]{:S(2)}) collective-permute-start(bf16[384,1536]{1,0:T(8,128)(2,1)} %collective-permute-done.35.refs_7_.refs_16_), channel_id=1, source_target_pairs={{0,16},{8,24},{16,0},{24,8},{1,17},{9,25},{17,1},{25,9},{2,18},{10... | collective-permute-start | bytes 3538952 | tf_op jit(solution)/shard_map/ppermute | solution.py:537
  309.1 34.5 %collective-permute-start.39 = (bf16[768,768]{1,0:T(8,128)(2,1)}, bf16[768,768]{1,0:T(8,128)(2,1)}, u32[]{:S(2)}, u32[]{:S(2)}) collective-permute-start(bf16[768,768]{1,0:T(8,128)(2,1)} %broadcast_select_fusion), channel_id=1, source_target_pairs={{0,4},{4,0},{1,5},{5,1},{2,6},{6,2},{3,7},{7,3},{8,12},{12,8},{9,1... | collective-permute-start | bytes 3538952 | tf_op jit(solution)/shard_map/ppermute | solution.py:534
  331.6 47.8 %collective-permute-start.46 = (bf16[224,1536]{1,0:T(8,128)(2,1)S(1)}, bf16[224,1536]{1,0:T(8,128)(2,1)}, u32[]{:S(2)}, u32[]{:S(2)}) collective-permute-start(bf16[224,1536]{1,0:T(8,128)(2,1)S(1)} %add_convert_fusion.3.refs_14_.refs_22_), channel_id=1, source_target_pairs={{0,8},{8,0},{16,24},{24,16},{1,9},{9,1},{17,25},{25,17},{2,10},{10... | collective-permute-start | bytes 2064392 | tf_op jit(solution)/shard_map/ppermute | solution.py:537
  345.5 31.9 %collective-permute-start.40 = (bf16[768,768]{1,0:T(8,128)(2,1)}, bf16[768,768]{1,0:T(8,128)(2,1)S(1)}, u32[]{:S(2)}, u32[]{:S(2)}) collective-permute-start(bf16[768,768]{1,0:T(8,128)(2,1)} %collective-permute-done.39.refs_12_.refs_11_), channel_id=1, source_target_pairs={{0,16},{8,24},{16,0},{24,8},{1,17},{9,25},{17,1},{25,9},{2,18},{10... | collective-permute-start | bytes 3538952 | tf_op jit(solution)/shard_map/ppermute | solution.py:537
  365.7 62.2 %collective-permute-start.94 = (bf16[48,384]{1,0:T(8,128)(2,1)S(1)}, bf16[48,384]{1,0:T(8,128)(2,1)S(1)}, u32[]{:S(2)}, u32[]{:S(2)}) collective-permute-start(bf16[48,384]{1,0:T(8,128)(2,1)S(1)} %broadcast_select_fusion.18), channel_id=1, source_target_pairs={{0,1},{1,0},{2,3},{3,2},{4,5},{5,4},{6,7},{7,6},{8,9},{9,8},{10,11... | collective-permute-start | bytes 110600 | tf_op jit(solution)/shard_map/ppermute | solution.py:531
  371.4 31.6 %collective-permute-start.53 = (bf16[224,1536]{1,0:T(8,128)(2,1)S(1)}, bf16[224,1536]{1,0:T(8,128)(2,1)S(1)}, u32[]{:S(2)}, u32[]{:S(2)}) collective-permute-start(bf16[224,1536]{1,0:T(8,128)(2,1)S(1)} %get-tuple-element.228.refs_18_), channel_id=1, source_target_pairs={{0,8},{8,0},{16,24},{24,16},{1,9},{9,1},{17,25},{25,17},{2,10},{10... | collective-permute-start | bytes 2064392 | tf_op jit(solution)/shard_map/ppermute | solution.py:537
  379.4 47.9 %collective-permute-start.73 = (f32[1,2,1664]{2,1,0:T(2,128)S(1)}, f32[1,2,1664]{2,1,0:T(2,128)S(1)}, u32[]{:S(2)}, u32[]{:S(2)}) collective-permute-start(f32[1,2,1664]{2,1,0:T(2,128)S(1)} %bitcast.346), channel_id=1, source_target_pairs={{0,8},{8,0},{16,24},{24,16},{1,9},{9,1},{17,25},{25,17},{2,10},{10... | collective-permute-start | bytes 39944 | tf_op jit(solution)/shard_map/ppermute | solution.py:537
  465.2 218.5 %all-gather.3.cloned.1.call-start = ((), (), s32[]{:S(2)}) async-start(), calls=%async_computation.2 | async-start | bytes 2654208 | tf_op jit(solution)/shard_map/all_gather | solution.py:1200
  465.3 29.3 %collective-permute-start.59 = (bf16[224,1536]{1,0:T(8,128)(2,1)}, bf16[224,1536]{1,0:T(8,128)(2,1)}, u32[]{:S(2)}, u32[]{:S(2)}) collective-permute-start(bf16[224,1536]{1,0:T(8,128)(2,1)} %get-tuple-element.234), channel_id=1, source_target_pairs={{0,8},{8,0},{16,24},{24,16},{1,9},{9,1},{17,25},{25,17},{2,10},{10... | collective-permute-start | bytes 2064392 | tf_op jit(solution)/shard_map/ppermute | solution.py:537
  467.9 34.3 %collective-permute-start.61 = (bf16[224,1536]{1,0:T(8,128)(2,1)}, bf16[224,1536]{1,0:T(8,128)(2,1)}, u32[]{:S(2)}, u32[]{:S(2)}) collective-permute-start(bf16[224,1536]{1,0:T(8,128)(2,1)} %add_convert_fusion.1), channel_id=1, source_target_pairs={{0,1},{1,0},{2,3},{3,2},{4,5},{5,4},{6,7},{7,6},{8,9},{9,8},{10,11... | collective-permute-start | bytes 2064392 | tf_op jit(solution)/shard_map/ppermute | solution.py:531
  504.5 94.8 %collective-permute-start.62 = (bf16[224,1536]{1,0:T(8,128)(2,1)S(1)}, bf16[224,1536]{1,0:T(8,128)(2,1)}, u32[]{:S(2)}, u32[]{:S(2)}) collective-permute-start(bf16[224,1536]{1,0:T(8,128)(2,1)S(1)} %multiply_convert_fusion), channel_id=1, source_target_pairs={{2,8},{3,9},{8,2},{9,3},{18,24},{19,25},{24,18},{25,19},{6,12},{7,... | collective-permute-start | bytes 2064392 | tf_op jit(solution)/shard_map/ppermute | solution.py:547
  561.7 65.5 %collective-permute-start.66 = (bf16[224,1536]{1,0:T(8,128)(2,1)}, bf16[224,1536]{1,0:T(8,128)(2,1)S(1)}, u32[]{:S(2)}, u32[]{:S(2)}) collective-permute-start(bf16[224,1536]{1,0:T(8,128)(2,1)} %get-tuple-element.246), channel_id=1, source_target_pairs={{0,8},{8,0},{16,24},{24,16},{1,9},{9,1},{17,25},{25,17},{2,10},{10... | collective-permute-start | bytes 2064392 | tf_op jit(solution)/shard_map/ppermute | solution.py:537
  582.6 44.6 %collective-permute-start.68 = (bf16[224,1536]{1,0:T(8,128)(2,1)S(1)}, bf16[224,1536]{1,0:T(8,128)(2,1)S(1)}, u32[]{:S(2)}, u32[]{:S(2)}) collective-permute-start(bf16[224,1536]{1,0:T(8,128)(2,1)S(1)} %add_convert_fusion), channel_id=1, source_target_pairs={{0,1},{1,0},{2,3},{3,2},{4,5},{5,4},{6,7},{7,6},{8,9},{9,8},{10,11... | collective-permute-start | bytes 2064392 | tf_op jit(solution)/shard_map/ppermute | solution.py:531
  639.4 42.3 %collective-permute-start.69 = (bf16[224,1536]{1,0:T(8,128)(2,1)}, bf16[224,1536]{1,0:T(8,128)(2,1)S(1)}, u32[]{:S(2)}, u32[]{:S(2)}) collective-permute-start(bf16[224,1536]{1,0:T(8,128)(2,1)} %fusion.24), channel_id=1, source_target_pairs={{2,8},{3,9},{8,2},{9,3},{18,24},{19,25},{24,18},{25,19},{6,12},{7,... | collective-permute-start | bytes 2064392 | tf_op jit(solution)/shard_map/ppermute | solution.py:547
  (217 other events, 2687.6 us)
Sparse Core Ops, SparseCore 0:
  465.3 21.1 reduce-scatter.1
Sparse Core Ops, SparseCore 1:
  578.9 35.0 all-gather.2
